TPU v7x, 256 devices: a whole 4x4x8 slice. The times are simulated.
256 devices in a mesh: gx: 8 (over x, core), gy: 32 (over z, y).
Axes of the slice: x: 4, y: 4, z: 8, core: 2. Of those that a mesh axis runs over, the one named last changes fastest.
Arguments:
- residual: float32 [1024, 1024, 256], P('gx', 'gy'), may hold values from -6 to 6
- local_x: bfloat16 [136, 136], replicated, may hold values from -0.5 to 0.5
- local_y: bfloat16 [40, 40], replicated, may hold values from -1 to 1
- local_z: bfloat16 [256, 256], replicated, may hold values from -0.375 to 0.375
- eig_x: float32 [136], replicated, may hold values from 0.1 to 2
- eig_y: float32 [40], replicated, may hold values from 0.1 to 2
- eig_z: float32 [256], replicated, may hold values from 0.1 to 2
- coarse_x: bfloat16 [128, 4], replicated, may hold values from -0.5 to 0.5
- coarse_y: bfloat16 [32, 4], replicated, may hold values from -1 to 1
- coarse_z: bfloat16 [256, 4], replicated, may hold values from -0.375 to 0.375
- mode_x: float32 [32, 32], replicated, may hold values from -1 to 1
- mode_y: float32 [128, 128], replicated, may hold values from -0.5 to 0.5
- mode_z: float32 [4, 4], replicated, may hold values from -3 to 3
- coarse_eig_x: float32 [32], replicated, may hold values from 0.002 to 0.02
- coarse_eig_y: float32 [128], replicated, may hold values from 0.002 to 0.02
- coarse_eig_z: float32 [4], replicated, may hold values from 0.002 to 0.02
Outputs:
- preconditioned: float32 [1024, 1024, 256], P('gx', 'gy')
All inputs are finite; a program needn't handle non-finite values.
Results may differ from a plain program's by a relative error of at most 0.0045.
Values may be sent and summed in bfloat16 or wider, within the bound.
No kernel may reach another device: no remote copies, remote signals or barrier semaphores. Data moves between devices by JAX's collectives and lax.ppermute only.
A program may use at most 64 MiB of HBM per device.

v0:
```python
import jax
import jax.numpy as jnp
from jax import lax
from jax.sharding import PartitionSpec as P

OV = 4
MODES = 4


def with_halo(x, sides, width):
    for axis, dim in sides:
        size, length = (lax.axis_size(axis), x.shape[dim])
        up = [(i, (i + 1) % size) for i in range(size)]
        down = [(j, i) for i, j in up]
        last = lax.slice_in_dim(x, length - width, length, axis=dim)
        initial = lax.slice_in_dim(x, 0, width, axis=dim)
        before = lax.ppermute(last, axis, up)
        after = lax.ppermute(initial, axis, down)
        x = jnp.concatenate([before, x, after], axis=dim)
    return x


def solve_local(block, local_x, local_y, local_z, scales):
    first_x = jnp.einsum("xa,xyz->ayz", local_x, block, preferred_element_type=jnp.float32).astype(
        jnp.bfloat16
    )
    first_y = jnp.einsum(
        "yb,ayz->abz", local_y, first_x, preferred_element_type=jnp.float32
    ).astype(jnp.bfloat16)
    along = jnp.einsum("zc,abz->abc", local_z, first_y, preferred_element_type=jnp.float32)
    spectral = (along / scales).astype(jnp.bfloat16)
    back_z = jnp.einsum(
        "zc,abc->abz", local_z, spectral, preferred_element_type=jnp.float32
    ).astype(jnp.bfloat16)
    back_y = jnp.einsum("yb,abz->ayz", local_y, back_z, preferred_element_type=jnp.float32).astype(
        jnp.bfloat16
    )
    return jnp.einsum("xa,ayz->xyz", local_x, back_y, preferred_element_type=jnp.float32)


def strips_rows(field):
    return jnp.concatenate([field[:OV], field[field.shape[0] - OV :]], 0)


def strips_cols(field):
    return jnp.concatenate([field[:, :OV], field[:, field.shape[1] - OV :]], 1)


def add_rows(field, received):
    inner = field[OV : field.shape[0] - OV]
    inner = inner.at[:OV].add(received[:OV])
    return inner.at[inner.shape[0] - OV :].add(received[received.shape[0] - OV :])


def add_cols(field, received):
    inner = field[:, OV : field.shape[1] - OV]
    inner = inner.at[:, :OV].add(received[:, :OV])
    return inner.at[:, inner.shape[1] - OV :].add(received[:, received.shape[1] - OV :])


def local(
    residual,
    local_x,
    local_y,
    local_z,
    eig_x,
    eig_y,
    eig_z,
    coarse_x,
    coarse_y,
    coarse_z,
    mode_x,
    mode_y,
    mode_z,
    coarse_eig_x,
    coarse_eig_y,
    coarse_eig_z,
):
    cells_x, cells_y, levels = residual.shape
    rounded = residual.astype(jnp.bfloat16)
    along_z = jnp.dot(rounded.reshape(-1, levels), coarse_z, preferred_element_type=jnp.float32)
    along_z = along_z.reshape(cells_x, cells_y, MODES)
    basis_x = coarse_x.astype(jnp.float32)
    basis_y = coarse_y.astype(jnp.float32)
    own_coarse = jnp.einsum(
        "xyp,xm,yn->mnp", along_z, basis_x, basis_y, precision=lax.Precision.HIGHEST
    )
    row_index = lax.axis_index("gx")
    col_index = lax.axis_index("gy")
    rows_x = lax.dynamic_slice_in_dim(mode_x, row_index * MODES, MODES, 0)
    rows_y = lax.dynamic_slice_in_dim(mode_y, col_index * MODES, MODES, 0)
    partial_rows = lax.all_gather(own_coarse, "gx", axis=0, tiled=True)
    coarse_res = lax.all_gather(partial_rows, "gy", axis=1, tiled=True)
    coarse_hat = jnp.einsum(
        "IJp,Ia,Jb,pc->abc", coarse_res, mode_x, mode_y, mode_z, precision=lax.Precision.HIGHEST
    )
    coarse_hat = coarse_hat / (
        coarse_eig_x[:, None, None] + coarse_eig_y[None, :, None] + coarse_eig_z[None, None, :]
    )
    own_sol = jnp.einsum(
        "abc,ma,nb,pc->mnp", coarse_hat, rows_x, rows_y, mode_z, precision=lax.Precision.HIGHEST
    )
    spread = jnp.einsum(
        "mnp,xm,yn->xyp", own_sol, basis_x, basis_y, precision=lax.Precision.HIGHEST
    )
    coarse_fix = jnp.dot(
        spread.reshape(-1, MODES), coarse_z.astype(jnp.float32).T, precision=lax.Precision.HIGHEST
    )
    coarse_fix = coarse_fix.reshape(cells_x, cells_y, levels)
    extended = with_halo(rounded, (("gx", 0), ("gy", 1)), OV)
    scales = eig_x[:, None, None] + eig_y[None, :, None] + eig_z[None, None, :]
    local_fix = solve_local(extended, local_x, local_y, local_z, scales)
    received = with_halo(strips_rows(local_fix).astype(jnp.bfloat16), (("gx", 0),), OV).astype(
        jnp.float32
    )
    folded = add_rows(local_fix, received)
    received = with_halo(strips_cols(folded).astype(jnp.bfloat16), (("gy", 1),), OV).astype(
        jnp.float32
    )
    folded = add_cols(folded, received)
    return folded + coarse_fix


def solution(mesh):
    placed = (
        P("gx", "gy", None),
        P(),
        P(),
        P(),
        P(),
        P(),
        P(),
        P(),
        P(),
        P(),
        P(),
        P(),
        P(),
        P(),
        P(),
        P(),
    )
    return jax.shard_map(
        local, mesh=mesh, in_specs=placed, out_specs=P("gx", "gy", None), check_vma=False
    )
```

profile of v0, /device:TPU:1, one launch (start us, length us, event | category | flops | bytes accessed | tf_op | source)
XLA Modules:
  0.0 123.9 jit_solution(12545552153308260391)
XLA Ops:
  0.1 4.5 %copy.79 = bf16[128,32,256]{2,0,1:T(8,128)(2,1)S(1)} copy(f32[128,32,256]{2,1,0:T(8,128)} %param.24) | data formatting | bytes 6291456 | tf_op args[0]
  4.6 0.0 copy-start.10
  4.7 0.1 fusion.75
  4.7 2.6 %collective-permute-start = (bf16[4,32,256]{2,0,1:T(4,128)(2,1)S(1)}, bf16[4,32,256]{2,0,1:T(4,128)(2,1)S(1)}, u32[]{:S(2)}, u32[]{:S(2)}) collective-permute-start(bf16[4,32,256]{2,0,1:T(4,128)(2,1)S(1)} %get-tuple-element.59), channel_id=1, source_target_pairs={{0,32},{32,64},{64,96},{96,128},{128,160},{160,192},{192,224},{224... | collective-permute-start | bytes 196616 | tf_op jit(solution)/shard_map/ppermute | solution.py:17
  7.3 0.6 collective-permute-start.1
  7.9 0.6 fusion.61
  8.6 0.2 convolution_bitcast_fusion.4
  8.8 0.2 convolution_bitcast_fusion.3
  9.0 0.1 copy.28
  9.1 15.5 %all_gather.6 = f32[32,4,4]{2,1,0:T(4,128)S(1)} all-gather(f32[4,4,4]{2,1,0:T(4,128)S(1)} %copy.28), channel_id=1, replica_groups=mesh['gx'=8,'gy'=32] {'gx'}, dimensions={0}, use_global_device_ids=true | all-gather | bytes 2304 | tf_op jit(solution)/shard_map/all_gather | solution.py:92
  24.6 0.1 copy.29
  24.7 38.5 %all_gather.7 = f32[32,128,4]{0,2,1:T(4,128)S(1)} all-gather(f32[32,4,4]{0,2,1:T(4,128)S(1)} %copy.29), channel_id=1, replica_groups=mesh['gx'=8,'gy'=32] {'gy'}, dimensions={1}, use_global_device_ids=true | all-gather | bytes 67584 | tf_op jit(solution)/shard_map/all_gather | solution.py:93
  63.2 0.1 broadcast_add_fusion.1
  63.3 0.4 convolution_bitcast_fusion.1
  63.7 0.0 copy-done.1
  63.7 0.2 fusion.41
  64.0 0.3 convolution_divide_fusion
  64.3 0.3 fusion.44
  64.6 0.2 pad_maximum_fusion.2
  64.8 0.8 collective-permute-start.2
  65.6 4.0 %collective-permute-start.3 = (bf16[136,4,256]{2,0,1:T(8,128)(2,1)S(1)}, bf16[136,4,256]{2,0,1:T(8,128)(2,1)S(1)}, u32[]{:S(2)}, u32[]{:S(2)}) collective-permute-start(bf16[136,4,256]{2,0,1:T(8,128)(2,1)S(1)} %get-tuple-element.58), channel_id=1, source_target_pairs={{1,0},{2,1},{3,2},{4,3},{5,4},{6,5},{7,6},{8,7},{9,8},{10,9},{11,1... | collective-permute-start | bytes 835592 | tf_op jit(solution)/shard_map/ppermute | solution.py:18
  69.7 0.3 fusion.54
  70.0 0.1 broadcast_add_fusion
  70.1 3.6 %collective-permute-done.2 = bf16[136,4,256]{2,0,1:T(8,128)(2,1)S(1)} collective-permute-done((bf16[136,4,256]{2,0,1:T(8,128)(2,1)S(1)}, bf16[136,4,256]{2,0,1:T(8,128)(2,1)S(1)}, u32[]{:S(2)}, u32[]{:S(2)}) %collective-permute-start.2) | collective-permute-done | bytes 278560 | tf_op jit(solution)/shard_map/ppermute | solution.py:17
  73.7 2.6 %convert_bitcast_fusion.1 = bf16[136,40,256]{2,0,1:T(8,128)(2,1)} fusion(bf16[136,4,256]{2,0,1:T(8,128)(2,1)S(1)} %collective-permute-done.3, bf16[4,32,256]{2,0,1:T(4,128)(2,1)S(1)} %collective-permute-done.1, bf16[128,32,256]{2,0,1:T(8,128)(2,1)S(1)} %copy.79, bf16[4,32,256]{2,0,1:T(4,128)(2,1)S(1)} %collective-permute-done, ...), kind=kOutput, calls=%fused_computation.22 | convolution fusion | flops 394117120 | bytes 5607552 | tf_op jit(solution)/shard_map/xa,xyz->ayz/dot_general | solution.py:24
  76.3 5.9 %fusion.10 = f32[136,40,256]{2,1,0:T(8,128)} fusion(bf16[136,40,256]{2,0,1:T(8,128)(2,1)} %convert_bitcast_fusion.1, bf16[256,256]{1,0:T(8,128)(2,1)S(1)} %copy-done, bf16[40,40]{1,0:T(8,128)(2,1)S(1)} %copy-done.4), kind=kOutput, calls=%fused_computation.12 | convolution fusion | flops 825835520 | bytes 8490112 | tf_op jit(solution)/shard_map/zc,abz->abc/dot_general | solution.py:30
  82.2 4.6 %convert_bitcast_fusion = bf16[136,40,256]{2,1,0:T(8,128)(2,1)S(1)} fusion(f32[136,40,256]{2,1,0:T(8,128)} %fusion.10, f32[256]{0:T(256)S(1)} %copy-done.13, f32[136,40]{1,0:T(8,128)S(1)} %broadcast_add_fusion, bf16[256,256]{1,0:T(8,128)(2,1)S(1)} %copy-done, bf16[40,40]{1,0:T(8,128)(2,1)S(1)} %copy-done.4), kind=kOutput, calls=%fused_computation.18 | convolution fusion | flops 831406080 | bytes 8512896 | tf_op jit(solution)/shard_map/yb,abz->ayz/dot_general | solution.py:35
  86.9 1.0 fusion.76
  87.8 0.1 fusion.73
  87.9 13.8 %collective-permute-start.4 = (bf16[4,40,256]{2,0,1:T(4,128)(2,1)S(1)}, bf16[4,40,256]{2,0,1:T(4,128)(2,1)S(1)}, u32[]{:S(2)}, u32[]{:S(2)}) collective-permute-start(bf16[4,40,256]{2,0,1:T(4,128)(2,1)S(1)} %get-tuple-element.53), channel_id=1, source_target_pairs={{0,32},{32,64},{64,96},{96,128},{128,160},{160,192},{192,224},{224... | collective-permute-start | bytes 245768 | tf_op jit(solution)/shard_map/ppermute | solution.py:17
  101.6 0.1 collective-permute-start.5
  101.7 0.2 convolution_bitcast_fusion.5
  101.9 0.7 slice.168
  102.6 0.5 collective-permute-done.4
  103.1 2.7 %collective-permute-done.5 = bf16[4,40,256]{2,0,1:T(4,128)(2,1)S(1)} collective-permute-done((bf16[4,40,256]{2,0,1:T(4,128)(2,1)S(1)}, bf16[4,40,256]{2,0,1:T(4,128)(2,1)S(1)}, u32[]{:S(2)}, u32[]{:S(2)}) %collective-permute-start.5) | collective-permute-done | bytes 81952 | tf_op jit(solution)/shard_map/ppermute | solution.py:18
  105.8 0.1 fusion.35
  106.0 0.2 fusion.34
  106.2 0.4 convert.13
  106.6 0.1 collective-permute-start.6
  106.7 5.4 %collective-permute-start.7 = (bf16[128,4,256]{2,0,1:T(8,128)(2,1)S(1)}, bf16[128,4,256]{2,0,1:T(8,128)(2,1)S(1)}, u32[]{:S(2)}, u32[]{:S(2)}) collective-permute-start(bf16[128,4,256]{2,0,1:T(8,128)(2,1)S(1)} %get-tuple-element.56), channel_id=1, source_target_pairs={{1,0},{2,1},{3,2},{4,3},{5,4},{6,5},{7,6},{8,7},{9,8},{10,9},{11,1... | collective-permute-start | bytes 786440 | tf_op jit(solution)/shard_map/ppermute | solution.py:18
  112.0 0.2 convolution_bitcast_fusion.2
  112.2 0.3 convolution_bitcast_fusion
  112.5 0.3 slice.173
  112.8 4.7 %collective-permute-done.6 = bf16[128,4,256]{2,0,1:T(8,128)(2,1)S(1)} collective-permute-done((bf16[128,4,256]{2,0,1:T(8,128)(2,1)S(1)}, bf16[128,4,256]{2,0,1:T(8,128)(2,1)S(1)}, u32[]{:S(2)}, u32[]{:S(2)}) %collective-permute-start.6) | collective-permute-done | bytes 262176 | tf_op jit(solution)/shard_map/ppermute | solution.py:17
  117.4 0.1 fusion.32
  117.5 0.1 fusion.31
  117.6 1.9 %convolution_add_fusion = f32[128,32,256]{2,0,1:T(8,128)S(1)} fusion(f32[128,32,256]{2,0,1:T(8,128)S(1)} %fusion.31, f32[128,32,4]{0,1,2:T(8,128)S(1)} %convolution_bitcast_fusion, bf16[256,4]{0,1:T(4,128)(2,1)S(1)} %copy-done.5), kind=kOutput, calls=%fused_computation.25 | convolution fusion | flops 51380224 | bytes 8456192 | tf_op jit(solution)/shard_map/dot_general | solution.py:106
  119.5 4.4 %copy.40 = f32[128,32,256]{2,1,0:T(8,128)} copy(f32[128,32,256]{2,0,1:T(8,128)S(1)} %convolution_add_fusion) | data formatting | bytes 8388608 | tf_op jit(solution)/shard_map/add | solution.py:121
  (33 shorter events, 0.1 us)
Async XLA Ops:
  0.0 76.3 %copy-start = (bf16[256,256]{1,0:T(8,128)(2,1)S(1)}, bf16[256,256]{1,0:T(8,128)(2,1)}, u32[]{:S(2)}) copy-start(bf16[256,256]{1,0:T(8,128)(2,1)} %param.27) | copy-start | bytes 393220
  0.0 7.9 %copy-start.5 = (bf16[256,4]{0,1:T(4,128)(2,1)S(1)}, bf16[256,4]{0,1:T(4,128)(2,1)}, u32[]{:S(2)}) copy-start(bf16[256,4]{0,1:T(4,128)(2,1)} %param.33) | copy-start | bytes 6148
  0.0 8.6 %copy-start.6 = (bf16[128,4]{0,1:T(4,128)(2,1)S(1)}, bf16[128,4]{0,1:T(4,128)(2,1)}, u32[]{:S(2)}) copy-start(bf16[128,4]{0,1:T(4,128)(2,1)} %param.31) | copy-start | bytes 3076
  0.0 8.8 %copy-start.7 = (bf16[32,4]{0,1:T(4,128)(2,1)S(1)}, bf16[32,4]{0,1:T(4,128)(2,1)}, u32[]{:S(2)}) copy-start(bf16[32,4]{0,1:T(4,128)(2,1)} %param.32) | copy-start | bytes 772
  0.0 63.2 %copy-start.11 = (f32[128]{0:T(128)S(1)}, f32[128]{0:T(128)}, u32[]{:S(2)}) copy-start(f32[128]{0:T(128)} %param.38) | copy-start | bytes 1540
  0.0 63.2 %copy-start.12 = (f32[32]{0:T(128)S(1)}, f32[32]{0:T(128)}, u32[]{:S(2)}) copy-start(f32[32]{0:T(128)} %param.37) | copy-start | bytes 388
  0.0 63.3 %copy-start.3 = (f32[32,32]{1,0:T(8,128)S(1)}, f32[32,32]{1,0:T(8,128)}, u32[]{:S(2)}) copy-start(f32[32,32]{1,0:T(8,128)} %param.34) | copy-start | bytes 12292
  0.1 63.7 %copy-start.1 = (f32[128,128]{1,0:T(8,128)S(1)}, f32[128,128]{1,0:T(8,128)}, u32[]{:S(2)}) copy-start(f32[128,128]{1,0:T(8,128)} %param.35) | copy-start | bytes 196612
  0.1 63.9 %copy-start.8 = (f32[4,4]{1,0:T(4,128)S(1)}, f32[4,4]{1,0:T(4,128)}, u32[]{:S(2)}) copy-start(f32[4,4]{1,0:T(4,128)} %param.36) | copy-start | bytes 196
  0.1 63.9 %copy-start.14 = (f32[4]{0:T(128)S(1)}, f32[4]{0:T(128)}, u32[]{:S(2)}) copy-start(f32[4]{0:T(128)} %param.39) | copy-start | bytes 52
  4.6 65.4 %copy-start.9 = (f32[136]{0:T(256)S(1)}, f32[136]{0:T(256)}, u32[]{:S(2)}) copy-start(f32[136]{0:T(256)} %param.28) | copy-start | bytes 1636
  4.6 65.4 %copy-start.10 = (f32[40]{0:T(128)S(1)}, f32[40]{0:T(128)}, u32[]{:S(2)}) copy-start(f32[40]{0:T(128)} %param.29) | copy-start | bytes 484
  4.6 69.1 %copy-start.2 = (bf16[136,136]{1,0:T(8,128)(2,1)S(1)}, bf16[136,136]{1,0:T(8,128)(2,1)}, u32[]{:S(2)}) copy-start(bf16[136,136]{1,0:T(8,128)(2,1)} %param.25) | copy-start | bytes 110980
  4.7 59.9 %collective-permute-start = (bf16[4,32,256]{2,0,1:T(4,128)(2,1)S(1)}, bf16[4,32,256]{2,0,1:T(4,128)(2,1)S(1)}, u32[]{:S(2)}, u32[]{:S(2)}) collective-permute-start(bf16[4,32,256]{2,0,1:T(4,128)(2,1)S(1)} %get-tuple-element.59), channel_id=1, source_target_pairs={{0,32},{32,64},{64,96},{96,128},{128,160},{160,192},{192,224},{224... | collective-permute-start | bytes 196616 | tf_op jit(solution)/shard_map/ppermute | solution.py:17
  7.3 57.3 %collective-permute-start.1 = (bf16[4,32,256]{2,0,1:T(4,128)(2,1)S(1)}, bf16[4,32,256]{2,0,1:T(4,128)(2,1)S(1)}, u32[]{:S(2)}, u32[]{:S(2)}) collective-permute-start(bf16[4,32,256]{2,0,1:T(4,128)(2,1)S(1)} %get-tuple-element.60), channel_id=1, source_target_pairs={{32,0},{64,32},{96,64},{128,96},{160,128},{192,160},{224,192},{0,2... | collective-permute-start | bytes 196616 | tf_op jit(solution)/shard_map/ppermute | solution.py:18
  64.8 8.9 %collective-permute-start.2 = (bf16[136,4,256]{2,0,1:T(8,128)(2,1)S(1)}, bf16[136,4,256]{2,0,1:T(8,128)(2,1)S(1)}, u32[]{:S(2)}, u32[]{:S(2)}) collective-permute-start(bf16[136,4,256]{2,0,1:T(8,128)(2,1)S(1)} %get-tuple-element.57), channel_id=1, source_target_pairs={{0,1},{1,2},{2,3},{3,4},{4,5},{5,6},{6,7},{7,8},{8,9},{9,10},{10,1... | collective-permute-start | bytes 835592 | tf_op jit(solution)/shard_map/ppermute | solution.py:17
  65.6 8.1 %collective-permute-start.3 = (bf16[136,4,256]{2,0,1:T(8,128)(2,1)S(1)}, bf16[136,4,256]{2,0,1:T(8,128)(2,1)S(1)}, u32[]{:S(2)}, u32[]{:S(2)}) collective-permute-start(bf16[136,4,256]{2,0,1:T(8,128)(2,1)S(1)} %get-tuple-element.58), channel_id=1, source_target_pairs={{1,0},{2,1},{3,2},{4,3},{5,4},{6,5},{7,6},{8,7},{9,8},{10,9},{11,1... | collective-permute-start | bytes 835592 | tf_op jit(solution)/shard_map/ppermute | solution.py:18
  70.1 6.2 %copy-start.4 = (bf16[40,40]{1,0:T(8,128)(2,1)S(1)}, bf16[40,40]{1,0:T(8,128)(2,1)}, u32[]{:S(2)}) copy-start(bf16[40,40]{1,0:T(8,128)(2,1)} %param.26) | copy-start | bytes 9604
  76.3 5.9 %copy-start.13 = (f32[256]{0:T(256)S(1)}, f32[256]{0:T(256)}, u32[]{:S(2)}) copy-start(f32[256]{0:T(256)} %param.30) | copy-start | bytes 3076
  87.9 15.2 %collective-permute-start.4 = (bf16[4,40,256]{2,0,1:T(4,128)(2,1)S(1)}, bf16[4,40,256]{2,0,1:T(4,128)(2,1)S(1)}, u32[]{:S(2)}, u32[]{:S(2)}) collective-permute-start(bf16[4,40,256]{2,0,1:T(4,128)(2,1)S(1)} %get-tuple-element.53), channel_id=1, source_target_pairs={{0,32},{32,64},{64,96},{96,128},{128,160},{160,192},{192,224},{224... | collective-permute-start | bytes 245768 | tf_op jit(solution)/shard_map/ppermute | solution.py:17
  101.6 4.2 %collective-permute-start.5 = (bf16[4,40,256]{2,0,1:T(4,128)(2,1)S(1)}, bf16[4,40,256]{2,0,1:T(4,128)(2,1)S(1)}, u32[]{:S(2)}, u32[]{:S(2)}) collective-permute-start(bf16[4,40,256]{2,0,1:T(4,128)(2,1)S(1)} %get-tuple-element.54), channel_id=1, source_target_pairs={{32,0},{64,32},{96,64},{128,96},{160,128},{192,160},{224,192},{0,2... | collective-permute-start | bytes 245768 | tf_op jit(solution)/shard_map/ppermute | solution.py:18
  106.6 10.9 %collective-permute-start.6 = (bf16[128,4,256]{2,0,1:T(8,128)(2,1)S(1)}, bf16[128,4,256]{2,0,1:T(8,128)(2,1)S(1)}, u32[]{:S(2)}, u32[]{:S(2)}) collective-permute-start(bf16[128,4,256]{2,0,1:T(8,128)(2,1)S(1)} %get-tuple-element.55), channel_id=1, source_target_pairs={{0,1},{1,2},{2,3},{3,4},{4,5},{5,6},{6,7},{7,8},{8,9},{9,10},{10,1... | collective-permute-start | bytes 786440 | tf_op jit(solution)/shard_map/ppermute | solution.py:17
  106.7 10.8 %collective-permute-start.7 = (bf16[128,4,256]{2,0,1:T(8,128)(2,1)S(1)}, bf16[128,4,256]{2,0,1:T(8,128)(2,1)S(1)}, u32[]{:S(2)}, u32[]{:S(2)}) collective-permute-start(bf16[128,4,256]{2,0,1:T(8,128)(2,1)S(1)} %get-tuple-element.56), channel_id=1, source_target_pairs={{1,0},{2,1},{3,2},{4,3},{5,4},{6,5},{7,6},{8,7},{9,8},{10,9},{11,1... | collective-permute-start | bytes 786440 | tf_op jit(solution)/shard_map/ppermute | solution.py:18
where the time goes:
time: 124 us
  blocking collectives  54 us (44%)
  starting transfers between devices  27.3 us (22%)
  matrix products  19.1 us (15%)
  waiting for transfers between devices  11.5 us (9%)
  local copies, waits for them, and re-layouts  10.4 us (8%)
  other arithmetic  1.26 us (1%)
    all_gather x1, blocking collectives, local(): coarse_res = lax.all_gather(partial_rows, 'gy', axis=1, tiled=True)  38.5 us
    ppermute x4, starting transfers between devices, with_halo(): before = lax.ppermute(last, axis, up)  17.3 us
    all_gather x1, blocking collectives, local(): partial_rows = lax.all_gather(own_coarse, 'gx', axis=0, tiled=True)  15.5 us
    ppermute x4, starting transfers between devices, with_halo(): after = lax.ppermute(initial, axis, down)  10.1 us
    ppermute x4, waiting for transfers between devices, with_halo(): before = lax.ppermute(last, axis, up)  8.78 us
    dot_general x1, matrix products, solve_local(): jnp.einsum('zc,abz->abc', local_z, first_y, preferred_element_type=jnp.fl...  5.94 us
    dot_general x1, matrix products, solve_local(): jnp.einsum('yb,abz->ayz', local_y, back_z, preferred_element_type=jnp.flo...  4.64 us
    unnamed x31, local copies, waits for them, and re-layouts  4.63 us
  transfers between devices with their start and end apart: 8, of which 4 were waited for; matrix products, arithmetic and copies ran while one was open for 4% of the time, Pallas kernels for 0%

commit v1 on v0

v1 whole, which is shorter than its diff:
```python
import jax
import jax.numpy as jnp
from jax import lax
from jax.experimental import pallas as pl
from jax.experimental.pallas import tpu as pltpu
from jax.sharding import PartitionSpec as P

OV = 4
MODES = 4
CX = 128
CY = 32
NZ = 256
EX = 136
EY = 40
GX = 4
ROWS = GX * EY
BLOCKS = CX // GX
BB = 8
HI = lax.Precision.HIGHEST
f32 = jnp.float32
bf16 = jnp.bfloat16


def dot(a, b):
    return jnp.dot(a, b, preferred_element_type=f32)


def solve_kernel(
    own, xlo, xhi, ylo, yhi, wy, wyt, wx, wxt, lz, lzt, ex, ey, ez,
    fix, out_xlo, out_xhi, out_ylo, out_yhi, field, mid,
):
    own_rows = GX * CY
    halo_rows = GX * OV

    def put(rows, value):
        field[0, rows, :] = value[:, :128]
        field[1, rows, :] = value[:, 128:]

    def take(rows):
        return jnp.concatenate([field[0, rows, :], field[1, rows, :]], 1)

    def forward_y(main, k):
        low = ylo[pl.ds(pl.multiple_of(k * halo_rows, halo_rows), halo_rows), :]
        high = yhi[pl.ds(pl.multiple_of(k * halo_rows, halo_rows), halo_rows), :]
        data = jnp.concatenate([main, low, high], 0)
        put(pl.ds(pl.multiple_of(k * ROWS, ROWS), ROWS), dot(wy[...], data))

    def first(k, carry):
        forward_y(own[pl.ds(pl.multiple_of(k * own_rows, own_rows), own_rows), :], k)
        return carry

    lax.fori_loop(0, BLOCKS, first, 0, unroll=4)
    forward_y(xlo[...], BLOCKS)
    forward_y(xhi[...], BLOCKS + 1)

    def middle(step, carry):
        base = step * BB
        for i in range(BB):
            plane = take(pl.ds(base + i, EX, stride=EY)).astype(bf16)
            mid[i * EX : (i + 1) * EX, :] = dot(wx[...], plane).astype(bf16)
        for i in range(BB):
            rows = slice(i * EX, (i + 1) * EX)
            along = dot(mid[rows, :], lz[...])
            spectral = (along / (ex[...] + (ez[...] + ey[base + i]))).astype(bf16)
            mid[rows, :] = dot(spectral, lzt[...]).astype(bf16)
        for i in range(BB):
            put(pl.ds(base + i, EX, stride=EY), dot(wxt[...], mid[i * EX : (i + 1) * EX, :]))
        return carry

    lax.fori_loop(0, EY // BB, middle, 0)

    def backward_y(k):
        rows = take(pl.ds(pl.multiple_of(k * ROWS, ROWS), ROWS)).astype(bf16)
        return dot(wyt[...], rows)

    def last(k, carry):
        out = backward_y(k)
        fix[pl.ds(pl.multiple_of(k * own_rows, own_rows), own_rows), :] = out[:own_rows]
        at = pl.ds(pl.multiple_of(k * halo_rows, halo_rows), halo_rows)
        out_ylo[at, :] = out[own_rows : own_rows + halo_rows].astype(bf16)
        out_yhi[at, :] = out[own_rows + halo_rows :].astype(bf16)
        return carry

    lax.fori_loop(0, BLOCKS, last, 0, unroll=4)
    out_xlo[...] = backward_y(BLOCKS).astype(bf16)
    out_xhi[...] = backward_y(BLOCKS + 1).astype(bf16)


VM = pl.BlockSpec(memory_space=pltpu.VMEM)
SM = pl.BlockSpec(memory_space=pltpu.SMEM)


def solve(own, xlo, xhi, ylo, yhi, wy, wx, local_z, eig_x, eig_y, eig_z):
    sds = jax.ShapeDtypeStruct
    return pl.pallas_call(
        solve_kernel,
        out_shape=(
            sds((CX * CY, NZ), f32),
            sds((ROWS, NZ), bf16),
            sds((ROWS, NZ), bf16),
            sds((CX * OV, NZ), bf16),
            sds((CX * OV, NZ), bf16),
        ),
        in_specs=[VM] * 12 + [SM, VM],
        out_specs=(VM,) * 5,
        scratch_shapes=[
            pltpu.VMEM((2, EX * EY, NZ // 2), f32),
            pltpu.VMEM((BB * EX, NZ), bf16),
        ],
        name="solve",
    )(
        own, xlo, xhi, ylo, yhi, wy, wy.T, wx, wx.T, local_z, local_z.T,
        eig_x[:, None], eig_y, eig_z[None, :],
    )


def halo_order(w, overlap):
    inner = w.shape[0] - overlap
    return jnp.concatenate([w[overlap:inner], w[:overlap], w[inner:]], 0)


def y_matrix(local_y):
    eye = jnp.eye(GX, dtype=bf16)
    parts = [
        jnp.einsum("ij,yb->ibjy", eye, part).reshape(ROWS, -1)
        for part in (local_y[OV : EY - OV], local_y[:OV], local_y[EY - OV :])
    ]
    return jnp.concatenate(parts, 1)


def split(x):
    high = x.astype(bf16)
    return high, (x - high.astype(f32)).astype(bf16)


def restrict_kernel(residual, basis, own, acc):
    step = pl.program_id(0)

    @pl.when(step == 0)
    def _():
        acc[...] = jnp.zeros_like(acc)

    rounded = residual[...].astype(bf16)
    own[...] = rounded
    acc[...] += dot(basis[...], rounded)


def restrict(residual, basis):
    steps = 8
    rows = CX * CY // steps
    sds = jax.ShapeDtypeStruct
    return pl.pallas_call(
        restrict_kernel,
        grid=(steps,),
        out_shape=(sds((CX * CY, NZ), bf16), sds((32, NZ), f32)),
        in_specs=[
            pl.BlockSpec((rows, NZ), lambda i: (i, 0)),
            pl.BlockSpec((32, rows), lambda i: (0, i)),
        ],
        out_specs=(
            pl.BlockSpec((rows, NZ), lambda i: (i, 0)),
            pl.BlockSpec((32, NZ), lambda i: (0, 0)),
        ),
        name="restrict",
    )(residual, basis)


def combine_kernel(fix, basis, shape, rxlo, rxhi, rylo, ryhi, out):
    step = pl.program_id(0)
    total = fix[...] + dot(basis[...], shape[...])
    planes = total.reshape(-1, CY, NZ)
    low = rylo[...].astype(f32).reshape(-1, OV, NZ)
    high = ryhi[...].astype(f32).reshape(-1, OV, NZ)
    zeros = jnp.zeros((planes.shape[0], CY - 2 * OV, NZ), f32)
    planes = planes + jnp.concatenate([low, zeros, high], 1)
    out[...] = planes.reshape(-1, NZ)

    @pl.when(step == 0)
    def _():
        out[: GX * CY, :] += rxlo[: GX * CY, :].astype(f32)

    @pl.when(step == pl.num_programs(0) - 1)
    def _():
        out[out.shape[0] - GX * CY :, :] += rxhi[: GX * CY, :].astype(f32)


def combine(fix, basis, shape, rxlo, rxhi, rylo, ryhi):
    steps = 8
    rows = CX * CY // steps
    rim = CX * OV // steps
    whole = lambda i: (0, 0)
    part = lambda i: (i, 0)
    return pl.pallas_call(
        combine_kernel,
        grid=(steps,),
        out_shape=jax.ShapeDtypeStruct((CX * CY, NZ), f32),
        in_specs=[
            pl.BlockSpec((rows, NZ), part),
            pl.BlockSpec((rows, 64), part),
            pl.BlockSpec((64, NZ), whole),
            pl.BlockSpec((ROWS, NZ), whole),
            pl.BlockSpec((ROWS, NZ), whole),
            pl.BlockSpec((rim, NZ), part),
            pl.BlockSpec((rim, NZ), part),
        ],
        out_specs=pl.BlockSpec((rows, NZ), part),
        name="combine",
    )(fix, basis, shape, rxlo, rxhi, rylo, ryhi)


def shift(x, axis, step):
    size = lax.axis_size(axis)
    return lax.ppermute(x, axis, [(i, (i + step) % size) for i in range(size)])


def gather(x, axis):
    size = lax.axis_size(axis)
    return lax.all_to_all(jnp.broadcast_to(x[None], (size,) + x.shape), axis, 0, 0)


def local(
    residual, local_x, local_y, local_z, eig_x, eig_y, eig_z, coarse_x, coarse_y, coarse_z,
    mode_x, mode_y, mode_z, coarse_eig_x, coarse_eig_y, coarse_eig_z,
):
    low_x = residual[:OV].astype(bf16).reshape(OV * CY, NZ)
    high_x = residual[CX - OV :].astype(bf16).reshape(OV * CY, NZ)
    xlo = shift(high_x, "gx", 1)
    xhi = shift(low_x, "gx", -1)

    def rim(lo, hi, at):
        cut = slice(0, OV) if at == 0 else slice(CY - OV, CY)
        own_rim = residual[:, cut].astype(bf16).reshape(CX * OV, NZ)
        parts = [part.reshape(OV, CY, NZ)[:, cut].reshape(OV * OV, NZ) for part in (lo, hi)]
        return jnp.concatenate([own_rim] + parts, 0)

    ylo = shift(rim(xlo, xhi, 1), "gy", 1)
    yhi = shift(rim(xlo, xhi, 0), "gy", -1)

    basis = (
        coarse_x.astype(f32)[:, None, :, None] * coarse_y.astype(f32)[None, :, None, :]
    ).reshape(CX * CY, MODES * MODES)
    basis_high, basis_low = split(basis)
    both = jnp.concatenate([basis_high, basis_low], 1)
    own, acc = restrict(residual.reshape(CX * CY, NZ), both.T)
    own_coarse = jnp.dot(acc[:16] + acc[16:], coarse_z.astype(f32), precision=HI)
    own_coarse = own_coarse.reshape(MODES, MODES, MODES).transpose(1, 0, 2).reshape(MODES, 16)
    modes_xz = jnp.einsum("Ia,pc->Ipac", mode_x, mode_z, precision=HI).reshape(128, 128)
    rows_x = gather(own_coarse, "gx")
    rows_x = rows_x.transpose(1, 0, 2).reshape(MODES, 128)
    part = jnp.dot(rows_x, modes_xz, precision=HI)

    wy = y_matrix(local_y)
    wx = halo_order(local_x, OV).T
    fix, out_xlo, out_xhi, out_ylo, out_yhi = solve(
        own, xlo, xhi, ylo, yhi, wy, wx, local_z, eig_x, eig_y, eig_z
    )

    rxlo = shift(out_xhi, "gx", 1)
    rxhi = shift(out_xlo, "gx", -1)
    edge = GX * CY
    width = GX * OV

    def folded(strip, start):
        rows = slice(start, start + width)
        strip = strip.astype(f32)
        strip = strip.at[:width].add(rxlo[rows].astype(f32))
        strip = strip.at[CX * OV - width :].add(rxhi[rows].astype(f32))
        return strip.astype(bf16)

    rylo = shift(folded(out_yhi, edge + width), "gy", 1)
    ryhi = shift(folded(out_ylo, edge), "gy", -1)

    columns = gather(part, "gy").reshape(128, 128)
    row_index = lax.axis_index("gx")
    col_index = lax.axis_index("gy")
    rows_y = lax.dynamic_slice_in_dim(mode_y, col_index * MODES, MODES, 0)
    eig_xz = (coarse_eig_x[:, None] + coarse_eig_z[None, :]).reshape(1, 128)
    hat = jnp.dot(mode_y.T, columns, precision=HI) / (coarse_eig_y[:, None] + eig_xz)
    rows_xz = lax.dynamic_slice_in_dim(modes_xz, row_index * 16, 16, 0)
    sol = jnp.dot(rows_y, jnp.dot(hat, rows_xz.T, precision=HI), precision=HI)
    sol = sol.reshape(MODES, MODES, MODES).transpose(1, 0, 2).reshape(16, MODES)
    shape = jnp.dot(sol, coarse_z.astype(f32).T, precision=HI)
    shape_high, shape_low = split(shape)
    shape4 = jnp.concatenate([shape_high, shape_low, shape_high, shape_low], 0)
    basis4 = jnp.concatenate([basis_high, basis_high, basis_low, basis_low], 1)

    out = combine(fix, basis4, shape4, rxlo, rxhi, rylo, ryhi)
    return out.reshape(CX, CY, NZ)


def solution(mesh):
    placed = (P("gx", "gy", None),) + (P(),) * 15
    return jax.shard_map(
        local, mesh=mesh, in_specs=placed, out_specs=P("gx", "gy", None), check_vma=False
    )
```

time: 124 us -> 102 us (0.82)
  blocking collectives: 54 us -> 0 us
  Pallas kernels: 0 us -> 26.8 us
  matrix products: 19.1 us -> 1.77 us
  other arithmetic: 1.26 us -> 11.5 us
  local copies, waits for them, and re-layouts: 10.4 us -> 15.3 us
  starting transfers between devices: 27.3 us -> 30.8 us
  waiting for transfers between devices: 11.5 us -> 15 us
    all_gather x2 -> x0, blocking collectives: 54 us -> none  [the longest x1 38.5 us: local(): coarse_res = lax.all_gather(partial_rows, 'gy', axis=1, tiled=True)]
    pallas_call x0 -> x3, Pallas kernels: none -> 26.8 us  [the longest x1 13 us: solve(): pl.pallas_call(solve_kernel, out_shape=(sds((CX * CY, NZ), f32), sds((ROW...]
    dot_general x16 -> x6, matrix products: 19.1 us -> 1.77 us  [the longest x1 0.85 us: local(): jnp.dot(acc[:16] + acc[16:], coarse_z.astype(f32), precision=HI)]
    all_to_all x0 -> x2, starting transfers between devices: none -> 15.7 us  [gather(): lax.all_to_all(jnp.broadcast_to(x[None], (size,) + x.shape), axis, 0, 0)]
    ppermute x8, starting transfers between devices: 27.3 us -> 15.1 us  [shift(): return lax.ppermute(x, axis, [(i, (i + step) % size) for i in range(size)])]
    add x1, local copies, waits for them, and re-layouts: 4.44 us -> 0.1 us  [local(): eig_xz = (coarse_eig_x[:, None] + coarse_eig_z[None, :]).reshape(1, 128)]
    convert_element_type x0 -> x8, other arithmetic: none -> 3.9 us  [the longest x2 1.98 us: folded(): strip = strip.astype(f32)]
    concatenate x0 -> x5, other arithmetic: none -> 3.51 us  [the longest x1 2.2 us: local(): basis4 = jnp.concatenate([basis_high, basis_high, basis_low, basis_low], 1)]
  transfers between devices with their start and end apart: 8 -> 10, of which waited for: 4 -> 4; matrix products, arithmetic and copies ran while one was open for 4% -> 23% of each run, Pallas kernels for 0% -> 6%
where the time goes in v1:
time: 102 us
  starting transfers between devices  30.8 us (30%)
  Pallas kernels  26.8 us (26%)
  local copies, waits for them, and re-layouts  15.3 us (15%)
  waiting for transfers between devices  15 us (15%)
  other arithmetic  11.5 us (11%)
  matrix products  1.77 us (2%)
    all_to_all x2, starting transfers between devices, gather(): lax.all_to_all(jnp.broadcast_to(x[None], (size,) + x.shape), axis, 0, 0)  15.7 us
    ppermute x8, starting transfers between devices, shift(): return lax.ppermute(x, axis, [(i, (i + step) % size) for i in range(size)])  15.1 us
    pallas_call x1, Pallas kernels, solve(): pl.pallas_call(solve_kernel, out_shape=(sds((CX * CY, NZ), f32), sds((ROW...  13 us
    ppermute x8, waiting for transfers between devices, shift(): return lax.ppermute(x, axis, [(i, (i + step) % size) for i in range(size)])  11.9 us
    pallas_call x1, Pallas kernels, combine(): pl.pallas_call(combine_kernel, grid=(steps,), out_shape=jax.ShapeDtypeStr...  7.63 us
    pallas_call x1, Pallas kernels, restrict(): pl.pallas_call(restrict_kernel, grid=(steps,), out_shape=(sds((CX * CY, N...  6.23 us
    all_to_all x2, waiting for transfers between devices, gather(): lax.all_to_all(jnp.broadcast_to(x[None], (size,) + x.shape), axis, 0, 0)  3.06 us
    another operation x2, other arithmetic  2.55 us
  transfers between devices with their start and end apart: 10, of which 4 were waited for; matrix products, arithmetic and copies ran while one was open for 23% of the time, Pallas kernels for 6%

profile of v1, /device:TPU:1, one launch (start us, length us, event | category | flops | bytes accessed | tf_op | source)
XLA Modules:
  0.0 101.6 jit_solution(11099229955827139106)
XLA Ops:
  0.0 2.5 %convert.15 = bf16[128,32,256]{2,1,0:T(8,128)(2,1)S(1)} convert(f32[128,32,256]{2,1,0:T(8,128)} %param.24) | non-fusion elementwise | flops 1048576 | bytes 6291456 | tf_op jit(solution)/shard_map/convert.6
  2.6 0.7 fusion.18
  3.3 2.6 %collective-permute-start = (bf16[128,256]{1,0:T(8,128)(2,1)}, bf16[128,256]{1,0:T(8,128)(2,1)S(1)}, u32[]{:S(2)}, u32[]{:S(2)}) collective-permute-start(bf16[128,256]{1,0:T(8,128)(2,1)} %bitcast.2), channel_id=1, source_target_pairs={{0,32},{32,64},{64,96},{96,128},{128,160},{160,192},{192,224},{224... | collective-permute-start | bytes 196616 | tf_op jit(solution)/shard_map/ppermute | solution.py:213
  5.9 0.6 collective-permute-start.1
  6.5 0.2 broadcast_multiply_fusion
  6.7 0.5 mul.26
  7.2 0.6 copy.45
  7.8 1.7 %copy.46 = f32[4096,16]{1,0:T(8,128)} copy(bf16[4096,16]{0,1:T(8,128)(2,1)S(1)} %convert_element_type.57) | data formatting | bytes 393216 | tf_op jit(solution)/shard_map/convert_element_type | solution.py:133
  9.5 1.8 %subtract_convert_fusion = bf16[4096,16]{1,0:T(8,128)(2,1)S(1)} fusion(f32[4096,16]{1,0:T(8,128)S(1)} %copy.45, f32[4096,16]{1,0:T(8,128)} %copy.46), kind=kLoop, calls=%fused_computation.1 | loop fusion | flops 131072 | bytes 655360 | tf_op jit(solution)/shard_map/convert_element_type | solution.py:133
  11.3 0.3 copy.47
  11.6 0.8 maximum_bitcast_fusion.basis
  12.4 6.2 %restrict.1 = (bf16[4096,256]{1,0:T(8,128)(2,1)}, f32[32,256]{1,0:T(8,128)}) custom-call(f32[4096,256]{1,0:T(8,128)} %bitcast.55, bf16[32,4096]{1,0:T(8,128)(2,1)} %maximum_bitcast_fusion.basis), custom_call_target="tpu_custom_call" | custom-call | tf_op jit(solution)/shard_map/restrict/pallas_call | solution.py:152
  18.6 0.9 fusion.5
  19.8 0.6 broadcast_in_dim.13
  20.4 6.2 %all-to-all-start = ((f32[8,4,16]{2,1,0:T(4,128)}), f32[8,4,16]{2,1,0:T(4,128)S(1)}, u32[]{:S(2)}, u32[]{:S(2)}) async-start(f32[8,4,16]{2,1,0:T(4,128)} %broadcast_in_dim.13), calls=%async_computation | async-start | bytes 32768 | tf_op jit(solution)/shard_map/all_to_all | solution.py:218
  26.7 0.5 copy.52
  27.2 1.4 %fusion.17 = (bf16[128,4,256]{2,1,0:T(4,128)(2,1)S(1)}, bf16[128,4,256]{2,1,0:T(4,128)(2,1)S(1)}) fusion(bf16[128,32,256]{2,1,0:T(8,128)(2,1)} %copy-done.1), kind=kLoop, calls=%fused_computation.40 | loop fusion | bytes 1048576 | tf_op jit(solution)/shard_map/slice | solution.py:232
  29.2 2.2 %pad_maximum_fusion.basis = bf16[4096,64]{1,0:T(8,128)(2,1)} fusion(bf16[4096,16]{1,0:T(8,128)(2,1)S(1)} %subtract_convert_fusion, bf16[4096,16]{1,0:T(8,128)(2,1)S(1)} %copy.52), kind=kLoop, calls=%fused_computation.4 | loop fusion | flops 2097152 | bytes 786432 | tf_op jit(solution)/shard_map/concatenate | solution.py:285
  31.5 0.3 multiply_bitcast_fusion
  31.8 0.7 pad_maximum_fusion.3
  32.6 0.7 copy.51.ex
  33.3 0.7 copy.50.wx
  34.0 0.7 copy.49.wy
  34.8 0.8 copy.48
  35.7 1.6 %reshape.202 = f32[128,128]{1,0:T(8,128)S(1)} reshape(f32[32,4,32,4]{3,2,1,0:T(8,128)S(1)} %multiply_bitcast_fusion) | data formatting | bytes 131072 | tf_op jit(solution)/shard_map/reshape | solution.py:247
  37.4 0.2 fusion.23
  37.6 0.7 broadcast_in_dim.28
  38.2 9.5 %all-to-all-start.1 = ((f32[32,4,128]{2,1,0:T(4,128)}), f32[32,4,128]{2,1,0:T(4,128)S(1)}, u32[]{:S(2)}, u32[]{:S(2)}) async-start(f32[32,4,128]{2,1,0:T(4,128)} %broadcast_in_dim.28), calls=%async_computation.1 | async-start | bytes 131072 | tf_op jit(solution)/shard_map/all_to_all | solution.py:218
  47.8 0.7 fusion.21
  48.6 1.3 %collective-permute-start.2 = (bf16[544,256]{1,0:T(8,128)(2,1)S(1)}, bf16[544,256]{1,0:T(8,128)(2,1)S(1)}, u32[]{:S(2)}, u32[]{:S(2)}) collective-permute-start(bf16[544,256]{1,0:T(8,128)(2,1)S(1)} %pad_maximum_fusion.1), channel_id=1, source_target_pairs={{0,1},{1,2},{2,3},{3,4},{4,5},{5,6},{6,7},{7,8},{8,9},{9,10},{10,1... | collective-permute-start | bytes 835592 | tf_op jit(solution)/shard_map/ppermute | solution.py:213
  50.0 3.6 %collective-permute-start.3 = (bf16[544,256]{1,0:T(8,128)(2,1)S(1)}, bf16[544,256]{1,0:T(8,128)(2,1)S(1)}, u32[]{:S(2)}, u32[]{:S(2)}) collective-permute-start(bf16[544,256]{1,0:T(8,128)(2,1)S(1)} %pad_maximum_fusion.2), channel_id=1, source_target_pairs={{0,31},{1,0},{2,1},{3,2},{4,3},{5,4},{6,5},{7,6},{8,7},{9,8},{10,9... | collective-permute-start | bytes 835592 | tf_op jit(solution)/shard_map/ppermute | solution.py:213
  53.6 3.1 %all-to-all-done.1 = f32[32,4,128]{2,1,0:T(4,128)S(1)} async-done(((f32[32,4,128]{2,1,0:T(4,128)}), f32[32,4,128]{2,1,0:T(4,128)S(1)}, u32[]{:S(2)}, u32[]{:S(2)}) %all-to-all-start.1) | async-done | bytes 65568 | tf_op jit(solution)/shard_map/all_to_all | solution.py:218
  56.7 0.3 fusion
  57.0 0.2 fusion.9
  57.1 4.2 %collective-permute-done.2.ylo = bf16[544,256]{1,0:T(8,128)(2,1)S(1)} collective-permute-done((bf16[544,256]{1,0:T(8,128)(2,1)S(1)}, bf16[544,256]{1,0:T(8,128)(2,1)S(1)}, u32[]{:S(2)}, u32[]{:S(2)}) %collective-permute-start.2) | collective-permute-done | bytes 278560 | tf_op jit(solution)/shard_map/ppermute | solution.py:213
  61.3 0.7 copy-done.6
  62.2 13.0 %solve.1 = (f32[4096,256]{1,0:T(8,128)}, bf16[160,256]{1,0:T(8,128)(2,1)}, bf16[160,256]{1,0:T(8,128)(2,1)}, bf16[512,256]{1,0:T(8,128)(2,1)}, bf16[512,256]{1,0:T(8,128)(2,1)}) custom-call(bf16[4096,256]{1,0:T(8,128)(2,1)} %get-tuple-element.60.own, bf16[128,256]{1,0:T(8,128)(2,1)} %copy-done.12, bf16[128,256]{1,0:T(8,128)(2,1)} %collective-permute-done.1.xhi, ...), custom_call_target="tpu_custom_call" | custom-call | tf_op jit(solution)/shard_map/solve/pallas_call | solution.py:95
  75.1 2.1 %collective-permute-start.4 = (bf16[160,256]{1,0:T(8,128)(2,1)}, bf16[160,256]{1,0:T(8,128)(2,1)S(1)}, u32[]{:S(2)}, u32[]{:S(2)}) collective-permute-start(bf16[160,256]{1,0:T(8,128)(2,1)} %get-tuple-element.63), channel_id=1, source_target_pairs={{0,32},{32,64},{64,96},{96,128},{128,160},{160,192},{192,224},{224... | collective-permute-start | bytes 245768 | tf_op jit(solution)/shard_map/ppermute | solution.py:213
  77.2 0.1 fusion.11
  77.6 1.0 convert_element_type.63
  78.6 1.0 convert_element_type.67
  79.7 2.1 %collective-permute-done.5.rxhi = bf16[160,256]{1,0:T(8,128)(2,1)S(1)} collective-permute-done((bf16[160,256]{1,0:T(8,128)(2,1)}, bf16[160,256]{1,0:T(8,128)(2,1)S(1)}, u32[]{:S(2)}, u32[]{:S(2)}) %collective-permute-start.5) | collective-permute-done | bytes 81952 | tf_op jit(solution)/shard_map/ppermute | solution.py:213
  81.9 4.8 %collective-permute-start.7 = (bf16[512,256]{1,0:T(8,128)(2,1)S(1)}, bf16[512,256]{1,0:T(8,128)(2,1)S(1)}, u32[]{:S(2)}, u32[]{:S(2)}) collective-permute-start(bf16[512,256]{1,0:T(8,128)(2,1)S(1)} %convert_element_type.70), channel_id=1, source_target_pairs={{0,31},{1,0},{2,1},{3,2},{4,3},{5,4},{6,5},{7,6},{8,7},{9,8},{10,9... | collective-permute-start | bytes 786440 | tf_op jit(solution)/shard_map/ppermute | solution.py:213
  86.7 0.2 subtract_convert_fusion.1
  86.9 0.6 pad_maximum_fusion.4.shape
  87.5 5.6 %collective-permute-done.6.rylo = bf16[512,256]{1,0:T(8,128)(2,1)S(1)} collective-permute-done((bf16[512,256]{1,0:T(8,128)(2,1)S(1)}, bf16[512,256]{1,0:T(8,128)(2,1)S(1)}, u32[]{:S(2)}, u32[]{:S(2)}) %collective-permute-start.6) | collective-permute-done | bytes 262176 | tf_op jit(solution)/shard_map/ppermute | solution.py:213
  93.2 0.7 copy-done.8
  93.9 7.6 %combine.1 = f32[4096,256]{1,0:T(8,128)} custom-call(f32[4096,256]{1,0:T(8,128)} %get-tuple-element.61.fix, bf16[4096,64]{1,0:T(8,128)(2,1)} %pad_maximum_fusion.basis, bf16[64,256]{1,0:T(8,128)(2,1)} %pad_maximum_fusion.4.shape, bf16[160,256]{1,0:T(8,128)(2,1)} %copy-done.10, bf16[160,256]{1,0:T(8,128)(2,1)} %copy-done.11, bf16[512,256]{1,0:T(8,128)(2,1)} %copy-done.8, ...), custom_call_target="tpu_custom_call" | custom-call | tf_op jit(solution)/shard_map/combine/pallas_call | solution.py:193
  (93 shorter events, 2.1 us)
Async XLA Ops:
  0.0 56.7 %copy-start = (f32[128,128]{1,0:T(8,128)S(1)}, f32[128,128]{1,0:T(8,128)}, u32[]{:S(2)}) copy-start(f32[128,128]{1,0:T(8,128)} %param.35) | copy-start | bytes 196612
  0.0 6.5 %copy-start.19 = (bf16[128,4]{0,1:T(4,128)(2,1)S(1)}, bf16[128,4]{0,1:T(4,128)(2,1)}, u32[]{:S(2)}) copy-start(bf16[128,4]{0,1:T(4,128)(2,1)} %param.31) | copy-start | bytes 3076
  0.0 6.5 %copy-start.20 = (bf16[32,4]{0,1:T(4,128)(2,1)S(1)}, bf16[32,4]{0,1:T(4,128)(2,1)}, u32[]{:S(2)}) copy-start(bf16[32,4]{0,1:T(4,128)(2,1)} %param.32) | copy-start | bytes 772
  2.6 3.9 %copy-start.1 = (bf16[128,32,256]{2,1,0:T(8,128)(2,1)}, bf16[128,32,256]{2,1,0:T(8,128)(2,1)S(1)}, u32[]{:S(2)}) copy-start(bf16[128,32,256]{2,1,0:T(8,128)(2,1)S(1)} %convert.15) | copy-start | bytes 6291460
  3.3 44.5 %collective-permute-start = (bf16[128,256]{1,0:T(8,128)(2,1)}, bf16[128,256]{1,0:T(8,128)(2,1)S(1)}, u32[]{:S(2)}, u32[]{:S(2)}) collective-permute-start(bf16[128,256]{1,0:T(8,128)(2,1)} %bitcast.2), channel_id=1, source_target_pairs={{0,32},{32,64},{64,96},{96,128},{128,160},{160,192},{192,224},{224... | collective-permute-start | bytes 196616 | tf_op jit(solution)/shard_map/ppermute | solution.py:213
  5.9 41.9 %collective-permute-start.1 = (bf16[128,256]{1,0:T(8,128)(2,1)}, bf16[128,256]{1,0:T(8,128)(2,1)}, u32[]{:S(2)}, u32[]{:S(2)}) collective-permute-start(bf16[128,256]{1,0:T(8,128)(2,1)} %bitcast.3), channel_id=1, source_target_pairs={{0,224},{32,0},{64,32},{96,64},{128,96},{160,128},{192,160},{224,1... | collective-permute-start | bytes 196616 | tf_op jit(solution)/shard_map/ppermute | solution.py:213
  7.2 0.6 copy-start.2
  9.5 2.2 %copy-start.3 = (bf16[4096,16]{0,1:T(8,128)(2,1)S(1)}, bf16[4096,16]{0,1:T(8,128)(2,1)}, u32[]{:S(2)}) copy-start(bf16[4096,16]{0,1:T(8,128)(2,1)} %copy-done.2) | copy-start | bytes 393220
  12.4 6.2 %copy-start.16 = (bf16[256,4]{0,1:T(4,128)(2,1)S(1)}, bf16[256,4]{0,1:T(4,128)(2,1)}, u32[]{:S(2)}) copy-start(bf16[256,4]{0,1:T(4,128)(2,1)} %param.33) | copy-start | bytes 6148
  12.4 14.2 %copy-start.15 = (bf16[40,40]{1,0:T(8,128)(2,1)S(1)}, bf16[40,40]{1,0:T(8,128)(2,1)}, u32[]{:S(2)}) copy-start(bf16[40,40]{1,0:T(8,128)(2,1)} %param.26) | copy-start | bytes 9604
  12.4 14.2 %copy-start.13 = (bf16[136,136]{1,0:T(8,128)(2,1)S(1)}, bf16[136,136]{1,0:T(8,128)(2,1)}, u32[]{:S(2)}) copy-start(bf16[136,136]{1,0:T(8,128)(2,1)} %param.25) | copy-start | bytes 110980
  20.4 16.9 %all-to-all-start = ((f32[8,4,16]{2,1,0:T(4,128)}), f32[8,4,16]{2,1,0:T(4,128)S(1)}, u32[]{:S(2)}, u32[]{:S(2)}) async-start(f32[8,4,16]{2,1,0:T(4,128)} %broadcast_in_dim.13), calls=%async_computation | async-start | bytes 32768 | tf_op jit(solution)/shard_map/all_to_all | solution.py:218
  28.6 2.8 %copy-start.21 = (f32[4]{0:T(128)S(1)}, f32[4]{0:T(128)}, u32[]{:S(2)}) copy-start(f32[4]{0:T(128)} %param.39) | copy-start | bytes 52
  28.6 2.8 %copy-start.22 = (f32[32]{0:T(128)S(1)}, f32[32]{0:T(128)}, u32[]{:S(2)}) copy-start(f32[32]{0:T(128)} %param.37) | copy-start | bytes 388
  28.6 2.9 %copy-start.14 = (f32[32,32]{1,0:T(8,128)S(1)}, f32[32,32]{1,0:T(8,128)}, u32[]{:S(2)}) copy-start(f32[32,32]{1,0:T(8,128)} %param.34) | copy-start | bytes 12292
  28.6 2.8 %copy-start.17 = (f32[4,4]{1,0:T(4,128)S(1)}, f32[4,4]{1,0:T(4,128)}, u32[]{:S(2)}) copy-start(f32[4,4]{1,0:T(4,128)} %param.36) | copy-start | bytes 196
  29.2 3.4 %copy-start.18 = (f32[136]{0:T(256)S(1)}, f32[136]{0:T(256)}, u32[]{:S(2)}) copy-start(f32[136]{0:T(256)} %param.28) | copy-start | bytes 1636
  31.4 3.4 %copy-start.5 = (bf16[256,256]{1,0:T(8,128)(2,1)S(1)}, bf16[256,256]{1,0:T(8,128)(2,1)}, u32[]{:S(2)}) copy-start(bf16[256,256]{1,0:T(8,128)(2,1)} %lz.1) | copy-start | bytes 393220
  32.4 5.8 %copy-start.4 = (bf16[160,160]{0,1:T(8,128)(2,1)}, bf16[160,160]{0,1:T(8,128)(2,1)S(1)}, u32[]{:S(2)}) copy-start(bf16[160,160]{0,1:T(8,128)(2,1)S(1)} %constant_dynamic-update-slice_fusion) | copy-start | bytes 153604
  35.6 21.1 %copy-start.23 = (f32[128]{0:T(128)S(1)}, f32[128]{0:T(128)}, u32[]{:S(2)}) copy-start(f32[128]{0:T(128)} %param.38) | copy-start | bytes 1540
  38.2 18.4 %all-to-all-start.1 = ((f32[32,4,128]{2,1,0:T(4,128)}), f32[32,4,128]{2,1,0:T(4,128)S(1)}, u32[]{:S(2)}, u32[]{:S(2)}) async-start(f32[32,4,128]{2,1,0:T(4,128)} %broadcast_in_dim.28), calls=%async_computation.1 | async-start | bytes 131072 | tf_op jit(solution)/shard_map/all_to_all | solution.py:218
  47.8 13.6 %copy-start.12 = (bf16[128,256]{1,0:T(8,128)(2,1)}, bf16[128,256]{1,0:T(8,128)(2,1)S(1)}, u32[]{:S(2)}) copy-start(bf16[128,256]{1,0:T(8,128)(2,1)S(1)} %collective-permute-done.xlo) | copy-start | bytes 196612
  48.6 12.7 %collective-permute-start.2 = (bf16[544,256]{1,0:T(8,128)(2,1)S(1)}, bf16[544,256]{1,0:T(8,128)(2,1)S(1)}, u32[]{:S(2)}, u32[]{:S(2)}) collective-permute-start(bf16[544,256]{1,0:T(8,128)(2,1)S(1)} %pad_maximum_fusion.1), channel_id=1, source_target_pairs={{0,1},{1,2},{2,3},{3,4},{4,5},{5,6},{6,7},{7,8},{8,9},{9,10},{10,1... | collective-permute-start | bytes 835592 | tf_op jit(solution)/shard_map/ppermute | solution.py:213
  50.0 11.4 %collective-permute-start.3 = (bf16[544,256]{1,0:T(8,128)(2,1)S(1)}, bf16[544,256]{1,0:T(8,128)(2,1)S(1)}, u32[]{:S(2)}, u32[]{:S(2)}) collective-permute-start(bf16[544,256]{1,0:T(8,128)(2,1)S(1)} %pad_maximum_fusion.2), channel_id=1, source_target_pairs={{0,31},{1,0},{2,1},{3,2},{4,3},{5,4},{6,5},{7,6},{8,7},{9,8},{10,9... | collective-permute-start | bytes 835592 | tf_op jit(solution)/shard_map/ppermute | solution.py:213
  61.3 0.7 copy-start.6
  61.3 0.8 copy-start.7
  75.1 4.5 %collective-permute-start.4 = (bf16[160,256]{1,0:T(8,128)(2,1)}, bf16[160,256]{1,0:T(8,128)(2,1)S(1)}, u32[]{:S(2)}, u32[]{:S(2)}) collective-permute-start(bf16[160,256]{1,0:T(8,128)(2,1)} %get-tuple-element.63), channel_id=1, source_target_pairs={{0,32},{32,64},{64,96},{96,128},{128,160},{160,192},{192,224},{224... | collective-permute-start | bytes 245768 | tf_op jit(solution)/shard_map/ppermute | solution.py:213
  77.6 4.1 %collective-permute-start.5 = (bf16[160,256]{1,0:T(8,128)(2,1)}, bf16[160,256]{1,0:T(8,128)(2,1)S(1)}, u32[]{:S(2)}, u32[]{:S(2)}) collective-permute-start(bf16[160,256]{1,0:T(8,128)(2,1)} %get-tuple-element.64), channel_id=1, source_target_pairs={{0,224},{32,0},{64,32},{96,64},{128,96},{160,128},{192,160},{224,1... | collective-permute-start | bytes 245768 | tf_op jit(solution)/shard_map/ppermute | solution.py:213
  79.6 13.5 %copy-start.10 = (bf16[160,256]{1,0:T(8,128)(2,1)}, bf16[160,256]{1,0:T(8,128)(2,1)S(1)}, u32[]{:S(2)}) copy-start(bf16[160,256]{1,0:T(8,128)(2,1)S(1)} %collective-permute-done.4.rxlo) | copy-start | bytes 245764
  81.7 11.4 %copy-start.11 = (bf16[160,256]{1,0:T(8,128)(2,1)}, bf16[160,256]{1,0:T(8,128)(2,1)S(1)}, u32[]{:S(2)}) copy-start(bf16[160,256]{1,0:T(8,128)(2,1)S(1)} %collective-permute-done.5.rxhi) | copy-start | bytes 245764
  81.8 11.3 %collective-permute-start.6 = (bf16[512,256]{1,0:T(8,128)(2,1)S(1)}, bf16[512,256]{1,0:T(8,128)(2,1)S(1)}, u32[]{:S(2)}, u32[]{:S(2)}) collective-permute-start(bf16[512,256]{1,0:T(8,128)(2,1)S(1)} %convert_element_type.66), channel_id=1, source_target_pairs={{0,1},{1,2},{2,3},{3,4},{4,5},{5,6},{6,7},{7,8},{8,9},{9,10},{10,1... | collective-permute-start | bytes 786440 | tf_op jit(solution)/shard_map/ppermute | solution.py:213
  81.9 11.2 %collective-permute-start.7 = (bf16[512,256]{1,0:T(8,128)(2,1)S(1)}, bf16[512,256]{1,0:T(8,128)(2,1)S(1)}, u32[]{:S(2)}, u32[]{:S(2)}) collective-permute-start(bf16[512,256]{1,0:T(8,128)(2,1)S(1)} %convert_element_type.70), channel_id=1, source_target_pairs={{0,31},{1,0},{2,1},{3,2},{4,3},{5,4},{6,5},{7,6},{8,7},{9,8},{10,9... | collective-permute-start | bytes 786440 | tf_op jit(solution)/shard_map/ppermute | solution.py:213
  93.1 0.7 copy-start.8
  93.1 0.8 copy-start.9

commit v2 on v0

v2 whole, which is shorter than its diff:
```python
import jax
import jax.numpy as jnp
from jax import lax
from jax.experimental import pallas as pl
from jax.experimental.pallas import tpu as pltpu
from jax.sharding import Mesh, PartitionSpec as P

OV = 4
MODES = 4
CX = 128
CY = 32
NZ = 256
EX = 136
EY = 40
GX = 4
ROWS = GX * EY
OWN = GX * CY
RIM = GX * OV
BLOCKS = CX // GX
CELLS = CX * CY
CHUNKS = 8
HI = lax.Precision.HIGHEST
f32 = jnp.float32
bf16 = jnp.bfloat16
sds = jax.ShapeDtypeStruct

VM = pl.BlockSpec(memory_space=pltpu.VMEM)
SM = pl.BlockSpec(memory_space=pltpu.SMEM)
ANY = pl.BlockSpec(memory_space=pl.ANY)


def dot(a, b):
    return jnp.dot(a, b, preferred_element_type=f32)


def dot_t(a, b):
    return lax.dot_general(a, b, (((1,), (1,)), ((), ())), preferred_element_type=f32)


def dot_hi(a, b):
    return jnp.dot(a, b, preferred_element_type=f32, precision=HI)


def dot_t_hi(a, b):
    dims = (((1,), (1,)), ((), ()))
    return lax.dot_general(a, b, dims, preferred_element_type=f32, precision=HI)


def split(x):
    high = x.astype(bf16)
    return high, (x - high.astype(f32)).astype(bf16)


def iotas(shape):
    return lax.broadcasted_iota(jnp.int32, shape, 0), lax.broadcasted_iota(jnp.int32, shape, 1)


def pick(mask, kind=bf16):
    return jnp.where(mask, 1.0, 0.0).astype(kind)


def call(kernel, name, out_shape, in_specs, mib, out_specs=None, scratch=()):
    if out_specs is None:
        out_specs = jax.tree.map(lambda _: VM, out_shape)
    return pl.pallas_call(
        kernel,
        out_shape=out_shape,
        in_specs=in_specs,
        out_specs=out_specs,
        scratch_shapes=list(scratch),
        compiler_params=pltpu.CompilerParams(vmem_limit_bytes=mib << 20),
        name=name,
    )


def tile(ref, k, rows):
    return ref[pl.ds(pl.multiple_of(k * rows, rows), rows), :]


def selection(cy):
    row, col = iotas((3 * RIM, OWN))
    k, y = iotas((OWN, CY))
    spread = dot(pick((k & 31) == y), cy).astype(bf16)
    row4, n = iotas((3 * RIM, MODES))
    modes = dot_t(pick((row4 & 3) == n), spread)
    plane = ((row >> 2) & 3) == (col >> 5)
    inner = col & 31
    target = jnp.where(row < RIM, row & 3, CY - OV + (row & 3))
    ones = jnp.where(inner == target, 1.0, 0.0)
    value = jnp.where(row < 2 * RIM, ones, modes)
    return jnp.where(plane, value, 0.0).astype(bf16)


def load_kernel(residual, cy, own, first_x, last_x, rim_lo, rim_hi, along_y, sel, buf, sems):
    rows = CELLS // CHUNKS

    def copy(c):
        at = pl.ds(c * rows, rows)
        return pltpu.make_async_copy(residual.at[at, :], buf.at[at, :], sems.at[c])

    for c in range(CHUNKS):
        copy(c).start()
    take = selection(cy[...])
    sel[...] = take
    for c in range(CHUNKS):
        copy(c).wait()
        for b in range(rows // OWN):
            k = c * (rows // OWN) + b
            data = buf[k * OWN : (k + 1) * OWN, :].astype(bf16)
            own[k * OWN : (k + 1) * OWN, :] = data
            if k == 0:
                first_x[...] = data
            if k == BLOCKS - 1:
                last_x[...] = data
            out = dot(take, data)
            at = slice(k * RIM, (k + 1) * RIM)
            rim_lo[at, :] = out[:RIM].astype(bf16)
            rim_hi[at, :] = out[RIM : 2 * RIM].astype(bf16)
            along_y[at, :] = out[2 * RIM :]


def load(residual, coarse_y):
    rim = sds((CX * OV, NZ), bf16)
    return call(
        load_kernel,
        "load",
        (
            sds((CELLS, NZ), bf16), sds((OWN, NZ), bf16), sds((OWN, NZ), bf16), rim, rim,
            sds((CX * MODES, NZ), f32), sds((3 * RIM, OWN), bf16),
        ),
        [ANY, VM],
        16,
        scratch=[pltpu.VMEM((CELLS, NZ), f32), pltpu.SemaphoreType.DMA((CHUNKS,))],
    )(residual, coarse_y)


def corners_kernel(sel, rim_lo, rim_hi, xlo, xhi, down, up):
    down[: CX * OV, :] = rim_lo[...]
    up[: CX * OV, :] = rim_hi[...]
    for i, strip in enumerate((xlo, xhi)):
        out = dot(sel[: 2 * RIM, :], strip[...]).astype(bf16)
        at = slice(CX * OV + i * RIM, CX * OV + (i + 1) * RIM)
        down[at, :] = out[:RIM]
        up[at, :] = out[RIM:]


def corners(sel, rim_lo, rim_hi, xlo, xhi):
    side = sds((EX * OV, NZ), bf16)
    return call(corners_kernel, "corners", (side, side), [VM] * 5, 8)(sel, rim_lo, rim_hi, xlo, xhi)


def prepare_kernel(
    lx, ly, lz, eig_x, cx, cy, mode_x, mode_y, mode_z, ceig_x, ceig_z,
    wy, wyt, wx, wxt, lzt, ex, bx, bxt, spread, modes_xz, mode_yt, ceig_xz,
):
    def cell(k):
        y = jnp.where(k < OWN, OV + (k & 31), jnp.where(k < OWN + RIM, k & 3, EY - OV + (k & 3)))
        plane = jnp.where(k < OWN, k >> 5, ((k - OWN) >> 2) & 3)
        return y, plane

    def mode(j):
        plane = (j >= EY).astype(jnp.int32) + (j >= 2 * EY) + (j >= 3 * EY)
        return j - EY * plane, plane

    k, y = iotas((ROWS, EY))
    by_cell = dot(pick(cell(k)[0] == y), ly[...]).astype(bf16)
    b, j = iotas((EY, ROWS))
    k, col = iotas((ROWS, ROWS))
    value = dot(by_cell, pick(mode(j)[0] == b))
    wyt[...] = jnp.where(cell(k)[1] == mode(col)[1], value, 0.0).astype(bf16)
    j, b = iotas((ROWS, EY))
    value = dot_t(pick(mode(j)[0] == b), by_cell)
    wy[...] = jnp.where(mode(k)[1] == cell(col)[1], value, 0.0).astype(bf16)

    k, x = iotas((EX, EX))
    source = jnp.where(k < CX, k + OV, jnp.where(k < CX + OV, k - CX, k))
    moved = dot(pick(source == x), lx[...]).astype(bf16)
    wxt[...] = moved
    wx[...] = dot_t(pick(k == x), moved).astype(bf16)
    ex[...] = jnp.sum(jnp.where(k == x, eig_x[...], 0.0), axis=1, keepdims=True)
    c, z = iotas((NZ, NZ))
    lzt[...] = dot_t(pick(c == z), lz[...]).astype(bf16)

    row, x = iotas((CX * MODES, CX))
    by_row = dot(pick((row >> 2) == x), cx[...]).astype(bf16)
    m, col = iotas((MODES, 16))
    row, col16 = iotas((CX * MODES, 16))
    value = dot(by_row, pick((col >> 2) == m))
    half = jnp.where((row & 3) == (col16 & 3), value, 0.0).astype(bf16)
    bxt[...] = jnp.concatenate([half, half], 1)
    col, m = iotas((16, MODES))
    value = dot_t(pick((col >> 2) == m), by_row)
    col, row = iotas((16, CX * MODES))
    bx[...] = jnp.where((row & 3) == (col & 3), value, 0.0).astype(bf16)

    k, y = iotas((OWN, CY))
    by_k = dot(pick((k & 31) == y), cy[...]).astype(bf16)
    n, col = iotas((MODES, 4 * RIM))
    value = dot(by_k, pick((col & 3) == n))
    k, col = iotas((OWN, 4 * RIM))
    inner = k & 31
    plane = (k >> 5) == ((col >> 2) & 3)
    target = jnp.where(col < 3 * RIM, col & 3, CY - OV + (col & 3))
    ones = jnp.where(inner == target, 1.0, 0.0)
    value = jnp.where(col < 2 * RIM, value, ones)
    spread[...] = jnp.where(plane, value, 0.0).astype(bf16)

    r, i = iotas((128, 32))
    a, col = iotas((32, 128))
    to_a = pick((col >> 2) == a, f32)
    part_x = dot_hi(dot_hi(pick((r >> 2) == i, f32), mode_x[...]), to_a)
    r, p = iotas((128, MODES))
    c, col = iotas((MODES, 128))
    to_c = pick((col & 3) == c, f32)
    part_z = dot_hi(dot_hi(pick((r & 3) == p, f32), mode_z[...]), to_c)
    modes_xz[...] = part_x * part_z
    mode_yt[...] = mode_y[...].T
    eight_x = jnp.broadcast_to(ceig_x[...], (8, 32))
    eight_z = jnp.broadcast_to(ceig_z[...], (8, MODES))
    ceig_xz[...] = dot_hi(eight_x, to_a) + dot_hi(eight_z, to_c)


def prepare(lx, ly, lz, eig_x, cx, cy, mode_x, mode_y, mode_z, ceig_x, ceig_z):
    return call(
        prepare_kernel,
        "prepare",
        (
            sds((ROWS, ROWS), bf16), sds((ROWS, ROWS), bf16), sds((EX, EX), bf16),
            sds((EX, EX), bf16), sds((NZ, NZ), bf16), sds((EX, 1), f32),
            sds((16, CX * MODES), bf16), sds((CX * MODES, 32), bf16), sds((OWN, 64), bf16),
            sds((128, 128), f32), sds((128, 128), f32), sds((8, 128), f32),
        ),
        [VM] * 11,
        8,
    )(
        lx, ly, lz, eig_x[None, :], cx, cy, mode_x, mode_y, mode_z,
        ceig_x[None, :], ceig_z[None, :],
    )


def solve_kernel(
    own, xlo, xhi, ylo, yhi, wy, wyt, wx, wxt, lz, lzt, ex, ey, ez,
    fix, out_xlo, out_xhi, out_ylo, out_yhi, field, mid,
):
    def put(rows, value):
        field[0, rows, :] = value[:, :128]
        field[1, rows, :] = value[:, 128:]

    def take(rows):
        return jnp.concatenate([field[0, rows, :], field[1, rows, :]], 1)

    def forward_y(main, k):
        data = jnp.concatenate([main, tile(ylo, k, RIM), tile(yhi, k, RIM)], 0)
        put(pl.ds(pl.multiple_of(k * ROWS, ROWS), ROWS), dot(wy[...], data))

    def first(k, carry):
        forward_y(tile(own, k, OWN), k)
        return carry

    lax.fori_loop(0, BLOCKS, first, 0, unroll=4)
    forward_y(xlo[...], BLOCKS)
    forward_y(xhi[...], BLOCKS + 1)

    def mid_rows(b):
        return pl.ds(pl.multiple_of(b * EX, 8), EX)

    def forward_x(b, carry):
        plane = take(pl.ds(b, EX, stride=EY)).astype(bf16)
        mid[mid_rows(b), :] = dot(wx[...], plane)
        return carry

    lax.fori_loop(0, EY, forward_x, 0, unroll=8)

    def both_z(i, carry):
        at = pl.ds(pl.multiple_of(i * 4 * EX, 8), 4 * EX)
        along = dot(mid[at, :].astype(bf16), lz[...])
        parts = []
        for q in range(4):
            scale = ex[...] + (ez[...] + ey[i * 4 + q])
            parts.append((along[q * EX : (q + 1) * EX] / scale))
        spectral = jnp.concatenate(parts, 0).astype(bf16)
        mid[at, :] = dot(spectral, lzt[...])
        return carry

    lax.fori_loop(0, EY // 4, both_z, 0)

    def backward_x(b, carry):
        put(pl.ds(b, EX, stride=EY), dot(wxt[...], mid[mid_rows(b), :].astype(bf16)))
        return carry

    lax.fori_loop(0, EY, backward_x, 0, unroll=8)

    def backward_y(k):
        rows = take(pl.ds(pl.multiple_of(k * ROWS, ROWS), ROWS)).astype(bf16)
        return dot(wyt[...], rows)

    def last(k, carry):
        out = backward_y(k)
        fix[pl.ds(pl.multiple_of(k * OWN, OWN), OWN), :] = out[:OWN]
        at = pl.ds(pl.multiple_of(k * RIM, RIM), RIM)
        out_ylo[at, :] = out[OWN : OWN + RIM].astype(bf16)
        out_yhi[at, :] = out[OWN + RIM :].astype(bf16)
        return carry

    lax.fori_loop(0, BLOCKS, last, 0, unroll=4)
    out_xlo[...] = backward_y(BLOCKS).astype(bf16)
    out_xhi[...] = backward_y(BLOCKS + 1).astype(bf16)


def solve(own, xlo, xhi, ylo, yhi, weights, lz, ey, ez):
    strip = sds((ROWS, NZ), bf16)
    rim = sds((CX * OV, NZ), bf16)
    wy, wyt, wx, wxt, lzt, ex = weights
    return call(
        solve_kernel,
        "solve",
        (sds((CELLS, NZ), f32), strip, strip, rim, rim),
        [VM] * 12 + [SM, VM],
        32,
        scratch=[pltpu.VMEM((2, EX * EY, NZ // 2), f32), pltpu.VMEM((EX * EY, NZ), f32)],
    )(own, xlo, xhi, ylo, yhi, wy, wyt, wx, wxt, lz, lzt, ex, ey, ez[None, :])


def fold_kernel(out_ylo, out_yhi, rxlo, rxhi, down, up):
    end = CX * OV
    for strip, start, out in ((out_ylo, OWN, down), (out_yhi, OWN + RIM, up)):
        rows = slice(start, start + RIM)
        out[...] = strip[...]
        low = strip[:RIM, :].astype(f32) + rxlo[rows, :].astype(f32)
        high = strip[end - RIM :, :].astype(f32) + rxhi[rows, :].astype(f32)
        out[:RIM, :] = low.astype(bf16)
        out[end - RIM :, :] = high.astype(bf16)


def fold(out_ylo, out_yhi, rxlo, rxhi):
    rim = sds((CX * OV, NZ), bf16)
    return call(fold_kernel, "fold", (rim, rim), [VM] * 4, 8)(out_ylo, out_yhi, rxlo, rxhi)


def restrict_kernel(along_y, bx, cz, out):
    high, low = split(along_y[...])
    both = dot(bx[...], high) + dot(bx[...], low)
    own = dot_hi(both, cz[...].astype(f32))
    for i in range(out.shape[0]):
        for m in range(MODES):
            out[i, :, m * MODES : (m + 1) * MODES] = own[m * MODES : (m + 1) * MODES, :]


def coarse_x_kernel(rows, modes_xz, out):
    part = sum(dot_hi(rows[i], modes_xz[16 * i : 16 * i + 16, :]) for i in range(8))
    for i in range(out.shape[0]):
        out[i] = part


def coarse_y_kernel(rows, out):
    for i in range(out.shape[0]):
        for j in range(rows.shape[0]):
            out[i, MODES * j : MODES * (j + 1), :] = rows[j]


def coarse_kernel(place, rows, modes_xz, mode_y, mode_yt, ceig_xz, ceig_y, cz, bxt, out):
    hat = dot_hi(mode_yt[...], rows[...].reshape(128, 128))
    hat = hat / (ceig_y[...] + ceig_xz[:1, :])
    row, col = iotas((8, 128))
    mine = pick(col == place[1] * MODES + row, f32)
    rows_y = dot_hi(mine, mode_y[...])
    rows_xz = modes_xz[pl.ds(pl.multiple_of(place[0] * 16, 16), 16), :]
    sol = dot_t_hi(dot_hi(rows_y, hat), rows_xz)
    levels = cz[...].astype(f32)
    shape = jnp.concatenate(
        [dot_t_hi(sol[:, m * MODES : (m + 1) * MODES], levels)[:MODES] for m in range(MODES)], 0
    )
    high, low = split(shape)
    value = dot(bxt[...], jnp.concatenate([high, low], 0))
    high, low = split(value)
    for k in range(BLOCKS):
        at = slice(k * RIM, (k + 1) * RIM)
        out[2 * k * RIM : (2 * k + 1) * RIM, :] = high[at]
        out[(2 * k + 1) * RIM : (2 * k + 2) * RIM, :] = low[at]


def combine_kernel(fix, spread, shape, rxlo, rxhi, rylo, ryhi, out, buf, sems):
    rows = CELLS // CHUNKS

    def copy(c):
        at = pl.ds(c * rows, rows)
        return pltpu.make_async_copy(buf.at[at, :], out.at[at, :], sems.at[c])

    for c in range(CHUNKS):
        for b in range(rows // OWN):
            k = c * (rows // OWN) + b
            rim = slice(k * RIM, (k + 1) * RIM)
            data = jnp.concatenate(
                [shape[2 * k * RIM : 2 * (k + 1) * RIM, :], rylo[rim, :], ryhi[rim, :]], 0
            )
            total = fix[k * OWN : (k + 1) * OWN, :] + dot(spread[...], data)
            if k == 0:
                total = total + rxlo[:OWN, :].astype(f32)
            if k == BLOCKS - 1:
                total = total + rxhi[:OWN, :].astype(f32)
            buf[k * OWN : (k + 1) * OWN, :] = total
        copy(c).start()
    for c in range(CHUNKS):
        copy(c).wait()


def combine(*args):
    return call(
        combine_kernel,
        "combine",
        sds((CELLS, NZ), f32),
        [VM] * 7,
        16,
        out_specs=ANY,
        scratch=[pltpu.VMEM((CELLS, NZ), f32), pltpu.SemaphoreType.DMA((CHUNKS,))],
    )(*args)


GY = ("gz", "gw")


def shift(x, axis, step):
    size = lax.axis_size(axis)
    return lax.ppermute(x, axis, [(i, (i + step) % size) for i in range(size)])


def exchange(x, axis):
    return lax.all_to_all(x, axis, 0, 0)


def local(
    residual, local_x, local_y, local_z, eig_x, eig_y, eig_z, coarse_x, coarse_y, coarse_z,
    mode_x, mode_y, mode_z, coarse_eig_x, coarse_eig_y, coarse_eig_z,
):
    own, first_x, last_x, rim_lo, rim_hi, along_y, sel = load(
        residual.reshape(CELLS, NZ), coarse_y
    )
    xlo = shift(last_x, "gx", 1)
    xhi = shift(first_x, "gx", -1)
    wy, wyt, wx, wxt, lzt, ex, bx, bxt, spread, modes_xz, mode_yt, ceig_xz = prepare(
        local_x, local_y, local_z, eig_x, coarse_x, coarse_y, mode_x, mode_y, mode_z,
        coarse_eig_x, coarse_eig_z,
    )
    own_coarse = call(
        restrict_kernel, "restrict", sds((8, MODES, 16), f32), [VM] * 3, 8
    )(along_y, bx, coarse_z)
    down, up = corners(sel, rim_lo, rim_hi, xlo, xhi)
    ylo = shift(up, GY, 1)
    yhi = shift(down, GY, -1)

    rows = exchange(own_coarse, "gx")
    rows = call(coarse_x_kernel, "coarse_x", sds((4, MODES, 128), f32), [VM] * 2, 4)(
        rows, modes_xz
    )

    fix, out_xlo, out_xhi, out_ylo, out_yhi = solve(
        own, xlo, xhi, ylo, yhi, (wy, wyt, wx, wxt, lzt, ex), local_z, eig_y, eig_z
    )

    rxlo = shift(out_xhi, "gx", 1)
    rxhi = shift(out_xlo, "gx", -1)
    down, up = fold(out_ylo, out_yhi, rxlo, rxhi)
    rylo = shift(up, GY, 1)
    ryhi = shift(down, GY, -1)

    rows = exchange(rows, "gw")
    rows = call(coarse_y_kernel, "coarse_y", sds((8, 16, 128), f32), [VM], 4)(rows)
    rows = exchange(rows, "gz")
    place = jnp.stack([lax.axis_index("gx"), lax.axis_index(GY)]).astype(jnp.int32)
    shape = call(
        coarse_kernel, "coarse", sds((2 * CX * MODES, NZ), bf16), [SM] + [VM] * 8, 8
    )(place, rows, modes_xz, mode_y, mode_yt, ceig_xz, coarse_eig_y[:, None], coarse_z, bxt)

    out = combine(fix, spread, shape, rxlo, rxhi, rylo, ryhi)
    return out.reshape(CX, CY, NZ)


def solution(mesh):
    fine = Mesh(mesh.devices.reshape(8, 8, 4), ("gx", "gz", "gw"))
    split_y = P("gx", ("gz", "gw"), None)
    return jax.shard_map(
        local, mesh=fine, in_specs=(split_y,) + (P(),) * 15, out_specs=split_y, check_vma=False
    )
```

time: 124 us -> 97.3 us (0.78); the launches traced: 124 us -> 95.7 us
  blocking collectives: 54 us -> 16.2 us
  Pallas kernels: 0 us -> 22.3 us
  matrix products: 19.1 us -> 0 us
  local copies, waits for them, and re-layouts: 10.4 us -> 21.7 us
  starting transfers between devices: 27.3 us -> 21.9 us
  waiting for transfers between devices: 11.5 us -> 13.4 us
    all_gather x2 -> x0, blocking collectives: 54 us -> none  [the longest x1 38.5 us: local(): coarse_res = lax.all_gather(partial_rows, 'gy', axis=1, tiled=True)]
    pallas_call x0 -> x10, Pallas kernels: none -> 22.3 us  [the longest x1 12.6 us: solve(): call(solve_kernel, 'solve', (sds((CELLS, NZ), f32), strip, strip, rim, ri...]
    dot_general x16 -> x0, matrix products: 19.1 us -> none  [the longest x1 5.94 us: solve_local(): jnp.einsum('zc,abz->abc', local_z, first_y, preferred_element_type=jnp.fl...]
    unnamed x31 -> x53, local copies, waits for them, and re-layouts: 4.63 us -> 20.9 us
    all_to_all x0 -> x2, blocking collectives: none -> 16.2 us  [exchange(): return lax.all_to_all(x, axis, 0, 0)]
    ppermute x8, starting transfers between devices: 27.3 us -> 16.6 us  [shift(): return lax.ppermute(x, axis, [(i, (i + step) % size) for i in range(size)])]
    all_to_all x0 -> x1, waiting for transfers between devices: none -> 6.39 us  [exchange(): return lax.all_to_all(x, axis, 0, 0)]
    all_to_all x0 -> x1, starting transfers between devices: none -> 5.23 us  [exchange(): return lax.all_to_all(x, axis, 0, 0)]
  transfers between devices with their start and end apart: 8 -> 9, of which waited for: 4 -> 5; matrix products, arithmetic and copies ran while one was open for 4% -> 3% of each run, Pallas kernels for 0% -> 5%
where the time goes in v2:
time: 97.3 us; the launch traced here: 95.7 us
  Pallas kernels  22.3 us (23%)
  starting transfers between devices  21.9 us (23%)
  local copies, waits for them, and re-layouts  21.7 us (22%)
  blocking collectives  16.2 us (17%)
  waiting for transfers between devices  13.4 us (14%)
    unnamed x53, local copies, waits for them, and re-layouts  20.9 us
    ppermute x8, starting transfers between devices, shift(): return lax.ppermute(x, axis, [(i, (i + step) % size) for i in range(size)])  16.6 us
    all_to_all x2, blocking collectives, exchange(): return lax.all_to_all(x, axis, 0, 0)  16.2 us
    pallas_call x1, Pallas kernels, solve(): call(solve_kernel, 'solve', (sds((CELLS, NZ), f32), strip, strip, rim, ri...  12.6 us
    ppermute x8, waiting for transfers between devices, shift(): return lax.ppermute(x, axis, [(i, (i + step) % size) for i in range(size)])  7 us
    all_to_all x1, waiting for transfers between devices, exchange(): return lax.all_to_all(x, axis, 0, 0)  6.39 us
    all_to_all x1, starting transfers between devices, exchange(): return lax.all_to_all(x, axis, 0, 0)  5.23 us
    pallas_call x1, Pallas kernels, combine(): call(combine_kernel, 'combine', sds((CELLS, NZ), f32), [VM] * 7, 16, out_...  2.28 us
  transfers between devices with their start and end apart: 9, of which 5 were waited for; matrix products, arithmetic and copies ran while one was open for 3% of the time, Pallas kernels for 5%

profile of v2, /device:TPU:1, one launch (start us, length us, event | category | flops | bytes accessed | tf_op | source)
XLA Modules:
  0.0 95.7 jit_solution(13512735181805982854)
XLA Ops:
  0.0 0.8 copy.17.cy
  0.8 2.2 %copy-done.2 = f32[128,32,256]{2,1,0:T(8,128)S(1)} copy-done((f32[128,32,256]{2,1,0:T(8,128)S(1)}, f32[128,32,256]{2,1,0:T(8,128)}, u32[]{:S(2)}) %copy-start.2) | copy-done | bytes 4194328
  3.0 2.0 %load.1 = (bf16[4096,256]{1,0:T(8,128)(2,1)S(1)}, bf16[128,256]{1,0:T(8,128)(2,1)S(1)}, bf16[128,256]{1,0:T(8,128)(2,1)S(1)}, bf16[512,256]{1,0:T(8,128)(2,1)S(1...) custom-call(f32[4096,256]{1,0:T(8,128)S(1)} %bitcast.9, ...), custom_call_target="tpu_custom_call" | custom-call | tf_op jit(solution)/shard_map/load/pallas_call | solution.py:124
  5.0 2.6 %collective-permute-start = (bf16[128,256]{1,0:T(8,128)(2,1)S(1)}, bf16[128,256]{1,0:T(8,128)(2,1)S(1)}, u32[]{:S(2)}, u32[]{:S(2)}) collective-permute-start(bf16[128,256]{1,0:T(8,128)(2,1)S(1)} %get-tuple-element.34), channel_id=1, source_target_pairs={{0,32},{32,64},{64,96},{96,128},{128,160},{160,192},{192,224},{224... | collective-permute-start | bytes 196616 | tf_op jit(solution)/shard_map/ppermute | solution.py:424
  7.6 0.6 collective-permute-start.1
  8.3 0.7 collective-permute-done.xlo
  9.0 2.3 %collective-permute-done.1.xhi = bf16[128,256]{1,0:T(8,128)(2,1)S(1)} collective-permute-done((bf16[128,256]{1,0:T(8,128)(2,1)S(1)}, bf16[128,256]{1,0:T(8,128)(2,1)S(1)}, u32[]{:S(2)}, u32[]{:S(2)}) %collective-permute-start.1) | collective-permute-done | bytes 65568 | tf_op jit(solution)/shard_map/ppermute | solution.py:424
  11.3 0.9 corners.1
  12.3 1.3 %collective-permute-start.2 = (bf16[544,256]{1,0:T(8,128)(2,1)}, bf16[544,256]{1,0:T(8,128)(2,1)S(1)}, u32[]{:S(2)}, u32[]{:S(2)}) collective-permute-start(bf16[544,256]{1,0:T(8,128)(2,1)} %get-tuple-element.39), channel_id=1, source_target_pairs={{0,1},{1,2},{2,3},{3,4},{4,5},{5,6},{6,7},{7,8},{8,9},{9,10},{10,1... | collective-permute-start | bytes 835592 | tf_op jit(solution)/shard_map/ppermute | solution.py:424
  13.6 6.7 %collective-permute-start.3 = (bf16[544,256]{1,0:T(8,128)(2,1)}, bf16[544,256]{1,0:T(8,128)(2,1)S(1)}, u32[]{:S(2)}, u32[]{:S(2)}) collective-permute-start(bf16[544,256]{1,0:T(8,128)(2,1)} %get-tuple-element.40), channel_id=1, source_target_pairs={{0,31},{1,0},{2,1},{3,2},{4,3},{5,4},{6,5},{7,6},{8,7},{9,8},{10,9... | collective-permute-start | bytes 835592 | tf_op jit(solution)/shard_map/ppermute | solution.py:424
  20.3 0.8 copy.18.cx
  21.1 0.8 copy-done.4
  22.0 0.9 copy-done.8
  22.9 0.7 copy-done.15
  23.6 0.7 copy-done.16
  24.3 0.7 copy-done.22
  24.9 0.7 copy-done.23
  25.6 1.2 %prepare.1 = (bf16[160,160]{1,0:T(8,128)(2,1)S(1)}, bf16[160,160]{1,0:T(8,128)(2,1)S(1)}, bf16[136,136]{1,0:T(8,128)(2,1)S(1)}, bf16[136,136]{1,0:T(8,128)(2,1)S...) custom-call(bf16[136,136]{1,0:T(8,128)(2,1)S(1)} %copy-done.8, ...), custom_call_target="tpu_custom_call" | custom-call | tf_op jit(solution)/shard_map/prepare/pallas_call | solution.py:224
  26.8 0.6 copy-done.6
  27.4 0.6 copy-done.9
  28.0 0.6 copy-done.11
  28.7 0.6 copy-done.13
  29.3 0.6 copy-done.17
  29.8 0.7 copy-done.21
  30.5 0.7 copy-done.24
  31.2 12.6 %solve.1 = (f32[4096,256]{1,0:T(8,128)S(1)}, bf16[160,256]{1,0:T(8,128)(2,1)S(1)}, bf16[160,256]{1,0:T(8,128)(2,1)S(1)}, bf16[512,256]{1,0:T(8,128)(2,1)S(1)}, bf16[512,256]{1,0:T(8,128)(2,1)S(1)}) custom-call(bf16[4096,256]{1,0:T(8,128)(2,1)S(1)} %get-tuple-element.33.own, bf16[128,256]{1,0:T(8,128)(2,1)S(1)} %collective-permute-done.xlo, ...), custom_call_target="tpu_custom_call" | custom-call | tf_op jit(solution)/shard_map/solve/pallas_call | solution.py:314
  43.7 2.0 %copy-done = f32[4096,256]{1,0:T(8,128)} copy-done((f32[4096,256]{1,0:T(8,128)}, f32[4096,256]{1,0:T(8,128)S(1)}, u32[]{:S(2)}) %copy-start) | copy-done | bytes 4194328
  45.8 0.3 collective-permute-start.4
  46.0 0.2 collective-permute-start.5
  46.3 1.3 %collective-permute-done.4.rxlo = bf16[160,256]{1,0:T(8,128)(2,1)S(1)} collective-permute-done((bf16[160,256]{1,0:T(8,128)(2,1)S(1)}, bf16[160,256]{1,0:T(8,128)(2,1)S(1)}, u32[]{:S(2)}, u32[]{:S(2)}) %collective-permute-start.4) | collective-permute-done | bytes 81952 | tf_op jit(solution)/shard_map/ppermute | solution.py:424
  47.5 2.7 %collective-permute-done.5.rxhi = bf16[160,256]{1,0:T(8,128)(2,1)S(1)} collective-permute-done((bf16[160,256]{1,0:T(8,128)(2,1)S(1)}, bf16[160,256]{1,0:T(8,128)(2,1)S(1)}, u32[]{:S(2)}, u32[]{:S(2)}) %collective-permute-start.5) | collective-permute-done | bytes 81952 | tf_op jit(solution)/shard_map/ppermute | solution.py:424
  50.3 4.8 %collective-permute-start.7 = (bf16[512,256]{1,0:T(8,128)(2,1)S(1)}, bf16[512,256]{1,0:T(8,128)(2,1)S(1)}, u32[]{:S(2)}, u32[]{:S(2)}) collective-permute-start(bf16[512,256]{1,0:T(8,128)(2,1)S(1)} %get-tuple-element.60), channel_id=1, source_target_pairs={{0,31},{1,0},{2,1},{3,2},{4,3},{5,4},{6,5},{7,6},{8,7},{9,8},{10,9... | collective-permute-start | bytes 786440 | tf_op jit(solution)/shard_map/ppermute | solution.py:424
  55.1 0.8 copy.20.cz
  55.9 0.5 restrict.1
  56.4 9.7 %all_to_all.15.rows = f32[8,4,16]{2,1,0:T(4,128)S(1)} all-to-all(f32[8,4,16]{2,1,0:T(4,128)S(1)} %restrict.1), channel_id=1, replica_groups=mesh['gx'=8,'gz'=8,'gw'=4] {'gx'}, dimensions={0} | all-to-all | bytes 4096 | tf_op jit(solution)/shard_map/all_to_all | solution.py:428
  66.2 0.2 coarse_x.1
  66.4 6.5 %all_to_all.16.rows = f32[4,4,128]{2,1,0:T(4,128)S(1)} all-to-all(f32[4,4,128]{2,1,0:T(4,128)S(1)} %coarse_x.1), channel_id=1, replica_groups=mesh['gx'=8,'gz'=8,'gw'=4] {'gw'}, dimensions={0} | all-to-all | bytes 16384 | tf_op jit(solution)/shard_map/all_to_all | solution.py:428
  72.9 0.6 coarse_y.1
  73.5 5.2 %all-to-all-start.2 = ((f32[8,16,128]{2,1,0:T(8,128)}), f32[8,16,128]{2,1,0:T(8,128)S(1)}, u32[]{:S(2)}, u32[]{:S(2)}) async-start(f32[8,16,128]{2,1,0:T(8,128)} %coarse_y.1), calls=%async_computation.2 | async-start | bytes 131072 | tf_op jit(solution)/shard_map/all_to_all | solution.py:428
  78.8 0.8 copy.21.ceig_y
  79.6 6.4 %all-to-all-done.2.rows = f32[8,16,128]{2,1,0:T(8,128)S(1)} async-done(((f32[8,16,128]{2,1,0:T(8,128)}), f32[8,16,128]{2,1,0:T(8,128)S(1)}, u32[]{:S(2)}, u32[]{:S(2)}) %all-to-all-start.2) | async-done | bytes 65568 | tf_op jit(solution)/shard_map/all_to_all | solution.py:428
  86.0 0.8 copy-done.5
  86.8 0.9 copy-done.7
  87.7 0.8 copy-done.10
  88.6 0.7 copy-done.18
  89.2 1.9 %coarse.1.shape = bf16[1024,256]{1,0:T(8,128)(2,1)S(1)} custom-call(s32[2]{0:T(128)S(1)} %pad_add_fusion.place, f32[8,16,128]{2,1,0:T(8,128)S(1)} %all-to-all-done.2.rows, f32[128,128]{1,0:T(8,128)S(1)} %get-tuple-element.51.modes_xz, f32[128,128]{1,0:T(8,128)S(1)} %copy-done.5, f32[128,128]{1,0:T(8,128)S(1)} %copy-done.10, f32[8,128]{1,0:T(8,128)S(1)} %copy-done.18, ...), custom_call_target="tpu_custom_call" | custom-call | tf_op jit(solution)/shard_map/coarse/pallas_call | solution.py:470
  91.2 2.2 %copy-done.1 = f32[4096,256]{1,0:T(8,128)S(1)} copy-done((f32[4096,256]{1,0:T(8,128)S(1)}, f32[4096,256]{1,0:T(8,128)}, u32[]{:S(2)}) %copy-start.1) | copy-done | bytes 4194328
  93.4 2.3 %combine.1 = f32[4096,256]{1,0:T(8,128)} custom-call(f32[4096,256]{1,0:T(8,128)S(1)} %copy-done.1, bf16[128,64]{1,0:T(8,128)(2,1)S(1)} %copy-done.12, bf16[1024,256]{1,0:T(8,128)(2,1)S(1)} %coarse.1.shape, bf16[160,256]{1,0:T(8,128)(2,1)S(1)} %collective-permute-done.4.rxlo, bf16[160,256]{1,0:T(8,128)(2,1)S(1)} %collective-permute-done.5.rxhi, ...), custom_call_target="tpu_custom_call" | custom-call | tf_op jit(solution)/shard_map/combine/pallas_call | solution.py:408
  (37 shorter events, 0.3 us)
Async XLA Ops:
  0.0 21.1 %copy-start.19 = (f32[4,4]{1,0:T(4,128)S(1)}, f32[4,4]{1,0:T(4,128)}, u32[]{:S(2)}) copy-start(f32[4,4]{1,0:T(4,128)} %mode_z.1) | copy-start | bytes 196
  0.0 21.1 %copy-start.20 = (f32[136]{0:T(256)S(1)}, f32[136]{0:T(256)}, u32[]{:S(2)}) copy-start(f32[136]{0:T(256)} %param.20) | copy-start | bytes 1636
  0.8 2.2 %copy-start.2 = (f32[128,32,256]{2,1,0:T(8,128)S(1)}, f32[128,32,256]{2,1,0:T(8,128)}, u32[]{:S(2)}) copy-start(f32[128,32,256]{2,1,0:T(8,128)} %param.16) | copy-start | bytes 12582916
  3.0 18.1 %copy-start.3 = (bf16[256,256]{1,0:T(8,128)(2,1)S(1)}, bf16[256,256]{1,0:T(8,128)(2,1)}, u32[]{:S(2)}) copy-start(bf16[256,256]{1,0:T(8,128)(2,1)} %lz.3) | copy-start | bytes 393220
  5.0 4.0 %collective-permute-start = (bf16[128,256]{1,0:T(8,128)(2,1)S(1)}, bf16[128,256]{1,0:T(8,128)(2,1)S(1)}, u32[]{:S(2)}, u32[]{:S(2)}) collective-permute-start(bf16[128,256]{1,0:T(8,128)(2,1)S(1)} %get-tuple-element.34), channel_id=1, source_target_pairs={{0,32},{32,64},{64,96},{96,128},{128,160},{160,192},{192,224},{224... | collective-permute-start | bytes 196616 | tf_op jit(solution)/shard_map/ppermute | solution.py:424
  7.6 3.7 %collective-permute-start.1 = (bf16[128,256]{1,0:T(8,128)(2,1)S(1)}, bf16[128,256]{1,0:T(8,128)(2,1)S(1)}, u32[]{:S(2)}, u32[]{:S(2)}) collective-permute-start(bf16[128,256]{1,0:T(8,128)(2,1)S(1)} %get-tuple-element.35), channel_id=1, source_target_pairs={{0,224},{32,0},{64,32},{96,64},{128,96},{160,128},{192,160},{224,1... | collective-permute-start | bytes 196616 | tf_op jit(solution)/shard_map/ppermute | solution.py:424
  12.3 17.0 %collective-permute-start.2 = (bf16[544,256]{1,0:T(8,128)(2,1)}, bf16[544,256]{1,0:T(8,128)(2,1)S(1)}, u32[]{:S(2)}, u32[]{:S(2)}) collective-permute-start(bf16[544,256]{1,0:T(8,128)(2,1)} %get-tuple-element.39), channel_id=1, source_target_pairs={{0,1},{1,2},{2,3},{3,4},{4,5},{5,6},{6,7},{7,8},{8,9},{9,10},{10,1... | collective-permute-start | bytes 835592 | tf_op jit(solution)/shard_map/ppermute | solution.py:424
  13.6 15.7 %collective-permute-start.3 = (bf16[544,256]{1,0:T(8,128)(2,1)}, bf16[544,256]{1,0:T(8,128)(2,1)S(1)}, u32[]{:S(2)}, u32[]{:S(2)}) collective-permute-start(bf16[544,256]{1,0:T(8,128)(2,1)} %get-tuple-element.40), channel_id=1, source_target_pairs={{0,31},{1,0},{2,1},{3,2},{4,3},{5,4},{6,5},{7,6},{8,7},{9,8},{10,9... | collective-permute-start | bytes 835592 | tf_op jit(solution)/shard_map/ppermute | solution.py:424
  21.1 0.8 copy-start.4
  22.0 0.9 copy-start.8
  22.9 0.7 copy-start.15
  23.6 0.7 copy-start.16
  24.3 0.7 copy-start.22
  24.9 0.7 copy-start.23
  26.8 0.7 copy-start.6
  27.4 0.6 copy-start.9
  28.0 0.6 copy-start.11
  28.7 0.6 copy-start.13
  29.3 0.6 copy-start.17
  29.3 26.7 %copy-start.14 = (bf16[16,512]{1,0:T(8,128)(2,1)S(1)}, bf16[16,512]{1,0:T(8,128)(2,1)}, u32[]{:S(2)}) copy-start(bf16[16,512]{1,0:T(8,128)(2,1)} %copy-done.13) | copy-start | bytes 49156
  29.3 61.9 %copy-start.12 = (bf16[128,64]{1,0:T(8,128)(2,1)S(1)}, bf16[128,64]{1,0:T(8,128)(2,1)}, u32[]{:S(2)}) copy-start(bf16[128,64]{1,0:T(8,128)(2,1)} %copy-done.11) | copy-start | bytes 49156
  29.8 0.7 copy-start.21
  30.5 0.7 copy-start.24
  43.7 2.0 %copy-start = (f32[4096,256]{1,0:T(8,128)}, f32[4096,256]{1,0:T(8,128)S(1)}, u32[]{:S(2)}) copy-start(f32[4096,256]{1,0:T(8,128)S(1)} %get-tuple-element.47.fix) | copy-start | bytes 12582916
  45.8 1.8 %collective-permute-start.4 = (bf16[160,256]{1,0:T(8,128)(2,1)S(1)}, bf16[160,256]{1,0:T(8,128)(2,1)S(1)}, u32[]{:S(2)}, u32[]{:S(2)}) collective-permute-start(bf16[160,256]{1,0:T(8,128)(2,1)S(1)} %get-tuple-element.55), channel_id=1, source_target_pairs={{0,32},{32,64},{64,96},{96,128},{128,160},{160,192},{192,224},{224... | collective-permute-start | bytes 245768 | tf_op jit(solution)/shard_map/ppermute | solution.py:424
  46.0 4.2 %collective-permute-start.5 = (bf16[160,256]{1,0:T(8,128)(2,1)S(1)}, bf16[160,256]{1,0:T(8,128)(2,1)S(1)}, u32[]{:S(2)}, u32[]{:S(2)}) collective-permute-start(bf16[160,256]{1,0:T(8,128)(2,1)S(1)} %get-tuple-element.56), channel_id=1, source_target_pairs={{0,224},{32,0},{64,32},{96,64},{128,96},{160,128},{192,160},{224,1... | collective-permute-start | bytes 245768 | tf_op jit(solution)/shard_map/ppermute | solution.py:424
  50.2 40.9 %collective-permute-start.6 = (bf16[512,256]{1,0:T(8,128)(2,1)S(1)}, bf16[512,256]{1,0:T(8,128)(2,1)S(1)}, u32[]{:S(2)}, u32[]{:S(2)}) collective-permute-start(bf16[512,256]{1,0:T(8,128)(2,1)S(1)} %get-tuple-element.59), channel_id=1, source_target_pairs={{0,1},{1,2},{2,3},{3,4},{4,5},{5,6},{6,7},{7,8},{8,9},{9,10},{10,1... | collective-permute-start | bytes 786440 | tf_op jit(solution)/shard_map/ppermute | solution.py:424
  50.3 40.8 %collective-permute-start.7 = (bf16[512,256]{1,0:T(8,128)(2,1)S(1)}, bf16[512,256]{1,0:T(8,128)(2,1)S(1)}, u32[]{:S(2)}, u32[]{:S(2)}) collective-permute-start(bf16[512,256]{1,0:T(8,128)(2,1)S(1)} %get-tuple-element.60), channel_id=1, source_target_pairs={{0,31},{1,0},{2,1},{3,2},{4,3},{5,4},{6,5},{7,6},{8,7},{9,8},{10,9... | collective-permute-start | bytes 786440 | tf_op jit(solution)/shard_map/ppermute | solution.py:424
  73.5 12.5 %all-to-all-start.2 = ((f32[8,16,128]{2,1,0:T(8,128)}), f32[8,16,128]{2,1,0:T(8,128)S(1)}, u32[]{:S(2)}, u32[]{:S(2)}) async-start(f32[8,16,128]{2,1,0:T(8,128)} %coarse_y.1), calls=%async_computation.2 | async-start | bytes 131072 | tf_op jit(solution)/shard_map/all_to_all | solution.py:428
  86.0 0.8 copy-start.5
  86.8 0.9 copy-start.7
  87.7 0.8 copy-start.10
  88.6 0.7 copy-start.18
  91.2 2.2 %copy-start.1 = (f32[4096,256]{1,0:T(8,128)S(1)}, f32[4096,256]{1,0:T(8,128)}, u32[]{:S(2)}) copy-start(f32[4096,256]{1,0:T(8,128)} %copy-done) | copy-start | bytes 12582916

commit v3 on v2

v3 whole, which is shorter than its diff:
```python
import jax
import jax.numpy as jnp
from jax import lax
from jax.experimental import pallas as pl
from jax.experimental.pallas import tpu as pltpu
from jax.sharding import PartitionSpec as P

OV = 4
MODES = 4
CX = 128
CY = 32
NZ = 256
EX = 136
EY = 40
GX = 4
ROWS = GX * EY
OWN = GX * CY
RIM = GX * OV
BLOCKS = CX // GX
CELLS = CX * CY
CHUNKS = 8
HI = lax.Precision.HIGHEST
f32 = jnp.float32
bf16 = jnp.bfloat16
sds = jax.ShapeDtypeStruct

VM = pl.BlockSpec(memory_space=pltpu.VMEM)
SM = pl.BlockSpec(memory_space=pltpu.SMEM)
ANY = pl.BlockSpec(memory_space=pl.ANY)
HBM = pl.BlockSpec(memory_space=pltpu.HBM)


def dot(a, b):
    return jnp.dot(a, b, preferred_element_type=f32)


def dot_t(a, b):
    return lax.dot_general(a, b, (((1,), (1,)), ((), ())), preferred_element_type=f32)


def dot_hi(a, b):
    return jnp.dot(a, b, preferred_element_type=f32, precision=HI)


def dot_t_hi(a, b):
    dims = (((1,), (1,)), ((), ()))
    return lax.dot_general(a, b, dims, preferred_element_type=f32, precision=HI)


def split(x):
    high = x.astype(bf16)
    return high, (x - high.astype(f32)).astype(bf16)


def iotas(shape):
    return lax.broadcasted_iota(jnp.int32, shape, 0), lax.broadcasted_iota(jnp.int32, shape, 1)


def pick(mask, kind=bf16):
    return jnp.where(mask, 1.0, 0.0).astype(kind)


def call(kernel, name, out_shape, in_specs, mib, out_specs=None, scratch=()):
    if out_specs is None:
        out_specs = jax.tree.map(lambda _: VM, out_shape)
    return pl.pallas_call(
        kernel,
        out_shape=out_shape,
        in_specs=in_specs,
        out_specs=out_specs,
        scratch_shapes=list(scratch),
        compiler_params=pltpu.CompilerParams(vmem_limit_bytes=mib << 20),
        name=name,
    )


def tile(ref, k, rows):
    return ref[pl.ds(pl.multiple_of(k * rows, rows), rows), :]


def selection(cyt):
    row, col = iotas((3 * RIM, OWN))
    y, k = iotas((CY, OWN))
    spread = dot(cyt, pick((k & 31) == y)).astype(bf16)
    row4, n = iotas((3 * RIM, MODES))
    modes = dot(pick((row4 & 3) == n), spread)
    plane = ((row >> 2) & 3) == (col >> 5)
    inner = col & 31
    target = jnp.where(row < RIM, row & 3, CY - OV + (row & 3))
    ones = jnp.where(inner == target, 1.0, 0.0)
    value = jnp.where(row < 2 * RIM, ones, modes)
    return jnp.where(plane, value, 0.0).astype(bf16)


def load_kernel(residual, cyt, own, first_x, last_x, rim_lo, rim_hi, along_y, sel, buf, sems, cyt_buf, sem):
    rows = CELLS // CHUNKS

    def copy(c):
        at = pl.ds(c * rows, rows)
        return pltpu.make_async_copy(residual.at[at, :], buf.at[at, :], sems.at[c])

    for c in range(CHUNKS):
        copy(c).start()
    small = pltpu.make_async_copy(cyt, cyt_buf, sem)
    small.start()
    small.wait()
    take = selection(cyt_buf[...])
    sel[...] = take
    for c in range(CHUNKS):
        copy(c).wait()
        for b in range(rows // OWN):
            k = c * (rows // OWN) + b
            data = buf[k * OWN : (k + 1) * OWN, :].astype(bf16)
            own[k * OWN : (k + 1) * OWN, :] = data
            if k == 0:
                first_x[...] = data
            if k == BLOCKS - 1:
                last_x[...] = data
            out = dot(take, data)
            at = slice(k * RIM, (k + 1) * RIM)
            rim_lo[at, :] = out[:RIM].astype(bf16)
            rim_hi[at, :] = out[RIM : 2 * RIM].astype(bf16)
            along_y[at, :] = out[2 * RIM :]


def load(residual, coarse_y):
    rim = sds((CX * OV, NZ), bf16)
    return call(
        load_kernel,
        "load",
        (
            sds((CELLS, NZ), bf16), sds((OWN, NZ), bf16), sds((OWN, NZ), bf16), rim, rim,
            sds((CX * MODES, NZ), f32), sds((3 * RIM, OWN), bf16),
        ),
        [HBM, HBM],
        16,
        scratch=[
            pltpu.VMEM((CELLS, NZ), f32), pltpu.SemaphoreType.DMA((CHUNKS,)),
            pltpu.VMEM((MODES, CY), bf16), pltpu.SemaphoreType.DMA,
        ],
    )(residual, coarse_y.T)


def corners_kernel(sel, rim_lo, rim_hi, xlo, xhi, after, down, up):
    down[: CX * OV, :] = rim_lo[...]
    up[: CX * OV, :] = rim_hi[...]
    for i, strip in enumerate((xlo, xhi)):
        out = dot(sel[: 2 * RIM, :], strip[...]).astype(bf16)
        at = slice(CX * OV + i * RIM, CX * OV + (i + 1) * RIM)
        down[at, :] = out[:RIM]
        up[at, :] = out[RIM:]


def corners(*args):
    side = sds((EX * OV, NZ), bf16)
    return call(corners_kernel, "corners", (side, side), [VM] * 5 + [ANY], 8)(*args)


PARAMS = (
    ((EX, EX), bf16), ((EY, EY), bf16), ((NZ, NZ), bf16), ((1, EX), f32), ((1, EY), f32),
    ((1, NZ), f32), ((MODES, CX), bf16), ((MODES, CY), bf16), ((MODES, NZ), bf16),
    ((32, 32), f32), ((128, 128), f32), ((MODES, MODES), f32), ((1, 32), f32), ((1, 128), f32),
    ((1, MODES), f32),
)
WEIGHTS = (
    ((ROWS, ROWS), bf16), ((ROWS, ROWS), bf16), ((OWN, ROWS + 2 * RIM), bf16),
    ((OWN, 2 * RIM), bf16), ((EX, EX), bf16), ((EX, EX), bf16), ((NZ, NZ), bf16),
    ((NZ, NZ), bf16), ((EX, NZ), f32), ((EY, NZ), f32), ((16, CX * MODES), bf16),
    ((CX * MODES, 32), bf16), ((MODES, NZ), f32), ((128, 128), f32), ((128, 128), f32),
    ((128, 128), f32), ((128, 128), f32),
)


def prepare_kernel(*refs):
    n = len(PARAMS)
    sources, outs, bufs, sems = (
        refs[:n], refs[n : n + len(WEIGHTS)], refs[n + len(WEIGHTS) : -1], refs[-1]
    )
    copies = [
        pltpu.make_async_copy(source, buf, sems.at[i])
        for i, (source, buf) in enumerate(zip(sources, bufs))
    ]
    for copy in copies:
        copy.start()
    for copy in copies:
        copy.wait()
    (
        lx, ly, lz, eig_x, eig_y, eig_z, cxt, cyt, czt, mode_x, mode_y, mode_z,
        ceig_x, ceig_y, ceig_z,
    ) = bufs
    (
        wy, wyt, wfin, spread, wx, wxt, lz_out, lzt, exb, eyz, bx, bxt, czf, modes_xz,
        mode_y_out, mode_yt, ceig,
    ) = outs

    def cell(k):
        y = jnp.where(k < OWN, OV + (k & 31), jnp.where(k < OWN + RIM, k & 3, EY - OV + (k & 3)))
        plane = jnp.where(k < OWN, k >> 5, ((k - OWN) >> 2) & 3)
        return y, plane

    def mode(j):
        plane = (j >= EY).astype(jnp.int32) + (j >= 2 * EY) + (j >= 3 * EY)
        return j - EY * plane, plane

    k, y = iotas((ROWS, EY))
    by_cell = dot(pick(cell(k)[0] == y), ly[...]).astype(bf16)
    b, j = iotas((EY, ROWS))
    k, col = iotas((ROWS, ROWS))
    value = dot(by_cell, pick(mode(j)[0] == b))
    value = jnp.where(cell(k)[1] == mode(col)[1], value, 0.0).astype(bf16)
    wyt[...] = value
    j, b = iotas((ROWS, EY))
    back = dot_t(pick(mode(j)[0] == b), by_cell)
    wy[...] = jnp.where(mode(k)[1] == cell(col)[1], back, 0.0).astype(bf16)

    y, k = iotas((CY, OWN))
    by_k = dot(cyt[...], pick((k & 31) == y)).astype(bf16)
    k, own = iotas((OWN, OWN))
    turned = dot_t(pick(k == own), by_k).astype(bf16)
    n, col = iotas((MODES, 2 * RIM))
    coarse = dot(turned, pick((col & 3) == n))
    k, col = iotas((OWN, 2 * RIM))
    inner = k & 31
    plane = (k >> 5) == ((col >> 2) & 3)
    coarse = jnp.where(plane, coarse, 0.0).astype(bf16)
    wfin[...] = jnp.concatenate([value[:OWN], coarse], 1)
    target = jnp.where(col < RIM, col & 3, CY - OV + (col & 3))
    spread[...] = jnp.where(plane, jnp.where(inner == target, 1.0, 0.0), 0.0).astype(bf16)

    k, x = iotas((EX, EX))
    source = jnp.where(k < CX, k + OV, jnp.where(k < CX + OV, k - CX, k))
    moved = dot(pick(source == x), lx[...]).astype(bf16)
    wxt[...] = moved
    wx[...] = dot_t(pick(k == x), moved).astype(bf16)
    column = jnp.sum(jnp.where(k == x, eig_x[...], 0.0), axis=1, keepdims=True)
    exb[...] = jnp.broadcast_to(column, (EX, NZ))
    b, y = iotas((EY, EY))
    column = jnp.sum(jnp.where(b == y, eig_y[...], 0.0), axis=1, keepdims=True)
    eyz[...] = column + eig_z[...]
    c, z = iotas((NZ, NZ))
    lz_out[...] = lz[...]
    lzt[...] = dot_t(pick(c == z), lz[...]).astype(bf16)
    czf[...] = czt[...].astype(f32)

    x, row = iotas((CX, CX * MODES))
    by_row = dot(cxt[...], pick((row >> 2) == x)).astype(bf16)
    col, m = iotas((16, MODES))
    value = dot(pick((col >> 2) == m), by_row)
    col, row = iotas((16, CX * MODES))
    flat = jnp.where((row & 3) == (col & 3), value, 0.0).astype(bf16)
    bx[...] = flat
    col, i = iotas((32, 16))
    twice = dot(pick((col & 15) == i), flat)
    bxt[...] = twice.T.astype(bf16)

    r, i = iotas((128, 32))
    a, col = iotas((32, 128))
    to_a = pick((col >> 2) == a, f32)
    part_x = dot_hi(dot_hi(pick((r >> 2) == i, f32), mode_x[...]), to_a)
    r, p = iotas((128, MODES))
    c, col = iotas((MODES, 128))
    to_c = pick((col & 3) == c, f32)
    part_z = dot_hi(dot_hi(pick((r & 3) == p, f32), mode_z[...]), to_c)
    modes_xz[...] = part_x * part_z
    mode_y_out[...] = mode_y[...]
    mode_yt[...] = mode_y[...].T
    eight_x = jnp.broadcast_to(ceig_x[...], (8, 32))
    eight_z = jnp.broadcast_to(ceig_z[...], (8, MODES))
    row = (dot_hi(eight_x, to_a) + dot_hi(eight_z, to_c))[:1]
    r, b = iotas((128, 128))
    column = jnp.sum(jnp.where(r == b, ceig_y[...], 0.0), axis=1, keepdims=True)
    ceig[...] = column + row


def prepare(*params):
    return call(
        prepare_kernel,
        "prepare",
        tuple(sds(*w) for w in WEIGHTS),
        [HBM] * len(PARAMS),
        8,
        scratch=[pltpu.VMEM(*p) for p in PARAMS] + [pltpu.SemaphoreType.DMA((len(PARAMS),))],
    )(*params)


def solve_kernel(
    own, xlo, xhi, ylo, yhi, wy, wyt, wx, wxt, lz, lzt, exb, eyz, after,
    field, out_xlo, out_xhi, out_ylo, out_yhi, mid,
):
    def put(rows, value):
        field[0, rows, :] = value[:, :128]
        field[1, rows, :] = value[:, 128:]

    def take(rows):
        return jnp.concatenate([field[0, rows, :], field[1, rows, :]], 1)

    def forward_y(main, k):
        data = jnp.concatenate([main, tile(ylo, k, RIM), tile(yhi, k, RIM)], 0)
        put(pl.ds(pl.multiple_of(k * ROWS, ROWS), ROWS), dot(wy[...], data))

    def first(k, carry):
        forward_y(tile(own, k, OWN), k)
        return carry

    lax.fori_loop(0, BLOCKS, first, 0, unroll=4)
    forward_y(xlo[...], BLOCKS)
    forward_y(xhi[...], BLOCKS + 1)

    def mid_rows(b):
        return pl.ds(pl.multiple_of(b * EX, 8), EX)

    def forward_x(b, carry):
        plane = take(pl.ds(b, EX, stride=EY)).astype(bf16)
        mid[mid_rows(b), :] = dot(wx[...], plane)
        return carry

    lax.fori_loop(0, EY, forward_x, 0, unroll=8)

    def both_z(i, carry):
        at = pl.ds(pl.multiple_of(i * 4 * EX, 8), 4 * EX)
        along = dot(mid[at, :].astype(bf16), lz[...])
        parts = []
        for q in range(4):
            scale = exb[...] + eyz[pl.ds(i * 4 + q, 1), :]
            parts.append((along[q * EX : (q + 1) * EX] / scale))
        spectral = jnp.concatenate(parts, 0).astype(bf16)
        mid[at, :] = dot(spectral, lzt[...])
        return carry

    lax.fori_loop(0, EY // 4, both_z, 0)

    def backward_x(b, carry):
        put(pl.ds(b, EX, stride=EY), dot(wxt[...], mid[mid_rows(b), :].astype(bf16)))
        return carry

    lax.fori_loop(0, EY, backward_x, 0, unroll=8)

    def planes(k):
        return take(pl.ds(pl.multiple_of(k * ROWS, ROWS), ROWS)).astype(bf16)

    def last(k, carry):
        out = dot(wyt[OWN:, :], planes(k)).astype(bf16)
        at = pl.ds(pl.multiple_of(k * RIM, RIM), RIM)
        out_ylo[at, :] = out[:RIM]
        out_yhi[at, :] = out[RIM:]
        return carry

    out_xlo[...] = dot(wyt[...], planes(BLOCKS)).astype(bf16)
    out_xhi[...] = dot(wyt[...], planes(BLOCKS + 1)).astype(bf16)
    lax.fori_loop(0, BLOCKS, last, 0, unroll=4)


def solve(*args):
    strip = sds((ROWS, NZ), bf16)
    rim = sds((CX * OV, NZ), bf16)
    return call(
        solve_kernel,
        "solve",
        (sds((2, EX * EY, NZ // 2), f32), strip, strip, rim, rim),
        [VM] * 13 + [ANY],
        16,
        scratch=[pltpu.VMEM((EX * EY, NZ), f32)],
    )(*args)


def fold_kernel(out_ylo, out_yhi, rxlo, rxhi, after, down, up):
    end = CX * OV
    for strip, start, out in ((out_ylo, OWN, down), (out_yhi, OWN + RIM, up)):
        rows = slice(start, start + RIM)
        out[...] = strip[...]
        low = strip[:RIM, :].astype(f32) + rxlo[rows, :].astype(f32)
        high = strip[end - RIM :, :].astype(f32) + rxhi[rows, :].astype(f32)
        out[:RIM, :] = low.astype(bf16)
        out[end - RIM :, :] = high.astype(bf16)


def fold(*args):
    rim = sds((CX * OV, NZ), bf16)
    return call(fold_kernel, "fold", (rim, rim), [VM] * 4 + [ANY], 8)(*args)


def restrict_kernel(along_y, bx, czf, out):
    high, low = split(along_y[...])
    both = dot(bx[...], high) + dot(bx[...], low)
    own = dot_t_hi(both, czf[...])
    flat = jnp.concatenate([own[m * MODES : (m + 1) * MODES] for m in range(MODES)], 1)
    for i in range(out.shape[0]):
        out[i] = flat


def coarse_x_kernel(rows, modes_xz, out):
    part = sum(dot_hi(rows[i], modes_xz[16 * i : 16 * i + 16, :]) for i in range(8))
    for i in range(out.shape[0]):
        out[i] = part


def coarse_kernel(rows, modes_xz, mode_y, mode_yt, ceig, czf, bxt, out):
    columns = jnp.concatenate([rows[j] for j in range(rows.shape[0])], 0)
    hat = dot_hi(mode_yt[...], columns) / ceig[...]
    row, col = iotas((8, 128))
    mine = pick(col == lax.axis_index("gy") * MODES + row, f32)
    rows_y = dot_hi(mine, mode_y[...])
    rows_xz = modes_xz[pl.ds(pl.multiple_of(lax.axis_index("gx") * 16, 16), 16), :]
    sol = dot_t_hi(dot_hi(rows_y, hat), rows_xz)
    shape = jnp.concatenate(
        [dot_hi(sol[:, m * MODES : (m + 1) * MODES], czf[...])[:MODES] for m in range(MODES)], 0
    )
    high, low = split(shape)
    value = dot(bxt[...], jnp.concatenate([high, low], 0))
    high, low = split(value)
    for k in range(BLOCKS):
        at = slice(k * RIM, (k + 1) * RIM)
        out[2 * k * RIM : (2 * k + 1) * RIM, :] = high[at]
        out[(2 * k + 1) * RIM : (2 * k + 2) * RIM, :] = low[at]


def finish_kernel(field, wfin, shape, after, fix):
    def step(k, carry):
        at = pl.ds(pl.multiple_of(k * ROWS, ROWS), ROWS)
        planes = jnp.concatenate([field[0, at, :], field[1, at, :]], 1).astype(bf16)
        data = jnp.concatenate([planes, tile(shape, k, 2 * RIM)], 0)
        fix[pl.ds(pl.multiple_of(k * OWN, OWN), OWN), :] = dot(wfin[...], data)
        return carry

    lax.fori_loop(0, BLOCKS, step, 0, unroll=4)


def combine_kernel(fix, spread, rxlo, rxhi, rylo, ryhi, out, buf, sems):
    rows = CELLS // CHUNKS

    def copy(c):
        at = pl.ds(c * rows, rows)
        return pltpu.make_async_copy(buf.at[at, :], out.at[at, :], sems.at[c])

    for c in range(CHUNKS):
        for b in range(rows // OWN):
            k = c * (rows // OWN) + b
            rim = slice(k * RIM, (k + 1) * RIM)
            data = jnp.concatenate([rylo[rim, :], ryhi[rim, :]], 0)
            total = fix[k * OWN : (k + 1) * OWN, :] + dot(spread[...], data)
            if k == 0:
                total = total + rxlo[:OWN, :].astype(f32)
            if k == BLOCKS - 1:
                total = total + rxhi[:OWN, :].astype(f32)
            buf[k * OWN : (k + 1) * OWN, :] = total
        copy(c).start()
    for c in range(CHUNKS):
        copy(c).wait()


def combine(*args):
    return call(
        combine_kernel,
        "combine",
        sds((CELLS, NZ), f32),
        [VM] * 6,
        16,
        out_specs=HBM,
        scratch=[pltpu.VMEM((CELLS, NZ), f32), pltpu.SemaphoreType.DMA((CHUNKS,))],
    )(*args)


def shift(x, axis, step):
    size = lax.axis_size(axis)
    return lax.ppermute(x, axis, [(i, (i + step) % size) for i in range(size)])


def exchange(x, axis):
    return lax.all_to_all(x, axis, 0, 0)


def local(
    residual, local_x, local_y, local_z, eig_x, eig_y, eig_z, coarse_x, coarse_y, coarse_z,
    mode_x, mode_y, mode_z, coarse_eig_x, coarse_eig_y, coarse_eig_z,
):
    own, first_x, last_x, rim_lo, rim_hi, along_y, sel = load(
        residual.reshape(CELLS, NZ), coarse_y
    )
    xlo = shift(last_x, "gx", 1)
    xhi = shift(first_x, "gx", -1)
    (
        wy, wyt, wfin, spread, wx, wxt, lz, lzt, exb, eyz, bx, bxt, czf, modes_xz,
        mode_y, mode_yt, ceig,
    ) = prepare(
        local_x, local_y, local_z, eig_x[None], eig_y[None], eig_z[None], coarse_x.T, coarse_y.T,
        coarse_z.T, mode_x, mode_y, mode_z, coarse_eig_x[None], coarse_eig_y[None],
        coarse_eig_z[None],
    )
    own_coarse = call(
        restrict_kernel, "restrict", sds((8, MODES, 16), f32), [VM] * 3, 8
    )(along_y, bx, czf)
    rows = exchange(own_coarse, "gx")
    down, up = corners(sel, rim_lo, rim_hi, xlo, xhi, own_coarse)
    ylo = shift(up, "gy", 1)
    yhi = shift(down, "gy", -1)
    part = call(coarse_x_kernel, "coarse_x", sds((32, MODES, 128), f32), [VM] * 2, 4)(
        rows, modes_xz
    )
    rows = exchange(part, "gy")

    field, out_xlo, out_xhi, out_ylo, out_yhi = solve(
        own, xlo, xhi, ylo, yhi, wy, wyt, wx, wxt, lz, lzt, exb, eyz, part
    )

    rxlo = shift(out_xhi, "gx", 1)
    rxhi = shift(out_xlo, "gx", -1)
    shape = call(
        coarse_kernel, "coarse", sds((2 * CX * MODES, NZ), bf16), [VM] * 7, 8
    )(rows, modes_xz, mode_y, mode_yt, ceig, czf, bxt)
    down, up = fold(out_ylo, out_yhi, rxlo, rxhi, shape)
    rylo = shift(up, "gy", 1)
    ryhi = shift(down, "gy", -1)
    fix = call(
        finish_kernel, "finish", sds((CELLS, NZ), f32), [VM] * 3 + [ANY], 16
    )(field, wfin, shape, up)
    out = combine(fix, spread, rxlo, rxhi, rylo, ryhi)
    return out.reshape(CX, CY, NZ)


def solution(mesh):
    placed = (P("gx", "gy", None),) + (P(),) * 15
    return jax.shard_map(
        local, mesh=mesh, in_specs=placed, out_specs=P("gx", "gy", None), check_vma=False
    )
```

time: 97.3 us -> 82.6 us (0.85)
  the two profiles are of different devices: /device:TPU:1 before, /device:TPU:6 now
where the time goes in v3:
time: 82.6 us; the launch traced here: 81.9 us
  Pallas kernels  23.5 us (28%)
  starting transfers between devices  23 us (28%)
  local copies, waits for them, and re-layouts  20.6 us (25%)
  blocking collectives  7.85 us (10%)
  waiting for transfers between devices  6.49 us (8%)
    unnamed x88, local copies, waits for them, and re-layouts  20.6 us
    ppermute x8, starting transfers between devices, shift(): return lax.ppermute(x, axis, [(i, (i + step) % size) for i in range(size)])  17.1 us
    pallas_call x1, Pallas kernels, solve(): call(solve_kernel, 'solve', (sds((2, EX * EY, NZ // 2), f32), strip, stri...  12 us
    all_to_all x1, blocking collectives, exchange(): return lax.all_to_all(x, axis, 0, 0)  7.85 us
    ppermute x8, waiting for transfers between devices, shift(): return lax.ppermute(x, axis, [(i, (i + step) % size) for i in range(size)])  6.49 us
    all_to_all x1, starting transfers between devices, exchange(): return lax.all_to_all(x, axis, 0, 0)  5.89 us
    pallas_call x1, Pallas kernels, combine(): call(combine_kernel, 'combine', sds((CELLS, NZ), f32), [VM] * 6, 16, out_...  2.27 us
    pallas_call x1, Pallas kernels, prepare(): call(prepare_kernel, 'prepare', tuple((sds(*w) for w in WEIGHTS)), [HBM]...  2.13 us
  transfers between devices with their start and end apart: 9, of which 2 were waited for; matrix products, arithmetic and copies ran while one was open for 0% of the time, Pallas kernels for 22%

profile of v3, /device:TPU:6, one launch (start us, length us, event | category | flops | bytes accessed | tf_op | source)
XLA Modules:
  0.0 81.9 jit_solution(14986689142210219219)
XLA Ops:
  0.0 2.2 %copy-done.2 = f32[128,32,256]{2,1,0:T(8,128)S(1)} copy-done((f32[128,32,256]{2,1,0:T(8,128)S(1)}, f32[128,32,256]{2,1,0:T(8,128)}, u32[]{:S(2)}) %copy-start.2) | copy-done | bytes 4194328
  2.2 0.7 copy-done.34
  3.0 2.0 %load.1 = (bf16[4096,256]{1,0:T(8,128)(2,1)S(1)}, bf16[128,256]{1,0:T(8,128)(2,1)S(1)}, bf16[128,256]{1,0:T(8,128)(2,1)S(1)}, bf16[512,256]{1,0:T(8,128)(2,1)S(1...) custom-call(f32[4096,256]{1,0:T(8,128)S(1)} %bitcast.11, ...), custom_call_target="tpu_custom_call" | custom-call | tf_op jit(solution)/shard_map/load/pallas_call | solution.py:128
  5.0 0.0 collective-permute-start
  5.0 1.7 %collective-permute-start.1 = (bf16[128,256]{1,0:T(8,128)(2,1)S(1)}, bf16[128,256]{1,0:T(8,128)(2,1)S(1)}, u32[]{:S(2)}, u32[]{:S(2)}) collective-permute-start(bf16[128,256]{1,0:T(8,128)(2,1)S(1)} %get-tuple-element.40), channel_id=1, source_target_pairs={{0,224},{32,0},{64,32},{96,64},{128,96},{160,128},{192,160},{224,1... | collective-permute-start | bytes 196616 | tf_op jit(solution)/shard_map/ppermute | solution.py:465
  6.9 2.1 %prepare.1 = (bf16[160,160]{1,0:T(8,128)(2,1)S(1)}, bf16[160,160]{1,0:T(8,128)(2,1)S(1)}, bf16[128,192]{1,0:T(8,128)(2,1)S(1)}, bf16[128,32]{1,0:T(8,128)(2,1)S(...) custom-call(bf16[136,136]{1,0:T(8,128)(2,1)S(1)} %copy-done.18, ...), custom_call_target="tpu_custom_call" | custom-call | tf_op jit(solution)/shard_map/prepare/pallas_call | solution.py:276
  9.0 0.6 copy-done.16
  9.7 0.6 copy-done.28
  10.3 0.4 restrict.1.after
  10.7 0.0 collective-permute-done.xlo
  10.7 0.0 collective-permute-done.1.xhi
  10.8 0.2 copy-done.3
  10.9 0.0 copy-done.5
  11.0 0.1 copy-done.7
  11.0 0.0 copy-done.9
  11.1 0.9 %corners.1 = (bf16[544,256]{1,0:T(8,128)(2,1)S(1)}, bf16[544,256]{1,0:T(8,128)(2,1)}) custom-call(bf16[48,128]{1,0:T(8,128)(2,1)S(1)} %get-tuple-element.41.sel, bf16[512,256]{1,0:T(8,128)(2,1)S(1)} %get-tuple-element.42.rim_lo, bf16[512,256]{1,0:T(8,128)(2,1)S(1)} %get-tuple-element.43.rim_hi, bf16[128,256]{1,0:T(8,128)(2,1)S(1)} %collective-permute-done.xlo, ...), custom_call_target="tpu_custom_call" | custom-call | tf_op jit(solution)/shard_map/corners/pallas_call | solution.py:156
  11.9 1.6 %collective-permute-start.2 = (bf16[544,256]{1,0:T(8,128)(2,1)}, bf16[544,256]{1,0:T(8,128)(2,1)S(1)}, u32[]{:S(2)}, u32[]{:S(2)}) collective-permute-start(bf16[544,256]{1,0:T(8,128)(2,1)} %get-tuple-element.47), channel_id=1, source_target_pairs={{0,1},{1,2},{2,3},{3,4},{4,5},{5,6},{6,7},{7,8},{8,9},{9,10},{10,1... | collective-permute-start | bytes 835592 | tf_op jit(solution)/shard_map/ppermute | solution.py:465
  13.5 6.7 %collective-permute-start.3 = (bf16[544,256]{1,0:T(8,128)(2,1)S(1)}, bf16[544,256]{1,0:T(8,128)(2,1)S(1)}, u32[]{:S(2)}, u32[]{:S(2)}) collective-permute-start(bf16[544,256]{1,0:T(8,128)(2,1)S(1)} %get-tuple-element.48), channel_id=1, source_target_pairs={{0,31},{1,0},{2,1},{3,2},{4,3},{5,4},{6,5},{7,6},{8,7},{9,8},{10,9... | collective-permute-start | bytes 835592 | tf_op jit(solution)/shard_map/ppermute | solution.py:465
  20.2 7.9 %all_to_all.10.rows = f32[8,4,16]{2,1,0:T(4,128)S(1)} all-to-all(f32[8,4,16]{2,1,0:T(4,128)S(1)} %restrict.1.after), channel_id=1, replica_groups=mesh['gx'=8,'gy'=32] {'gx'}, dimensions={0} | all-to-all | bytes 4096 | tf_op jit(solution)/shard_map/all_to_all | solution.py:469
  28.1 0.9 %coarse_x.1.after = f32[32,4,128]{2,1,0:T(4,128)} custom-call(f32[8,4,16]{2,1,0:T(4,128)S(1)} %all_to_all.10.rows, f32[128,128]{1,0:T(8,128)S(1)} %get-tuple-element.57.modes_xz), custom_call_target="tpu_custom_call" | custom-call | tf_op jit(solution)/shard_map/coarse_x/pallas_call | solution.py:496
  29.0 5.9 %all-to-all-start.1 = ((f32[32,4,128]{2,1,0:T(4,128)}), f32[32,4,128]{2,1,0:T(4,128)S(1)}, u32[]{:S(2)}, u32[]{:S(2)}) async-start(f32[32,4,128]{2,1,0:T(4,128)} %coarse_x.1.after), calls=%async_computation.1 | async-start | bytes 131072 | tf_op jit(solution)/shard_map/all_to_all | solution.py:469
  34.9 0.0 collective-permute-done.2.ylo
  34.9 0.0 collective-permute-done.3.yhi
  35.0 0.9 %copy-done.4 = f32[136,256]{1,0:T(8,128)S(1)} copy-done((f32[136,256]{1,0:T(8,128)S(1)}, f32[136,256]{1,0:T(8,128)}, u32[]{:S(2)}) %copy-start.4) | copy-done | bytes 139288
  35.9 0.9 %copy-done.6 = bf16[256,256]{1,0:T(8,128)(2,1)S(1)} copy-done((bf16[256,256]{1,0:T(8,128)(2,1)S(1)}, bf16[256,256]{1,0:T(8,128)(2,1)}, u32[]{:S(2)}) %copy-start.6) | copy-done | bytes 131096
  36.8 0.9 %copy-done.8 = bf16[256,256]{1,0:T(8,128)(2,1)S(1)} copy-done((bf16[256,256]{1,0:T(8,128)(2,1)S(1)}, bf16[256,256]{1,0:T(8,128)(2,1)}, u32[]{:S(2)}) %copy-start.8) | copy-done | bytes 131096
  37.7 0.9 %copy-done.13 = bf16[160,160]{1,0:T(8,128)(2,1)S(1)} copy-done((bf16[160,160]{1,0:T(8,128)(2,1)S(1)}, bf16[160,160]{1,0:T(8,128)(2,1)}, u32[]{:S(2)}) %copy-start.13) | copy-done | bytes 51224
  38.5 0.9 %copy-done.15 = bf16[136,136]{1,0:T(8,128)(2,1)S(1)} copy-done((bf16[136,136]{1,0:T(8,128)(2,1)S(1)}, bf16[136,136]{1,0:T(8,128)(2,1)}, u32[]{:S(2)}) %copy-start.15) | copy-done | bytes 37016
  39.4 0.9 %copy-done.17 = bf16[136,136]{1,0:T(8,128)(2,1)S(1)} copy-done((bf16[136,136]{1,0:T(8,128)(2,1)S(1)}, bf16[136,136]{1,0:T(8,128)(2,1)}, u32[]{:S(2)}) %copy-start.17) | copy-done | bytes 37016
  40.3 0.8 copy-done.29
  41.1 12.0 %solve.1 = (f32[2,5440,128]{2,1,0:T(8,128)S(1)}, bf16[160,256]{1,0:T(8,128)(2,1)}, bf16[160,256]{1,0:T(8,128)(2,1)}, bf16[512,256]{1,0:T(8,128)(2,1)S(1)}, bf16[512,256]{1,0:T(8,128)(2,1)S(1)}) custom-call(bf16[4096,256]{1,0:T(8,128)(2,1)S(1)} %get-tuple-element.38.own, bf16[128,256]{1,0:T(8,128)(2,1)S(1)} %collective-permute-done.xlo, ...), custom_call_target="tpu_custom_call" | custom-call | tf_op jit(solution)/shard_map/solve/pallas_call | solution.py:356
  53.1 2.4 %copy-done = f32[2,5440,128]{2,1,0:T(8,128)} copy-done((f32[2,5440,128]{2,1,0:T(8,128)}, f32[2,5440,128]{2,1,0:T(8,128)S(1)}, u32[]{:S(2)}) %copy-start) | copy-done | bytes 5570584
  55.6 0.0 collective-permute-start.4
  55.6 1.7 %collective-permute-start.5 = (bf16[160,256]{1,0:T(8,128)(2,1)}, bf16[160,256]{1,0:T(8,128)(2,1)S(1)}, u32[]{:S(2)}, u32[]{:S(2)}) collective-permute-start(bf16[160,256]{1,0:T(8,128)(2,1)} %get-tuple-element.67), channel_id=1, source_target_pairs={{0,224},{32,0},{64,32},{96,64},{128,96},{160,128},{192,160},{224,1... | collective-permute-start | bytes 245768 | tf_op jit(solution)/shard_map/ppermute | solution.py:465
  57.3 0.0 all-to-all-done.1.rows
  57.3 0.9 %copy-done.10 = bf16[512,32]{1,0:T(8,128)(2,1)S(1)} copy-done((bf16[512,32]{1,0:T(8,128)(2,1)S(1)}, bf16[512,32]{1,0:T(8,128)(2,1)}, u32[]{:S(2)}) %copy-start.10) | copy-done | bytes 32792
  58.2 0.8 %copy-done.21 = f32[128,128]{1,0:T(8,128)S(1)} copy-done((f32[128,128]{1,0:T(8,128)S(1)}, f32[128,128]{1,0:T(8,128)}, u32[]{:S(2)}) %copy-start.21) | copy-done | bytes 65560
  59.0 0.8 %copy-done.23 = f32[128,128]{1,0:T(8,128)S(1)} copy-done((f32[128,128]{1,0:T(8,128)S(1)}, f32[128,128]{1,0:T(8,128)}, u32[]{:S(2)}) %copy-start.23) | copy-done | bytes 65560
  59.9 0.8 %copy-done.25 = f32[128,128]{1,0:T(8,128)S(1)} copy-done((f32[128,128]{1,0:T(8,128)S(1)}, f32[128,128]{1,0:T(8,128)}, u32[]{:S(2)}) %copy-start.25) | copy-done | bytes 65560
  60.7 0.7 copy-done.31
  61.4 1.1 %coarse.1.after.shape = bf16[1024,256]{1,0:T(8,128)(2,1)S(1)} custom-call(f32[32,4,128]{2,1,0:T(4,128)S(1)} %all-to-all-done.1.rows, f32[128,128]{1,0:T(8,128)S(1)} %get-tuple-element.57.modes_xz, f32[128,128]{1,0:T(8,128)S(1)} %copy-done.21, f32[128,128]{1,0:T(8,128)S(1)} %copy-done.23, f32[128,128]{1,0:T(8,128)S(1)} %copy-done.25, ...), custom_call_target="tpu_custom_call" | custom-call | tf_op jit(solution)/shard_map/coarse/pallas_call | solution.py:507
  62.6 5.3 %collective-permute-start.7 = (bf16[512,256]{1,0:T(8,128)(2,1)S(1)}, bf16[512,256]{1,0:T(8,128)(2,1)S(1)}, u32[]{:S(2)}, u32[]{:S(2)}) collective-permute-start(bf16[512,256]{1,0:T(8,128)(2,1)S(1)} %get-tuple-element.70), channel_id=1, source_target_pairs={{0,31},{1,0},{2,1},{3,2},{4,3},{5,4},{6,5},{7,6},{8,7},{9,8},{10,9... | collective-permute-start | bytes 786440 | tf_op jit(solution)/shard_map/ppermute | solution.py:465
  67.8 2.6 %copy-done.1 = f32[2,5440,128]{2,1,0:T(8,128)S(1)} copy-done((f32[2,5440,128]{2,1,0:T(8,128)S(1)}, f32[2,5440,128]{2,1,0:T(8,128)}, u32[]{:S(2)}) %copy-start.1) | copy-done | bytes 5570584
  70.4 0.8 %copy-done.27 = bf16[128,192]{1,0:T(8,128)(2,1)S(1)} copy-done((bf16[128,192]{1,0:T(8,128)(2,1)S(1)}, bf16[128,192]{1,0:T(8,128)(2,1)}, u32[]{:S(2)}) %copy-start.27) | copy-done | bytes 49176
  71.3 1.9 %finish.1.fix = f32[4096,256]{1,0:T(8,128)S(1)} custom-call(f32[2,5440,128]{2,1,0:T(8,128)S(1)} %copy-done.1, bf16[128,192]{1,0:T(8,128)(2,1)S(1)} %copy-done.27, bf16[1024,256]{1,0:T(8,128)(2,1)S(1)} %coarse.1.after.shape, bf16[512,256]{1,0:T(8,128)(2,1)S(1)} %get-tuple-element.68.after), custom_call_target="tpu_custom_call" | custom-call | tf_op jit(solution)/shard_map/finish/pallas_call | solution.py:513
  73.1 0.9 %collective-permute-done.7.ryhi = bf16[512,256]{1,0:T(8,128)(2,1)S(1)} collective-permute-done((bf16[512,256]{1,0:T(8,128)(2,1)S(1)}, bf16[512,256]{1,0:T(8,128)(2,1)S(1)}, u32[]{:S(2)}, u32[]{:S(2)}) %collective-permute-start.7) | collective-permute-done | bytes 262176 | tf_op jit(solution)/shard_map/ppermute | solution.py:465
  74.1 5.5 %collective-permute-done.6.rylo = bf16[512,256]{1,0:T(8,128)(2,1)S(1)} collective-permute-done((bf16[512,256]{1,0:T(8,128)(2,1)S(1)}, bf16[512,256]{1,0:T(8,128)(2,1)S(1)}, u32[]{:S(2)}, u32[]{:S(2)}) %collective-permute-start.6) | collective-permute-done | bytes 262176 | tf_op jit(solution)/shard_map/ppermute | solution.py:465
  79.6 2.3 %combine.1 = f32[4096,256]{1,0:T(8,128)} custom-call(f32[4096,256]{1,0:T(8,128)S(1)} %finish.1.fix, bf16[128,32]{1,0:T(8,128)(2,1)S(1)} %get-tuple-element.69.spread, bf16[160,256]{1,0:T(8,128)(2,1)S(1)} %collective-permute-done.4.rxlo, bf16[160,256]{1,0:T(8,128)(2,1)S(1)} %collective-permute-done.5.rxhi, bf16[512,256]{1,0:T(8,128)(2,1)S(1)} %collective-permute-done.6.rylo, ...), custom_call_target="tpu_custom_call" | custom-call | tf_op jit(solution)/shard_map/combine/pallas_call | solution.py:452
  (69 shorter events, 0.2 us)
Async XLA Ops:
  0.0 6.8 %copy-start.35 = (bf16[256,4]{0,1:T(4,128)(2,1)S(1)}, bf16[256,4]{0,1:T(4,128)(2,1)}, u32[]{:S(2)}) copy-start(bf16[256,4]{0,1:T(4,128)(2,1)} %param.25) | copy-start | bytes 6148
  0.0 6.8 %copy-start.40 = (f32[40]{0:T(128)S(1)}, f32[40]{0:T(128)}, u32[]{:S(2)}) copy-start(f32[40]{0:T(128)} %param.21) | copy-start | bytes 484
  0.0 6.8 %copy-start.37 = (f32[136]{0:T(256)S(1)}, f32[136]{0:T(256)}, u32[]{:S(2)}) copy-start(f32[136]{0:T(256)} %param.20) | copy-start | bytes 1636
  0.0 2.2 %copy-start.2 = (f32[128,32,256]{2,1,0:T(8,128)S(1)}, f32[128,32,256]{2,1,0:T(8,128)}, u32[]{:S(2)}) copy-start(f32[128,32,256]{2,1,0:T(8,128)} %param.16) | copy-start | bytes 12582916
  2.9 3.9 %copy-start.11 = (bf16[256,256]{1,0:T(8,128)(2,1)S(1)}, bf16[256,256]{1,0:T(8,128)(2,1)}, u32[]{:S(2)}) copy-start(bf16[256,256]{1,0:T(8,128)(2,1)} %refs_2_.1) | copy-start | bytes 393220
  2.9 3.9 %copy-start.18 = (bf16[136,136]{1,0:T(8,128)(2,1)S(1)}, bf16[136,136]{1,0:T(8,128)(2,1)}, u32[]{:S(2)}) copy-start(bf16[136,136]{1,0:T(8,128)(2,1)} %refs_0_.1) | copy-start | bytes 110980
  2.9 3.9 %copy-start.19 = (f32[128,128]{1,0:T(8,128)S(1)}, f32[128,128]{1,0:T(8,128)}, u32[]{:S(2)}) copy-start(f32[128,128]{1,0:T(8,128)} %refs_10_.1) | copy-start | bytes 196612
  2.9 3.9 %copy-start.32 = (f32[32,32]{1,0:T(8,128)S(1)}, f32[32,32]{1,0:T(8,128)}, u32[]{:S(2)}) copy-start(f32[32,32]{1,0:T(8,128)} %refs_9_.1) | copy-start | bytes 12292
  2.9 3.9 %copy-start.33 = (bf16[40,40]{1,0:T(8,128)(2,1)S(1)}, bf16[40,40]{1,0:T(8,128)(2,1)}, u32[]{:S(2)}) copy-start(bf16[40,40]{1,0:T(8,128)(2,1)} %refs_1_.1) | copy-start | bytes 9604
  2.9 3.9 %copy-start.36 = (f32[4,4]{1,0:T(4,128)S(1)}, f32[4,4]{1,0:T(4,128)}, u32[]{:S(2)}) copy-start(f32[4,4]{1,0:T(4,128)} %refs_11_.1) | copy-start | bytes 196
  2.9 3.9 %copy-start.38 = (f32[256]{0:T(256)S(1)}, f32[256]{0:T(256)}, u32[]{:S(2)}) copy-start(f32[256]{0:T(256)} %param.22) | copy-start | bytes 3076
  3.0 3.9 %copy-start.39 = (bf16[128,4]{0,1:T(4,128)(2,1)S(1)}, bf16[128,4]{0,1:T(4,128)(2,1)}, u32[]{:S(2)}) copy-start(bf16[128,4]{0,1:T(4,128)(2,1)} %param.23) | copy-start | bytes 3076
  3.0 3.9 %copy-start.41 = (f32[32]{0:T(128)S(1)}, f32[32]{0:T(128)}, u32[]{:S(2)}) copy-start(f32[32]{0:T(128)} %param.29) | copy-start | bytes 388
  3.0 3.9 %copy-start.42 = (f32[128]{0:T(128)S(1)}, f32[128]{0:T(128)}, u32[]{:S(2)}) copy-start(f32[128]{0:T(128)} %param.30) | copy-start | bytes 1540
  3.0 3.9 %copy-start.43 = (f32[4]{0:T(128)S(1)}, f32[4]{0:T(128)}, u32[]{:S(2)}) copy-start(f32[4]{0:T(128)} %param.31) | copy-start | bytes 52
  5.0 5.7 %collective-permute-start = (bf16[128,256]{1,0:T(8,128)(2,1)S(1)}, bf16[128,256]{1,0:T(8,128)(2,1)S(1)}, u32[]{:S(2)}, u32[]{:S(2)}) collective-permute-start(bf16[128,256]{1,0:T(8,128)(2,1)S(1)} %get-tuple-element.39), channel_id=1, source_target_pairs={{0,32},{32,64},{64,96},{96,128},{128,160},{160,192},{192,224},{224... | collective-permute-start | bytes 196616 | tf_op jit(solution)/shard_map/ppermute | solution.py:465
  5.0 5.7 %collective-permute-start.1 = (bf16[128,256]{1,0:T(8,128)(2,1)S(1)}, bf16[128,256]{1,0:T(8,128)(2,1)S(1)}, u32[]{:S(2)}, u32[]{:S(2)}) collective-permute-start(bf16[128,256]{1,0:T(8,128)(2,1)S(1)} %get-tuple-element.40), channel_id=1, source_target_pairs={{0,224},{32,0},{64,32},{96,64},{128,96},{160,128},{192,160},{224,1... | collective-permute-start | bytes 196616 | tf_op jit(solution)/shard_map/ppermute | solution.py:465
  10.3 0.7 copy-start.5
  10.3 0.8 copy-start.7
  10.3 0.8 copy-start.9
  10.3 17.8 %copy-start.12 = (bf16[160,160]{1,0:T(8,128)(2,1)}, bf16[160,160]{1,0:T(8,128)(2,1)S(1)}, u32[]{:S(2)}) copy-start(bf16[160,160]{1,0:T(8,128)(2,1)S(1)} %get-tuple-element.50.wyt) | copy-start | bytes 153604
  10.3 17.8 %copy-start.14 = (bf16[136,136]{1,0:T(8,128)(2,1)}, bf16[136,136]{1,0:T(8,128)(2,1)S(1)}, u32[]{:S(2)}) copy-start(bf16[136,136]{1,0:T(8,128)(2,1)S(1)} %get-tuple-element.51.wx) | copy-start | bytes 110980
  10.3 17.8 %copy-start.20 = (f32[128,128]{1,0:T(8,128)}, f32[128,128]{1,0:T(8,128)S(1)}, u32[]{:S(2)}) copy-start(f32[128,128]{1,0:T(8,128)S(1)} %get-tuple-element.60.mode_y) | copy-start | bytes 196612
  10.3 17.8 %copy-start.22 = (f32[128,128]{1,0:T(8,128)}, f32[128,128]{1,0:T(8,128)S(1)}, u32[]{:S(2)}) copy-start(f32[128,128]{1,0:T(8,128)S(1)} %get-tuple-element.61.mode_yt) | copy-start | bytes 196612
  10.3 17.8 %copy-start.24 = (f32[128,128]{1,0:T(8,128)}, f32[128,128]{1,0:T(8,128)S(1)}, u32[]{:S(2)}) copy-start(f32[128,128]{1,0:T(8,128)S(1)} %get-tuple-element.62.ceig) | copy-start | bytes 196612
  10.3 17.8 %copy-start.26 = (bf16[128,192]{1,0:T(8,128)(2,1)}, bf16[128,192]{1,0:T(8,128)(2,1)S(1)}, u32[]{:S(2)}) copy-start(bf16[128,192]{1,0:T(8,128)(2,1)S(1)} %get-tuple-element.59.wfin) | copy-start | bytes 147460
  10.3 17.8 %copy-start.30 = (f32[4,256]{1,0:T(4,128)}, f32[4,256]{1,0:T(4,128)S(1)}, u32[]{:S(2)}) copy-start(f32[4,256]{1,0:T(4,128)S(1)} %get-tuple-element.46.czf) | copy-start | bytes 12292
  11.9 23.0 %collective-permute-start.2 = (bf16[544,256]{1,0:T(8,128)(2,1)}, bf16[544,256]{1,0:T(8,128)(2,1)S(1)}, u32[]{:S(2)}, u32[]{:S(2)}) collective-permute-start(bf16[544,256]{1,0:T(8,128)(2,1)} %get-tuple-element.47), channel_id=1, source_target_pairs={{0,1},{1,2},{2,3},{3,4},{4,5},{5,6},{6,7},{7,8},{8,9},{9,10},{10,1... | collective-permute-start | bytes 835592 | tf_op jit(solution)/shard_map/ppermute | solution.py:465
  13.5 21.4 %collective-permute-start.3 = (bf16[544,256]{1,0:T(8,128)(2,1)S(1)}, bf16[544,256]{1,0:T(8,128)(2,1)S(1)}, u32[]{:S(2)}, u32[]{:S(2)}) collective-permute-start(bf16[544,256]{1,0:T(8,128)(2,1)S(1)} %get-tuple-element.48), channel_id=1, source_target_pairs={{0,31},{1,0},{2,1},{3,2},{4,3},{5,4},{6,5},{7,6},{8,7},{9,8},{10,9... | collective-permute-start | bytes 835592 | tf_op jit(solution)/shard_map/ppermute | solution.py:465
  29.0 28.3 %all-to-all-start.1 = ((f32[32,4,128]{2,1,0:T(4,128)}), f32[32,4,128]{2,1,0:T(4,128)S(1)}, u32[]{:S(2)}, u32[]{:S(2)}) async-start(f32[32,4,128]{2,1,0:T(4,128)} %coarse_x.1.after), calls=%async_computation.1 | async-start | bytes 131072 | tf_op jit(solution)/shard_map/all_to_all | solution.py:469
  34.9 0.9 %copy-start.4 = (f32[136,256]{1,0:T(8,128)S(1)}, f32[136,256]{1,0:T(8,128)}, u32[]{:S(2)}) copy-start(f32[136,256]{1,0:T(8,128)} %copy-done.3) | copy-start | bytes 417796
  35.9 0.9 %copy-start.6 = (bf16[256,256]{1,0:T(8,128)(2,1)S(1)}, bf16[256,256]{1,0:T(8,128)(2,1)}, u32[]{:S(2)}) copy-start(bf16[256,256]{1,0:T(8,128)(2,1)} %copy-done.5) | copy-start | bytes 393220
  36.8 0.9 %copy-start.8 = (bf16[256,256]{1,0:T(8,128)(2,1)S(1)}, bf16[256,256]{1,0:T(8,128)(2,1)}, u32[]{:S(2)}) copy-start(bf16[256,256]{1,0:T(8,128)(2,1)} %copy-done.7) | copy-start | bytes 393220
  37.7 0.9 %copy-start.13 = (bf16[160,160]{1,0:T(8,128)(2,1)S(1)}, bf16[160,160]{1,0:T(8,128)(2,1)}, u32[]{:S(2)}) copy-start(bf16[160,160]{1,0:T(8,128)(2,1)} %copy-done.12) | copy-start | bytes 153604
  38.5 0.9 %copy-start.15 = (bf16[136,136]{1,0:T(8,128)(2,1)S(1)}, bf16[136,136]{1,0:T(8,128)(2,1)}, u32[]{:S(2)}) copy-start(bf16[136,136]{1,0:T(8,128)(2,1)} %copy-done.14) | copy-start | bytes 110980
  39.4 0.9 %copy-start.17 = (bf16[136,136]{1,0:T(8,128)(2,1)S(1)}, bf16[136,136]{1,0:T(8,128)(2,1)}, u32[]{:S(2)}) copy-start(bf16[136,136]{1,0:T(8,128)(2,1)} %copy-done.16) | copy-start | bytes 110980
  40.3 0.8 copy-start.29
  53.1 2.4 %copy-start = (f32[2,5440,128]{2,1,0:T(8,128)}, f32[2,5440,128]{2,1,0:T(8,128)S(1)}, u32[]{:S(2)}) copy-start(f32[2,5440,128]{2,1,0:T(8,128)S(1)} %get-tuple-element.58.field) | copy-start | bytes 16711684
  55.6 6.9 %collective-permute-start.4 = (bf16[160,256]{1,0:T(8,128)(2,1)}, bf16[160,256]{1,0:T(8,128)(2,1)S(1)}, u32[]{:S(2)}, u32[]{:S(2)}) collective-permute-start(bf16[160,256]{1,0:T(8,128)(2,1)} %get-tuple-element.66), channel_id=1, source_target_pairs={{0,32},{32,64},{64,96},{96,128},{128,160},{160,192},{192,224},{224... | collective-permute-start | bytes 245768 | tf_op jit(solution)/shard_map/ppermute | solution.py:465
  55.6 6.9 %collective-permute-start.5 = (bf16[160,256]{1,0:T(8,128)(2,1)}, bf16[160,256]{1,0:T(8,128)(2,1)S(1)}, u32[]{:S(2)}, u32[]{:S(2)}) collective-permute-start(bf16[160,256]{1,0:T(8,128)(2,1)} %get-tuple-element.67), channel_id=1, source_target_pairs={{0,224},{32,0},{64,32},{96,64},{128,96},{160,128},{192,160},{224,1... | collective-permute-start | bytes 245768 | tf_op jit(solution)/shard_map/ppermute | solution.py:465
  57.3 0.9 %copy-start.10 = (bf16[512,32]{1,0:T(8,128)(2,1)S(1)}, bf16[512,32]{1,0:T(8,128)(2,1)}, u32[]{:S(2)}) copy-start(bf16[512,32]{1,0:T(8,128)(2,1)} %copy-done.9) | copy-start | bytes 98308
  58.2 0.8 %copy-start.21 = (f32[128,128]{1,0:T(8,128)S(1)}, f32[128,128]{1,0:T(8,128)}, u32[]{:S(2)}) copy-start(f32[128,128]{1,0:T(8,128)} %copy-done.20) | copy-start | bytes 196612
  59.0 0.8 %copy-start.23 = (f32[128,128]{1,0:T(8,128)S(1)}, f32[128,128]{1,0:T(8,128)}, u32[]{:S(2)}) copy-start(f32[128,128]{1,0:T(8,128)} %copy-done.22) | copy-start | bytes 196612
  59.9 0.8 %copy-start.25 = (f32[128,128]{1,0:T(8,128)S(1)}, f32[128,128]{1,0:T(8,128)}, u32[]{:S(2)}) copy-start(f32[128,128]{1,0:T(8,128)} %copy-done.24) | copy-start | bytes 196612
  62.6 11.5 %collective-permute-start.7 = (bf16[512,256]{1,0:T(8,128)(2,1)S(1)}, bf16[512,256]{1,0:T(8,128)(2,1)S(1)}, u32[]{:S(2)}, u32[]{:S(2)}) collective-permute-start(bf16[512,256]{1,0:T(8,128)(2,1)S(1)} %get-tuple-element.70), channel_id=1, source_target_pairs={{0,31},{1,0},{2,1},{3,2},{4,3},{5,4},{6,5},{7,6},{8,7},{9,8},{10,9... | collective-permute-start | bytes 786440 | tf_op jit(solution)/shard_map/ppermute | solution.py:465
  67.8 11.8 %collective-permute-start.6 = (bf16[512,256]{1,0:T(8,128)(2,1)S(1)}, bf16[512,256]{1,0:T(8,128)(2,1)S(1)}, u32[]{:S(2)}, u32[]{:S(2)}) collective-permute-start(bf16[512,256]{1,0:T(8,128)(2,1)S(1)} %get-tuple-element.68.after), channel_id=1, source_target_pairs={{0,1},{1,2},{2,3},{3,4},{4,5},{5,6},{6,7},{7,8},{8,9},{9,10},{10,1... | collective-permute-start | bytes 786440 | tf_op jit(solution)/shard_map/ppermute | solution.py:465
  67.8 2.6 %copy-start.1 = (f32[2,5440,128]{2,1,0:T(8,128)S(1)}, f32[2,5440,128]{2,1,0:T(8,128)}, u32[]{:S(2)}) copy-start(f32[2,5440,128]{2,1,0:T(8,128)} %copy-done) | copy-start | bytes 16711684
  70.4 0.8 %copy-start.27 = (bf16[128,192]{1,0:T(8,128)(2,1)S(1)}, bf16[128,192]{1,0:T(8,128)(2,1)}, u32[]{:S(2)}) copy-start(bf16[128,192]{1,0:T(8,128)(2,1)} %copy-done.26) | copy-start | bytes 147460
  (5 other events, 3.3 us)

commit v4 on v3

--- a/solution.py
+++ b/solution.py
@@ -4,6 +4,7 @@
 from jax.experimental import pallas as pl
 from jax.experimental.pallas import tpu as pltpu
 from jax.sharding import PartitionSpec as P
+
 
 OV = 4
 MODES = 4
@@ -60,7 +61,7 @@
     return jnp.where(mask, 1.0, 0.0).astype(kind)
 
 
-def call(kernel, name, out_shape, in_specs, mib, out_specs=None, scratch=()):
+def call(kernel, out_shape, in_specs, mib, out_specs=None, scratch=()):
     if out_specs is None:
         out_specs = jax.tree.map(lambda _: VM, out_shape)
     return pl.pallas_call(
@@ -70,7 +71,6 @@
         out_specs=out_specs,
         scratch_shapes=list(scratch),
         compiler_params=pltpu.CompilerParams(vmem_limit_bytes=mib << 20),
-        name=name,
     )
 
 
@@ -127,7 +127,6 @@
     rim = sds((CX * OV, NZ), bf16)
     return call(
         load_kernel,
-        "load",
         (
             sds((CELLS, NZ), bf16), sds((OWN, NZ), bf16), sds((OWN, NZ), bf16), rim, rim,
             sds((CX * MODES, NZ), f32), sds((3 * RIM, OWN), bf16),
@@ -153,28 +152,39 @@
 
 def corners(*args):
     side = sds((EX * OV, NZ), bf16)
-    return call(corners_kernel, "corners", (side, side), [VM] * 5 + [ANY], 8)(*args)
+    return call(corners_kernel, (side, side), [VM] * 5 + [ANY], 8)(*args)
 
 
 PARAMS = (
     ((EX, EX), bf16), ((EY, EY), bf16), ((NZ, NZ), bf16), ((1, EX), f32), ((1, EY), f32),
-    ((1, NZ), f32), ((MODES, CX), bf16), ((MODES, CY), bf16), ((MODES, NZ), bf16),
-    ((32, 32), f32), ((128, 128), f32), ((MODES, MODES), f32), ((1, 32), f32), ((1, 128), f32),
-    ((1, MODES), f32),
+    ((1, NZ), f32), ((MODES, CY), bf16),
 )
 WEIGHTS = (
     ((ROWS, ROWS), bf16), ((ROWS, ROWS), bf16), ((OWN, ROWS + 2 * RIM), bf16),
     ((OWN, 2 * RIM), bf16), ((EX, EX), bf16), ((EX, EX), bf16), ((NZ, NZ), bf16),
-    ((NZ, NZ), bf16), ((EX, NZ), f32), ((EY, NZ), f32), ((16, CX * MODES), bf16),
-    ((CX * MODES, 32), bf16), ((MODES, NZ), f32), ((128, 128), f32), ((128, 128), f32),
-    ((128, 128), f32), ((128, 128), f32),
+    ((NZ, NZ), bf16), ((EX, NZ), f32), ((EY, NZ), f32),
 )
+
+
+def basis_x(cxt):
+    x, row = iotas((CX, CX * MODES))
+    by_row = dot(cxt, pick((row >> 2) == x)).astype(bf16)
+    col, m = iotas((16, MODES))
+    value = dot(pick((col >> 2) == m), by_row)
+    col, row = iotas((16, CX * MODES))
+    return jnp.where((row & 3) == (col & 3), value, 0.0).astype(bf16)
+
+
+def modes_a():
+    a, col = iotas((32, 128))
+    c, col4 = iotas((MODES, 128))
+    return pick((col >> 2) == a, f32), pick((col4 & 3) == c, f32)
 
 
 def prepare_kernel(*refs):
     n = len(PARAMS)
     sources, outs, bufs, sems = (
-        refs[:n], refs[n : n + len(WEIGHTS)], refs[n + len(WEIGHTS) : -1], refs[-1]
+        refs[:n], refs[n + 1 : n + 1 + len(WEIGHTS)], refs[n + 1 + len(WEIGHTS) : -1], refs[-1]
     )
     copies = [
         pltpu.make_async_copy(source, buf, sems.at[i])
@@ -184,14 +194,8 @@
         copy.start()
     for copy in copies:
         copy.wait()
-    (
-        lx, ly, lz, eig_x, eig_y, eig_z, cxt, cyt, czt, mode_x, mode_y, mode_z,
-        ceig_x, ceig_y, ceig_z,
-    ) = bufs
-    (
-        wy, wyt, wfin, spread, wx, wxt, lz_out, lzt, exb, eyz, bx, bxt, czf, modes_xz,
-        mode_y_out, mode_yt, ceig,
-    ) = outs
+    lx, ly, lz, eig_x, eig_y, eig_z, cyt = bufs
+    wy, wyt, wfin, spread, wx, wxt, lz_out, lzt, exb, eyz = outs
 
     def cell(k):
         y = jnp.where(k < OWN, OV + (k & 31), jnp.where(k < OWN + RIM, k & 3, EY - OV + (k & 3)))
@@ -240,44 +244,13 @@
     c, z = iotas((NZ, NZ))
     lz_out[...] = lz[...]
     lzt[...] = dot_t(pick(c == z), lz[...]).astype(bf16)
-    czf[...] = czt[...].astype(f32)
-
-    x, row = iotas((CX, CX * MODES))
-    by_row = dot(cxt[...], pick((row >> 2) == x)).astype(bf16)
-    col, m = iotas((16, MODES))
-    value = dot(pick((col >> 2) == m), by_row)
-    col, row = iotas((16, CX * MODES))
-    flat = jnp.where((row & 3) == (col & 3), value, 0.0).astype(bf16)
-    bx[...] = flat
-    col, i = iotas((32, 16))
-    twice = dot(pick((col & 15) == i), flat)
-    bxt[...] = twice.T.astype(bf16)
-
-    r, i = iotas((128, 32))
-    a, col = iotas((32, 128))
-    to_a = pick((col >> 2) == a, f32)
-    part_x = dot_hi(dot_hi(pick((r >> 2) == i, f32), mode_x[...]), to_a)
-    r, p = iotas((128, MODES))
-    c, col = iotas((MODES, 128))
-    to_c = pick((col & 3) == c, f32)
-    part_z = dot_hi(dot_hi(pick((r & 3) == p, f32), mode_z[...]), to_c)
-    modes_xz[...] = part_x * part_z
-    mode_y_out[...] = mode_y[...]
-    mode_yt[...] = mode_y[...].T
-    eight_x = jnp.broadcast_to(ceig_x[...], (8, 32))
-    eight_z = jnp.broadcast_to(ceig_z[...], (8, MODES))
-    row = (dot_hi(eight_x, to_a) + dot_hi(eight_z, to_c))[:1]
-    r, b = iotas((128, 128))
-    column = jnp.sum(jnp.where(r == b, ceig_y[...], 0.0), axis=1, keepdims=True)
-    ceig[...] = column + row
 
 
 def prepare(*params):
     return call(
         prepare_kernel,
-        "prepare",
         tuple(sds(*w) for w in WEIGHTS),
-        [HBM] * len(PARAMS),
+        [HBM] * len(PARAMS) + [ANY],
         8,
         scratch=[pltpu.VMEM(*p) for p in PARAMS] + [pltpu.SemaphoreType.DMA((len(PARAMS),))],
     )(*params)
@@ -285,7 +258,7 @@
 
 def solve_kernel(
     own, xlo, xhi, ylo, yhi, wy, wyt, wx, wxt, lz, lzt, exb, eyz, after,
-    field, out_xlo, out_xhi, out_ylo, out_yhi, mid,
+    kept, out_xlo, out_xhi, out_ylo, out_yhi, field, mid, buf, sems,
 ):
     def put(rows, value):
         field[0, rows, :] = value[:, :128]
@@ -338,16 +311,30 @@
     def planes(k):
         return take(pl.ds(pl.multiple_of(k * ROWS, ROWS), ROWS)).astype(bf16)
 
-    def last(k, carry):
-        out = dot(wyt[OWN:, :], planes(k)).astype(bf16)
-        at = pl.ds(pl.multiple_of(k * RIM, RIM), RIM)
-        out_ylo[at, :] = out[:RIM]
-        out_yhi[at, :] = out[RIM:]
-        return carry
-
     out_xlo[...] = dot(wyt[...], planes(BLOCKS)).astype(bf16)
     out_xhi[...] = dot(wyt[...], planes(BLOCKS + 1)).astype(bf16)
-    lax.fori_loop(0, BLOCKS, last, 0, unroll=4)
+    rows = BLOCKS * ROWS // CHUNKS
+    per = BLOCKS // CHUNKS
+
+    def copy(c):
+        at = pl.ds(pl.multiple_of(c * rows, rows), rows)
+        return pltpu.make_async_copy(buf.at[at, :], kept.at[at, :], sems.at[c])
+
+    def last(c, carry):
+        for b in range(per):
+            k = c * per + b
+            data = planes(k)
+            buf[pl.ds(pl.multiple_of(k * ROWS, ROWS), ROWS), :] = data
+            out = dot(wyt[OWN:, :], data).astype(bf16)
+            at = pl.ds(pl.multiple_of(k * RIM, RIM), RIM)
+            out_ylo[at, :] = out[:RIM]
+            out_yhi[at, :] = out[RIM:]
+        copy(c).start()
+        return carry
+
+    lax.fori_loop(0, CHUNKS, last, 0)
+    for c in range(CHUNKS):
+        copy(c).wait()
 
 
 def solve(*args):
@@ -355,11 +342,14 @@
     rim = sds((CX * OV, NZ), bf16)
     return call(
         solve_kernel,
-        "solve",
-        (sds((2, EX * EY, NZ // 2), f32), strip, strip, rim, rim),
+        (sds((BLOCKS * ROWS, NZ), bf16), strip, strip, rim, rim),
         [VM] * 13 + [ANY],
-        16,
-        scratch=[pltpu.VMEM((EX * EY, NZ), f32)],
+        24,
+        out_specs=(ANY, VM, VM, VM, VM),
+        scratch=[
+            pltpu.VMEM((2, EX * EY, NZ // 2), f32), pltpu.VMEM((EX * EY, NZ), f32),
+            pltpu.VMEM((BLOCKS * ROWS, NZ), bf16), pltpu.SemaphoreType.DMA((CHUNKS,)),
+        ],
     )(*args)
 
 
@@ -376,16 +366,23 @@
 
 def fold(*args):
     rim = sds((CX * OV, NZ), bf16)
-    return call(fold_kernel, "fold", (rim, rim), [VM] * 4 + [ANY], 8)(*args)
-
-
-def restrict_kernel(along_y, bx, czf, out):
+    return call(fold_kernel, (rim, rim), [VM] * 4 + [ANY], 8)(*args)
+
+
+def restrict_kernel(along_y, cxt, czt, mode_x, mode_z, out, modes_xz):
+    bx = basis_x(cxt[...])
     high, low = split(along_y[...])
-    both = dot(bx[...], high) + dot(bx[...], low)
-    own = dot_t_hi(both, czf[...])
+    both = dot(bx, high) + dot(bx, low)
+    own = dot_t_hi(both, czt[...].astype(f32))
     flat = jnp.concatenate([own[m * MODES : (m + 1) * MODES] for m in range(MODES)], 1)
     for i in range(out.shape[0]):
         out[i] = flat
+    to_a, to_c = modes_a()
+    r, i = iotas((128, 32))
+    part_x = dot_hi(dot_hi(pick((r >> 2) == i, f32), mode_x[...]), to_a)
+    r, p = iotas((128, MODES))
+    part_z = dot_hi(dot_hi(pick((r & 3) == p, f32), mode_z[...]), to_c)
+    modes_xz[...] = part_x * part_z
 
 
 def coarse_x_kernel(rows, modes_xz, out):
@@ -394,19 +391,28 @@
         out[i] = part
 
 
-def coarse_kernel(rows, modes_xz, mode_y, mode_yt, ceig, czf, bxt, out):
+def coarse_kernel(rows, modes_xz, mode_y, ceig_x, ceig_y, ceig_z, cxt, czt, out):
+    to_a, to_c = modes_a()
+    eight_x = jnp.broadcast_to(ceig_x[...], (8, 32))
+    eight_z = jnp.broadcast_to(ceig_z[...], (8, MODES))
+    row = (dot_hi(eight_x, to_a) + dot_hi(eight_z, to_c))[:1]
+    r, b = iotas((128, 128))
+    column = jnp.sum(jnp.where(r == b, ceig_y[...], 0.0), axis=1, keepdims=True)
     columns = jnp.concatenate([rows[j] for j in range(rows.shape[0])], 0)
-    hat = dot_hi(mode_yt[...], columns) / ceig[...]
+    hat = dot_hi(mode_y[...].T, columns) / (column + row)
     row, col = iotas((8, 128))
     mine = pick(col == lax.axis_index("gy") * MODES + row, f32)
     rows_y = dot_hi(mine, mode_y[...])
     rows_xz = modes_xz[pl.ds(pl.multiple_of(lax.axis_index("gx") * 16, 16), 16), :]
     sol = dot_t_hi(dot_hi(rows_y, hat), rows_xz)
+    levels = czt[...].astype(f32)
     shape = jnp.concatenate(
-        [dot_hi(sol[:, m * MODES : (m + 1) * MODES], czf[...])[:MODES] for m in range(MODES)], 0
+        [dot_hi(sol[:, m * MODES : (m + 1) * MODES], levels)[:MODES] for m in range(MODES)], 0
     )
     high, low = split(shape)
-    value = dot(bxt[...], jnp.concatenate([high, low], 0))
+    col, i = iotas((32, 16))
+    twice = dot(pick((col & 15) == i), basis_x(cxt[...]))
+    value = dot(twice.T.astype(bf16), jnp.concatenate([high, low], 0))
     high, low = split(value)
     for k in range(BLOCKS):
         at = slice(k * RIM, (k + 1) * RIM)
@@ -414,15 +420,26 @@
         out[(2 * k + 1) * RIM : (2 * k + 2) * RIM, :] = low[at]
 
 
-def finish_kernel(field, wfin, shape, after, fix):
-    def step(k, carry):
-        at = pl.ds(pl.multiple_of(k * ROWS, ROWS), ROWS)
-        planes = jnp.concatenate([field[0, at, :], field[1, at, :]], 1).astype(bf16)
-        data = jnp.concatenate([planes, tile(shape, k, 2 * RIM)], 0)
-        fix[pl.ds(pl.multiple_of(k * OWN, OWN), OWN), :] = dot(wfin[...], data)
+def finish_kernel(field, wfin, shape, after, fix, buf, sems):
+    rows = BLOCKS * ROWS // CHUNKS
+    per = BLOCKS // CHUNKS
+
+    def copy(c):
+        at = pl.ds(pl.multiple_of(c * rows, rows), rows)
+        return pltpu.make_async_copy(field.at[at, :], buf.at[at, :], sems.at[c])
+
+    for c in range(CHUNKS):
+        copy(c).start()
+
+    def step(c, carry):
+        copy(c).wait()
+        for b in range(per):
+            k = c * per + b
+            data = jnp.concatenate([tile(buf, k, ROWS), tile(shape, k, 2 * RIM)], 0)
+            fix[pl.ds(pl.multiple_of(k * OWN, OWN), OWN), :] = dot(wfin[...], data)
         return carry
 
-    lax.fori_loop(0, BLOCKS, step, 0, unroll=4)
+    lax.fori_loop(0, CHUNKS, step, 0)
 
 
 def combine_kernel(fix, spread, rxlo, rxhi, rylo, ryhi, out, buf, sems):
@@ -451,7 +468,6 @@
 def combine(*args):
     return call(
         combine_kernel,
-        "combine",
         sds((CELLS, NZ), f32),
         [VM] * 6,
         16,
@@ -478,40 +494,35 @@
     )
     xlo = shift(last_x, "gx", 1)
     xhi = shift(first_x, "gx", -1)
-    (
-        wy, wyt, wfin, spread, wx, wxt, lz, lzt, exb, eyz, bx, bxt, czf, modes_xz,
-        mode_y, mode_yt, ceig,
-    ) = prepare(
-        local_x, local_y, local_z, eig_x[None], eig_y[None], eig_z[None], coarse_x.T, coarse_y.T,
-        coarse_z.T, mode_x, mode_y, mode_z, coarse_eig_x[None], coarse_eig_y[None],
-        coarse_eig_z[None],
-    )
-    own_coarse = call(
-        restrict_kernel, "restrict", sds((8, MODES, 16), f32), [VM] * 3, 8
-    )(along_y, bx, czf)
+    own_coarse, modes_xz = call(
+        restrict_kernel, (sds((8, MODES, 16), f32), sds((128, 128), f32)), [VM] * 5, 8
+    )(along_y, coarse_x.T, coarse_z.T, mode_x, mode_z)
     rows = exchange(own_coarse, "gx")
     down, up = corners(sel, rim_lo, rim_hi, xlo, xhi, own_coarse)
     ylo = shift(up, "gy", 1)
     yhi = shift(down, "gy", -1)
-    part = call(coarse_x_kernel, "coarse_x", sds((32, MODES, 128), f32), [VM] * 2, 4)(
-        rows, modes_xz
-    )
+    part = call(coarse_x_kernel, sds((32, MODES, 128), f32), [VM] * 2, 4)(rows, modes_xz)
     rows = exchange(part, "gy")
 
+    wy, wyt, wfin, spread, wx, wxt, lz, lzt, exb, eyz = prepare(
+        local_x, local_y, local_z, eig_x[None], eig_y[None], eig_z[None], coarse_y.T, part
+    )
     field, out_xlo, out_xhi, out_ylo, out_yhi = solve(
         own, xlo, xhi, ylo, yhi, wy, wyt, wx, wxt, lz, lzt, exb, eyz, part
     )
 
     rxlo = shift(out_xhi, "gx", 1)
     rxhi = shift(out_xlo, "gx", -1)
-    shape = call(
-        coarse_kernel, "coarse", sds((2 * CX * MODES, NZ), bf16), [VM] * 7, 8
-    )(rows, modes_xz, mode_y, mode_yt, ceig, czf, bxt)
+    shape = call(coarse_kernel, sds((2 * CX * MODES, NZ), bf16), [VM] * 8, 8)(
+        rows, modes_xz, mode_y, coarse_eig_x[None], coarse_eig_y[None], coarse_eig_z[None],
+        coarse_x.T, coarse_z.T,
+    )
     down, up = fold(out_ylo, out_yhi, rxlo, rxhi, shape)
     rylo = shift(up, "gy", 1)
     ryhi = shift(down, "gy", -1)
     fix = call(
-        finish_kernel, "finish", sds((CELLS, NZ), f32), [VM] * 3 + [ANY], 16
+        finish_kernel, sds((CELLS, NZ), f32), [ANY] + [VM] * 2 + [ANY], 16,
+        scratch=[pltpu.VMEM((BLOCKS * ROWS, NZ), bf16), pltpu.SemaphoreType.DMA((CHUNKS,))],
     )(field, wfin, shape, up)
     out = combine(fix, spread, rxlo, rxhi, rylo, ryhi)
     return out.reshape(CX, CY, NZ)
@@ -519,6 +530,7 @@
 
 def solution(mesh):
     placed = (P("gx", "gy", None),) + (P(),) * 15
+
     return jax.shard_map(
         local, mesh=mesh, in_specs=placed, out_specs=P("gx", "gy", None), check_vma=False
     )

time: 82.6 us -> 77.8 us (0.942)
  the two profiles are of different devices: /device:TPU:6 before, /device:TPU:1 now
where the time goes in v4:
time: 77.8 us; the launch traced here: 77.1 us
  Pallas kernels  24.5 us (31%)
  starting transfers between devices  22.8 us (29%)
  local copies, waits for them, and re-layouts  10.6 us (14%)
  waiting for transfers between devices  10.1 us (13%)
  blocking collectives  8.78 us (11%)
    ppermute x8, starting transfers between devices, shift(): return lax.ppermute(x, axis, [(i, (i + step) % size) for i in range(size)])  17.5 us
    pallas_call x1, Pallas kernels, solve(): call(solve_kernel, (sds((BLOCKS * ROWS, NZ), bf16), strip, strip, rim, ri...  13 us
    unnamed x46, local copies, waits for them, and re-layouts  10.6 us
    ppermute x8, waiting for transfers between devices, shift(): return lax.ppermute(x, axis, [(i, (i + step) % size) for i in range(size)])  10.1 us
    all_to_all x1, blocking collectives, exchange(): return lax.all_to_all(x, axis, 0, 0)  8.78 us
    all_to_all x1, starting transfers between devices, exchange(): return lax.all_to_all(x, axis, 0, 0)  5.25 us
    pallas_call x1, Pallas kernels, local(): call(finish_kernel, sds((CELLS, NZ), f32), [ANY] + [VM] * 2 + [ANY], 16,...  2.77 us
    pallas_call x1, Pallas kernels, combine(): call(combine_kernel, sds((CELLS, NZ), f32), [VM] * 6, 16, out_specs=HBM,...  2.27 us
  transfers between devices with their start and end apart: 9, of which 4 were waited for; matrix products, arithmetic and copies ran while one was open for 0% of the time, Pallas kernels for 26%

profile of v4, /device:TPU:1, one launch (start us, length us, event | category | flops | bytes accessed | tf_op | source)
XLA Modules:
  0.0 77.1 jit_solution(8761353652974853022)
XLA Ops:
  0.0 0.0 copy-start
  0.0 2.2 %copy-done = f32[128,32,256]{2,1,0:T(8,128)S(1)} copy-done((f32[128,32,256]{2,1,0:T(8,128)S(1)}, f32[128,32,256]{2,1,0:T(8,128)}, u32[]{:S(2)}) %copy-start) | copy-done | bytes 4194328
  2.2 0.7 copy-done.13
  2.9 0.0 copy-start.8
  2.9 0.0 copy-start.11
  3.0 2.0 %shard_map.154 = (bf16[4096,256]{1,0:T(8,128)(2,1)S(1)}, bf16[128,256]{1,0:T(8,128)(2,1)S(1)}, bf16[128,256]{1,0:T(8,128)(2,1)S(1)}, bf16[512,256]{1,0:T(8,128)(...) custom-call(f32[4096,256]{1,0:T(8,128)S(1)} %bitcast.11, ...), custom_call_target="tpu_custom_call" | custom-call | tf_op jit(solution)/shard_map/pallas_call | solution.py:128
  5.0 0.0 copy-start.1
  5.0 1.3 %copy-done.1 = bf16[4096,256]{1,0:T(8,128)(2,1)} copy-done((bf16[4096,256]{1,0:T(8,128)(2,1)}, bf16[4096,256]{1,0:T(8,128)(2,1)S(1)}, u32[]{:S(2)}) %copy-start.1) | copy-done | bytes 2097176
  6.3 2.6 %collective-permute-start = (bf16[128,256]{1,0:T(8,128)(2,1)S(1)}, bf16[128,256]{1,0:T(8,128)(2,1)S(1)}, u32[]{:S(2)}, u32[]{:S(2)}) collective-permute-start(bf16[128,256]{1,0:T(8,128)(2,1)S(1)} %get-tuple-element.34), channel_id=1, source_target_pairs={{0,32},{32,64},{64,96},{96,128},{128,160},{160,192},{192,224},{224... | collective-permute-start | bytes 196616 | tf_op jit(solution)/shard_map/ppermute | solution.py:481
  8.9 0.6 collective-permute-start.1
  9.5 0.0 copy-done.12
  9.5 1.0 %shard_map.155 = (f32[8,4,16]{2,1,0:T(4,128)S(1)}, f32[128,128]{1,0:T(8,128)S(1)}) custom-call(f32[512,256]{1,0:T(8,128)S(1)} %get-tuple-element.39.along_y, bf16[4,128]{1,0:T(4,128)(2,1)S(1)} %bitcast.16, bf16[4,256]{1,0:T(4,128)(2,1)S(1)} %bitcast.12, f32[32,32]{1,0:T(8,128)S(1)} %copy-done.10, f32[4,4]{1,0:T(4,128)S(1)} %copy-done.16), custom_call_target="tpu_custom_call" | custom-call | tf_op jit(solution)/shard_map/pallas_call | solution.py:497
  10.6 0.0 collective-permute-done.xlo
  10.6 2.0 %collective-permute-done.1.xhi = bf16[128,256]{1,0:T(8,128)(2,1)S(1)} collective-permute-done((bf16[128,256]{1,0:T(8,128)(2,1)S(1)}, bf16[128,256]{1,0:T(8,128)(2,1)S(1)}, u32[]{:S(2)}, u32[]{:S(2)}) %collective-permute-start.1) | collective-permute-done | bytes 65568 | tf_op jit(solution)/shard_map/ppermute | solution.py:481
  12.6 0.1 shard_map.156
  12.7 1.3 %collective-permute-start.2 = (bf16[544,256]{1,0:T(8,128)(2,1)S(1)}, bf16[544,256]{1,0:T(8,128)(2,1)S(1)}, u32[]{:S(2)}, u32[]{:S(2)}) collective-permute-start(bf16[544,256]{1,0:T(8,128)(2,1)S(1)} %get-tuple-element.41), channel_id=1, source_target_pairs={{0,1},{1,2},{2,3},{3,4},{4,5},{5,6},{6,7},{7,8},{8,9},{9,10},{10,1... | collective-permute-start | bytes 835592 | tf_op jit(solution)/shard_map/ppermute | solution.py:481
  14.1 6.8 %collective-permute-start.3 = (bf16[544,256]{1,0:T(8,128)(2,1)S(1)}, bf16[544,256]{1,0:T(8,128)(2,1)S(1)}, u32[]{:S(2)}, u32[]{:S(2)}) collective-permute-start(bf16[544,256]{1,0:T(8,128)(2,1)S(1)} %get-tuple-element.42), channel_id=1, source_target_pairs={{0,31},{1,0},{2,1},{3,2},{4,3},{5,4},{6,5},{7,6},{8,7},{9,8},{10,9... | collective-permute-start | bytes 835592 | tf_op jit(solution)/shard_map/ppermute | solution.py:481
  20.9 8.8 %all_to_all.10.rows = f32[8,4,16]{2,1,0:T(4,128)S(1)} all-to-all(f32[8,4,16]{2,1,0:T(4,128)S(1)} %get-tuple-element.40.after), channel_id=1, replica_groups=mesh['gx'=8,'gy'=32] {'gx'}, dimensions={0} | all-to-all | bytes 4096 | tf_op jit(solution)/shard_map/all_to_all | solution.py:485
  29.7 0.9 %shard_map.157.refs_7_.after = f32[32,4,128]{2,1,0:T(4,128)} custom-call(f32[8,4,16]{2,1,0:T(4,128)S(1)} %all_to_all.10.rows, f32[128,128]{1,0:T(8,128)S(1)} %get-tuple-element.43.modes_xz), custom_call_target="tpu_custom_call" | custom-call | tf_op jit(solution)/shard_map/pallas_call | solution.py:504
  30.5 5.2 %all-to-all-start.1 = ((f32[32,4,128]{2,1,0:T(4,128)}), f32[32,4,128]{2,1,0:T(4,128)S(1)}, u32[]{:S(2)}, u32[]{:S(2)}) async-start(f32[32,4,128]{2,1,0:T(4,128)} %shard_map.157.refs_7_.after), calls=%async_computation.1 | async-start | bytes 131072 | tf_op jit(solution)/shard_map/all_to_all | solution.py:485
  35.9 1.0 %shard_map.158 = (bf16[160,160]{1,0:T(8,128)(2,1)S(1)}, bf16[160,160]{1,0:T(8,128)(2,1)S(1)}, bf16[128,192]{1,0:T(8,128)(2,1)S(1)}, bf16[128,32]{1,0:T(8,128)(2,...) custom-call(bf16[136,136]{1,0:T(8,128)(2,1)S(1)} %copy-done.8, ...), custom_call_target="tpu_custom_call" | custom-call | tf_op jit(solution)/shard_map/pallas_call | solution.py:250
  36.8 0.0 collective-permute-done.2.ylo
  36.8 0.0 collective-permute-done.3.yhi
  36.9 0.0 copy-start.2
  36.9 1.6 %copy-done.2 = bf16[4096,256]{1,0:T(8,128)(2,1)S(1)} copy-done((bf16[4096,256]{1,0:T(8,128)(2,1)S(1)}, bf16[4096,256]{1,0:T(8,128)(2,1)}, u32[]{:S(2)}) %copy-start.2) | copy-done | bytes 2097176
  38.4 13.0 %shard_map.159 = (bf16[5120,256]{1,0:T(8,128)(2,1)S(1)}, bf16[160,256]{1,0:T(8,128)(2,1)}, bf16[160,256]{1,0:T(8,128)(2,1)}, bf16[512,256]{1,0:T(8,128)(2,1)S(1)}, bf16[512,256]{1,0:T(8,128)(2,1)S(1)}) custom-call(bf16[4096,256]{1,0:T(8,128)(2,1)S(1)} %copy-done.2, bf16[128,256]{1,0:T(8,128)(2,1)S(1)} %collective-permute-done.xlo, ...), custom_call_target="tpu_custom_call" | custom-call | tf_op jit(solution)/shard_map/pallas_call | solution.py:343
  51.5 0.0 copy-start.3
  51.5 0.7 copy-done.3
  52.2 0.7 copy-done.5
  52.9 1.2 %collective-permute-start.4 = (bf16[160,256]{1,0:T(8,128)(2,1)}, bf16[160,256]{1,0:T(8,128)(2,1)S(1)}, u32[]{:S(2)}, u32[]{:S(2)}) collective-permute-start(bf16[160,256]{1,0:T(8,128)(2,1)} %get-tuple-element.56), channel_id=1, source_target_pairs={{0,32},{32,64},{64,96},{96,128},{128,160},{160,192},{192,224},{224... | collective-permute-start | bytes 245768 | tf_op jit(solution)/shard_map/ppermute | solution.py:481
  54.0 0.0 collective-permute-start.5
  54.0 0.0 all-to-all-done.1.rows
  54.0 0.0 copy-done.20
  54.0 0.0 copy-done.21
  54.0 0.0 copy-start.9
  54.1 0.8 %copy-done.9 = f32[128,128]{1,0:T(8,128)S(1)} copy-done((f32[128,128]{1,0:T(8,128)S(1)}, f32[128,128]{1,0:T(8,128)}, u32[]{:S(2)}) %copy-start.9) | copy-done | bytes 65560
  54.9 0.7 copy-done.22
  55.5 1.5 %shard_map.160.after.shape = bf16[1024,256]{1,0:T(8,128)(2,1)S(1)} custom-call(f32[32,4,128]{2,1,0:T(4,128)S(1)} %all-to-all-done.1.rows, f32[128,128]{1,0:T(8,128)S(1)} %get-tuple-element.43.modes_xz, f32[128,128]{1,0:T(8,128)S(1)} %copy-done.9, f32[1,32]{1,0:T(1,128)S(1)} %bitcast.21, f32[1,128]{1,0:T(1,128)S(1)} %bitcast.22, f32[1,4]{1,0:T(1,128)S(1)} %bitcast.23, ...), custom_call_target="tpu_custom_call" | custom-call | tf_op jit(solution)/shard_map/pallas_call | solution.py:516
  57.0 0.0 collective-permute-done.4.rxlo
  57.0 1.4 %collective-permute-done.5.rxhi = bf16[160,256]{1,0:T(8,128)(2,1)S(1)} collective-permute-done((bf16[160,256]{1,0:T(8,128)(2,1)}, bf16[160,256]{1,0:T(8,128)(2,1)S(1)}, u32[]{:S(2)}, u32[]{:S(2)}) %collective-permute-start.5) | collective-permute-done | bytes 81952 | tf_op jit(solution)/shard_map/ppermute | solution.py:481
  58.4 0.9 %copy-done.4 = bf16[512,256]{1,0:T(8,128)(2,1)S(1)} copy-done((bf16[512,256]{1,0:T(8,128)(2,1)S(1)}, bf16[512,256]{1,0:T(8,128)(2,1)}, u32[]{:S(2)}) %copy-start.4) | copy-done | bytes 262168
  59.4 0.9 %copy-done.6 = bf16[512,256]{1,0:T(8,128)(2,1)S(1)} copy-done((bf16[512,256]{1,0:T(8,128)(2,1)S(1)}, bf16[512,256]{1,0:T(8,128)(2,1)}, u32[]{:S(2)}) %copy-start.6) | copy-done | bytes 262168
  60.3 5.0 %collective-permute-start.7 = (bf16[512,256]{1,0:T(8,128)(2,1)S(1)}, bf16[512,256]{1,0:T(8,128)(2,1)S(1)}, u32[]{:S(2)}, u32[]{:S(2)}) collective-permute-start(bf16[512,256]{1,0:T(8,128)(2,1)S(1)} %get-tuple-element.60), channel_id=1, source_target_pairs={{0,31},{1,0},{2,1},{3,2},{4,3},{5,4},{6,5},{7,6},{8,7},{9,8},{10,9... | collective-permute-start | bytes 786440 | tf_op jit(solution)/shard_map/ppermute | solution.py:481
  65.3 0.0 collective-permute-start.6
  65.4 2.8 %shard_map.162.fix = f32[4096,256]{1,0:T(8,128)S(1)} custom-call(bf16[5120,256]{1,0:T(8,128)(2,1)S(1)} %get-tuple-element.52.field, bf16[128,192]{1,0:T(8,128)(2,1)S(1)} %get-tuple-element.53.wfin, bf16[1024,256]{1,0:T(8,128)(2,1)S(1)} %shard_map.160.after.shape, bf16[512,256]{1,0:T(8,128)(2,1)S(1)} %get-tuple-element.58.after), custom_call_target="tpu_custom_call" | custom-call | tf_op jit(solution)/shard_map/pallas_call | solution.py:523
  68.1 1.5 %collective-permute-done.7.ryhi = bf16[512,256]{1,0:T(8,128)(2,1)S(1)} collective-permute-done((bf16[512,256]{1,0:T(8,128)(2,1)S(1)}, bf16[512,256]{1,0:T(8,128)(2,1)S(1)}, u32[]{:S(2)}, u32[]{:S(2)}) %collective-permute-start.7) | collective-permute-done | bytes 262176 | tf_op jit(solution)/shard_map/ppermute | solution.py:481
  69.6 5.2 %collective-permute-done.6.rylo = bf16[512,256]{1,0:T(8,128)(2,1)S(1)} collective-permute-done((bf16[512,256]{1,0:T(8,128)(2,1)S(1)}, bf16[512,256]{1,0:T(8,128)(2,1)S(1)}, u32[]{:S(2)}, u32[]{:S(2)}) %collective-permute-start.6) | collective-permute-done | bytes 262176 | tf_op jit(solution)/shard_map/ppermute | solution.py:481
  74.8 2.3 %shard_map.163 = f32[4096,256]{1,0:T(8,128)} custom-call(f32[4096,256]{1,0:T(8,128)S(1)} %shard_map.162.fix, bf16[128,32]{1,0:T(8,128)(2,1)S(1)} %get-tuple-element.59.spread, bf16[160,256]{1,0:T(8,128)(2,1)S(1)} %collective-permute-done.4.rxlo, bf16[160,256]{1,0:T(8,128)(2,1)S(1)} %collective-permute-done.5.rxhi, ...), custom_call_target="tpu_custom_call" | custom-call | tf_op jit(solution)/shard_map/pallas_call | solution.py:469
  (27 shorter events, 0.1 us)
Async XLA Ops:
  0.0 35.8 %copy-start.14 = (bf16[32,4]{0,1:T(4,128)(2,1)S(1)}, bf16[32,4]{0,1:T(4,128)(2,1)}, u32[]{:S(2)}) copy-start(bf16[32,4]{0,1:T(4,128)(2,1)} %param.24) | copy-start | bytes 772
  0.0 9.5 %copy-start.12 = (bf16[256,4]{0,1:T(4,128)(2,1)S(1)}, bf16[256,4]{0,1:T(4,128)(2,1)}, u32[]{:S(2)}) copy-start(bf16[256,4]{0,1:T(4,128)(2,1)} %param.25) | copy-start | bytes 6148
  0.0 35.8 %copy-start.19 = (f32[40]{0:T(128)S(1)}, f32[40]{0:T(128)}, u32[]{:S(2)}) copy-start(f32[40]{0:T(128)} %param.21) | copy-start | bytes 484
  0.0 2.2 %copy-start = (f32[128,32,256]{2,1,0:T(8,128)S(1)}, f32[128,32,256]{2,1,0:T(8,128)}, u32[]{:S(2)}) copy-start(f32[128,32,256]{2,1,0:T(8,128)} %param.16) | copy-start | bytes 12582916
  2.2 0.7 copy-start.13
  2.9 6.6 %copy-start.10 = (f32[32,32]{1,0:T(8,128)S(1)}, f32[32,32]{1,0:T(8,128)}, u32[]{:S(2)}) copy-start(f32[32,32]{1,0:T(8,128)} %mode_x.1) | copy-start | bytes 12292
  2.9 6.6 %copy-start.15 = (bf16[128,4]{0,1:T(4,128)(2,1)S(1)}, bf16[128,4]{0,1:T(4,128)(2,1)}, u32[]{:S(2)}) copy-start(bf16[128,4]{0,1:T(4,128)(2,1)} %param.23) | copy-start | bytes 3076
  2.9 6.6 %copy-start.16 = (f32[4,4]{1,0:T(4,128)S(1)}, f32[4,4]{1,0:T(4,128)}, u32[]{:S(2)}) copy-start(f32[4,4]{1,0:T(4,128)} %mode_z.1) | copy-start | bytes 196
  2.9 32.9 %copy-start.7 = (bf16[256,256]{1,0:T(8,128)(2,1)S(1)}, bf16[256,256]{1,0:T(8,128)(2,1)}, u32[]{:S(2)}) copy-start(bf16[256,256]{1,0:T(8,128)(2,1)} %refs_2_.1) | copy-start | bytes 393220
  2.9 32.9 %copy-start.8 = (bf16[136,136]{1,0:T(8,128)(2,1)S(1)}, bf16[136,136]{1,0:T(8,128)(2,1)}, u32[]{:S(2)}) copy-start(bf16[136,136]{1,0:T(8,128)(2,1)} %refs_0_.1) | copy-start | bytes 110980
  2.9 32.9 %copy-start.11 = (bf16[40,40]{1,0:T(8,128)(2,1)S(1)}, bf16[40,40]{1,0:T(8,128)(2,1)}, u32[]{:S(2)}) copy-start(bf16[40,40]{1,0:T(8,128)(2,1)} %refs_1_.1) | copy-start | bytes 9604
  2.9 32.9 %copy-start.17 = (f32[136]{0:T(256)S(1)}, f32[136]{0:T(256)}, u32[]{:S(2)}) copy-start(f32[136]{0:T(256)} %param.20) | copy-start | bytes 1636
  2.9 32.9 %copy-start.18 = (f32[256]{0:T(256)S(1)}, f32[256]{0:T(256)}, u32[]{:S(2)}) copy-start(f32[256]{0:T(256)} %param.22) | copy-start | bytes 3076
  3.0 51.1 %copy-start.20 = (f32[32]{0:T(128)S(1)}, f32[32]{0:T(128)}, u32[]{:S(2)}) copy-start(f32[32]{0:T(128)} %param.29) | copy-start | bytes 388
  3.0 51.1 %copy-start.21 = (f32[128]{0:T(128)S(1)}, f32[128]{0:T(128)}, u32[]{:S(2)}) copy-start(f32[128]{0:T(128)} %param.30) | copy-start | bytes 1540
  5.0 1.3 %copy-start.1 = (bf16[4096,256]{1,0:T(8,128)(2,1)}, bf16[4096,256]{1,0:T(8,128)(2,1)S(1)}, u32[]{:S(2)}) copy-start(bf16[4096,256]{1,0:T(8,128)(2,1)S(1)} %get-tuple-element.33.own) | copy-start | bytes 6291460
  6.3 4.2 %collective-permute-start = (bf16[128,256]{1,0:T(8,128)(2,1)S(1)}, bf16[128,256]{1,0:T(8,128)(2,1)S(1)}, u32[]{:S(2)}, u32[]{:S(2)}) collective-permute-start(bf16[128,256]{1,0:T(8,128)(2,1)S(1)} %get-tuple-element.34), channel_id=1, source_target_pairs={{0,32},{32,64},{64,96},{96,128},{128,160},{160,192},{192,224},{224... | collective-permute-start | bytes 196616 | tf_op jit(solution)/shard_map/ppermute | solution.py:481
  8.9 3.7 %collective-permute-start.1 = (bf16[128,256]{1,0:T(8,128)(2,1)S(1)}, bf16[128,256]{1,0:T(8,128)(2,1)S(1)}, u32[]{:S(2)}, u32[]{:S(2)}) collective-permute-start(bf16[128,256]{1,0:T(8,128)(2,1)S(1)} %get-tuple-element.35), channel_id=1, source_target_pairs={{0,224},{32,0},{64,32},{96,64},{128,96},{160,128},{192,160},{224,1... | collective-permute-start | bytes 196616 | tf_op jit(solution)/shard_map/ppermute | solution.py:481
  12.7 24.1 %collective-permute-start.2 = (bf16[544,256]{1,0:T(8,128)(2,1)S(1)}, bf16[544,256]{1,0:T(8,128)(2,1)S(1)}, u32[]{:S(2)}, u32[]{:S(2)}) collective-permute-start(bf16[544,256]{1,0:T(8,128)(2,1)S(1)} %get-tuple-element.41), channel_id=1, source_target_pairs={{0,1},{1,2},{2,3},{3,4},{4,5},{5,6},{6,7},{7,8},{8,9},{9,10},{10,1... | collective-permute-start | bytes 835592 | tf_op jit(solution)/shard_map/ppermute | solution.py:481
  14.1 22.8 %collective-permute-start.3 = (bf16[544,256]{1,0:T(8,128)(2,1)S(1)}, bf16[544,256]{1,0:T(8,128)(2,1)S(1)}, u32[]{:S(2)}, u32[]{:S(2)}) collective-permute-start(bf16[544,256]{1,0:T(8,128)(2,1)S(1)} %get-tuple-element.42), channel_id=1, source_target_pairs={{0,31},{1,0},{2,1},{3,2},{4,3},{5,4},{6,5},{7,6},{8,7},{9,8},{10,9... | collective-permute-start | bytes 835592 | tf_op jit(solution)/shard_map/ppermute | solution.py:481
  30.5 23.5 %all-to-all-start.1 = ((f32[32,4,128]{2,1,0:T(4,128)}), f32[32,4,128]{2,1,0:T(4,128)S(1)}, u32[]{:S(2)}, u32[]{:S(2)}) async-start(f32[32,4,128]{2,1,0:T(4,128)} %shard_map.157.refs_7_.after), calls=%async_computation.1 | async-start | bytes 131072 | tf_op jit(solution)/shard_map/all_to_all | solution.py:485
  36.9 1.6 %copy-start.2 = (bf16[4096,256]{1,0:T(8,128)(2,1)S(1)}, bf16[4096,256]{1,0:T(8,128)(2,1)}, u32[]{:S(2)}) copy-start(bf16[4096,256]{1,0:T(8,128)(2,1)} %copy-done.1) | copy-start | bytes 6291460
  51.5 0.7 copy-start.3
  52.2 0.7 copy-start.5
  52.9 4.1 %collective-permute-start.4 = (bf16[160,256]{1,0:T(8,128)(2,1)}, bf16[160,256]{1,0:T(8,128)(2,1)S(1)}, u32[]{:S(2)}, u32[]{:S(2)}) collective-permute-start(bf16[160,256]{1,0:T(8,128)(2,1)} %get-tuple-element.56), channel_id=1, source_target_pairs={{0,32},{32,64},{64,96},{96,128},{128,160},{160,192},{192,224},{224... | collective-permute-start | bytes 245768 | tf_op jit(solution)/shard_map/ppermute | solution.py:481
  54.0 4.4 %collective-permute-start.5 = (bf16[160,256]{1,0:T(8,128)(2,1)}, bf16[160,256]{1,0:T(8,128)(2,1)S(1)}, u32[]{:S(2)}, u32[]{:S(2)}) collective-permute-start(bf16[160,256]{1,0:T(8,128)(2,1)} %get-tuple-element.57), channel_id=1, source_target_pairs={{0,224},{32,0},{64,32},{96,64},{128,96},{160,128},{192,160},{224,1... | collective-permute-start | bytes 245768 | tf_op jit(solution)/shard_map/ppermute | solution.py:481
  54.0 0.8 %copy-start.9 = (f32[128,128]{1,0:T(8,128)S(1)}, f32[128,128]{1,0:T(8,128)}, u32[]{:S(2)}) copy-start(f32[128,128]{1,0:T(8,128)} %mode_y.1) | copy-start | bytes 196612
  54.9 0.7 copy-start.22
  58.4 1.0 %copy-start.4 = (bf16[512,256]{1,0:T(8,128)(2,1)S(1)}, bf16[512,256]{1,0:T(8,128)(2,1)}, u32[]{:S(2)}) copy-start(bf16[512,256]{1,0:T(8,128)(2,1)} %copy-done.3) | copy-start | bytes 786436
  59.4 0.9 %copy-start.6 = (bf16[512,256]{1,0:T(8,128)(2,1)S(1)}, bf16[512,256]{1,0:T(8,128)(2,1)}, u32[]{:S(2)}) copy-start(bf16[512,256]{1,0:T(8,128)(2,1)} %copy-done.5) | copy-start | bytes 786436
  60.3 9.3 %collective-permute-start.7 = (bf16[512,256]{1,0:T(8,128)(2,1)S(1)}, bf16[512,256]{1,0:T(8,128)(2,1)S(1)}, u32[]{:S(2)}, u32[]{:S(2)}) collective-permute-start(bf16[512,256]{1,0:T(8,128)(2,1)S(1)} %get-tuple-element.60), channel_id=1, source_target_pairs={{0,31},{1,0},{2,1},{3,2},{4,3},{5,4},{6,5},{7,6},{8,7},{9,8},{10,9... | collective-permute-start | bytes 786440 | tf_op jit(solution)/shard_map/ppermute | solution.py:481
  65.3 9.5 %collective-permute-start.6 = (bf16[512,256]{1,0:T(8,128)(2,1)S(1)}, bf16[512,256]{1,0:T(8,128)(2,1)S(1)}, u32[]{:S(2)}, u32[]{:S(2)}) collective-permute-start(bf16[512,256]{1,0:T(8,128)(2,1)S(1)} %get-tuple-element.58.after), channel_id=1, source_target_pairs={{0,1},{1,2},{2,3},{3,4},{4,5},{5,6},{6,7},{7,8},{8,9},{9,10},{10,1... | collective-permute-start | bytes 786440 | tf_op jit(solution)/shard_map/ppermute | solution.py:481

commit v5 on v4

--- a/solution.py
+++ b/solution.py
@@ -3,7 +3,7 @@
 from jax import lax
 from jax.experimental import pallas as pl
 from jax.experimental.pallas import tpu as pltpu
-from jax.sharding import PartitionSpec as P
+from jax.sharding import Mesh, PartitionSpec as P
 
 
 OV = 4
@@ -20,6 +20,8 @@
 BLOCKS = CX // GX
 CELLS = CX * CY
 CHUNKS = 8
+WIDE_LOAD = 50
+WIDE_SOLVE = 48
 HI = lax.Precision.HIGHEST
 f32 = jnp.float32
 bf16 = jnp.bfloat16
@@ -92,7 +94,9 @@
     return jnp.where(plane, value, 0.0).astype(bf16)
 
 
-def load_kernel(residual, cyt, own, first_x, last_x, rim_lo, rim_hi, along_y, sel, buf, sems, cyt_buf, sem):
+def load_kernel(
+    residual, cyt, first_x, last_x, rim_lo, rim_hi, along_y, sel, buf, sems, cyt_buf, sem
+):
     rows = CELLS // CHUNKS
 
     def copy(c):
@@ -111,7 +115,6 @@
         for b in range(rows // OWN):
             k = c * (rows // OWN) + b
             data = buf[k * OWN : (k + 1) * OWN, :].astype(bf16)
-            own[k * OWN : (k + 1) * OWN, :] = data
             if k == 0:
                 first_x[...] = data
             if k == BLOCKS - 1:
@@ -128,11 +131,11 @@
     return call(
         load_kernel,
         (
-            sds((CELLS, NZ), bf16), sds((OWN, NZ), bf16), sds((OWN, NZ), bf16), rim, rim,
+            sds((OWN, NZ), bf16), sds((OWN, NZ), bf16), rim, rim,
             sds((CX * MODES, NZ), f32), sds((3 * RIM, OWN), bf16),
         ),
         [HBM, HBM],
-        16,
+        WIDE_LOAD,
         scratch=[
             pltpu.VMEM((CELLS, NZ), f32), pltpu.SemaphoreType.DMA((CHUNKS,)),
             pltpu.VMEM((MODES, CY), bf16), pltpu.SemaphoreType.DMA,
@@ -160,9 +163,8 @@
     ((1, NZ), f32), ((MODES, CY), bf16),
 )
 WEIGHTS = (
-    ((ROWS, ROWS), bf16), ((ROWS, ROWS), bf16), ((OWN, ROWS + 2 * RIM), bf16),
-    ((OWN, 2 * RIM), bf16), ((EX, EX), bf16), ((EX, EX), bf16), ((NZ, NZ), bf16),
-    ((NZ, NZ), bf16), ((EX, NZ), f32), ((EY, NZ), f32),
+    ((ROWS, ROWS), bf16), ((ROWS, ROWS), bf16), ((OWN, 4 * RIM), bf16), ((EX, EX), bf16),
+    ((EX, EX), bf16), ((NZ, NZ), bf16), ((NZ, NZ), bf16), ((EX, NZ), f32), ((EY, NZ), f32),
 )
 
 
@@ -195,7 +197,7 @@
     for copy in copies:
         copy.wait()
     lx, ly, lz, eig_x, eig_y, eig_z, cyt = bufs
-    wy, wyt, wfin, spread, wx, wxt, lz_out, lzt, exb, eyz = outs
+    wy, wyt, spread, wx, wxt, lz_out, lzt, exb, eyz = outs
 
     def cell(k):
         y = jnp.where(k < OWN, OV + (k & 31), jnp.where(k < OWN + RIM, k & 3, EY - OV + (k & 3)))
@@ -226,10 +228,10 @@
     k, col = iotas((OWN, 2 * RIM))
     inner = k & 31
     plane = (k >> 5) == ((col >> 2) & 3)
-    coarse = jnp.where(plane, coarse, 0.0).astype(bf16)
-    wfin[...] = jnp.concatenate([value[:OWN], coarse], 1)
+    coarse = jnp.where(plane, coarse, 0.0)
     target = jnp.where(col < RIM, col & 3, CY - OV + (col & 3))
-    spread[...] = jnp.where(plane, jnp.where(inner == target, 1.0, 0.0), 0.0).astype(bf16)
+    rims = jnp.where(plane, jnp.where(inner == target, 1.0, 0.0), 0.0)
+    spread[...] = jnp.concatenate([coarse, rims], 1).astype(bf16)
 
     k, x = iotas((EX, EX))
     source = jnp.where(k < CX, k + OV, jnp.where(k < CX + OV, k - CX, k))
@@ -257,8 +259,8 @@
 
 
 def solve_kernel(
-    own, xlo, xhi, ylo, yhi, wy, wyt, wx, wxt, lz, lzt, exb, eyz, after,
-    kept, out_xlo, out_xhi, out_ylo, out_yhi, field, mid, buf, sems,
+    residual, xlo, xhi, ylo, yhi, wy, wyt, wx, wxt, lz, lzt, exb, eyz, after,
+    kept, out_xlo, out_xhi, out_ylo, out_yhi, field, mid, spec, buf, sems,
 ):
     def put(rows, value):
         field[0, rows, :] = value[:, :128]
@@ -271,11 +273,25 @@
         data = jnp.concatenate([main, tile(ylo, k, RIM), tile(yhi, k, RIM)], 0)
         put(pl.ds(pl.multiple_of(k * ROWS, ROWS), ROWS), dot(wy[...], data))
 
-    def first(k, carry):
-        forward_y(tile(own, k, OWN), k)
-        return carry
-
-    lax.fori_loop(0, BLOCKS, first, 0, unroll=4)
+    rows = CELLS // CHUNKS
+    per = BLOCKS // CHUNKS
+
+    def copy(c):
+        at = pl.ds(pl.multiple_of(c * rows, rows), rows)
+        return pltpu.make_async_copy(residual.at[at, :], buf.at[at, :], sems.at[c])
+
+    for c in range(CHUNKS):
+        copy(c).start()
+
+    def first(c, carry):
+        for i in range(2):
+            copy(2 * c + i).wait()
+        for b in range(2 * per):
+            k = c * 2 * per + b
+            forward_y(tile(buf, k, OWN).astype(bf16), k)
+        return carry
+
+    lax.fori_loop(0, CHUNKS // 2, first, 0)
     forward_y(xlo[...], BLOCKS)
     forward_y(xhi[...], BLOCKS + 1)
 
@@ -287,54 +303,49 @@
         mid[mid_rows(b), :] = dot(wx[...], plane)
         return carry
 
-    lax.fori_loop(0, EY, forward_x, 0, unroll=8)
-
-    def both_z(i, carry):
-        at = pl.ds(pl.multiple_of(i * 4 * EX, 8), 4 * EX)
+    lax.fori_loop(0, EY, forward_x, 0, unroll=20)
+
+    def forward_z(i, carry):
+        at = pl.ds(pl.multiple_of(i * 4 * EX, 16), 4 * EX)
         along = dot(mid[at, :].astype(bf16), lz[...])
         parts = []
         for q in range(4):
             scale = exb[...] + eyz[pl.ds(i * 4 + q, 1), :]
             parts.append((along[q * EX : (q + 1) * EX] / scale))
-        spectral = jnp.concatenate(parts, 0).astype(bf16)
-        mid[at, :] = dot(spectral, lzt[...])
-        return carry
-
-    lax.fori_loop(0, EY // 4, both_z, 0)
+        spec[at, :] = jnp.concatenate(parts, 0).astype(bf16)
+        return carry
+
+    lax.fori_loop(0, EY // 4, forward_z, 0, unroll=5)
+
+    def backward_z(i, carry):
+        at = pl.ds(pl.multiple_of(i * 4 * EX, 16), 4 * EX)
+        mid[at, :] = dot(spec[at, :], lzt[...])
+        return carry
+
+    lax.fori_loop(0, EY // 4, backward_z, 0, unroll=5)
 
     def backward_x(b, carry):
         put(pl.ds(b, EX, stride=EY), dot(wxt[...], mid[mid_rows(b), :].astype(bf16)))
         return carry
 
-    lax.fori_loop(0, EY, backward_x, 0, unroll=8)
+    lax.fori_loop(0, EY, backward_x, 0, unroll=20)
 
     def planes(k):
         return take(pl.ds(pl.multiple_of(k * ROWS, ROWS), ROWS)).astype(bf16)
 
     out_xlo[...] = dot(wyt[...], planes(BLOCKS)).astype(bf16)
     out_xhi[...] = dot(wyt[...], planes(BLOCKS + 1)).astype(bf16)
-    rows = BLOCKS * ROWS // CHUNKS
-    per = BLOCKS // CHUNKS
-
-    def copy(c):
-        at = pl.ds(pl.multiple_of(c * rows, rows), rows)
-        return pltpu.make_async_copy(buf.at[at, :], kept.at[at, :], sems.at[c])
-
-    def last(c, carry):
-        for b in range(per):
-            k = c * per + b
-            data = planes(k)
-            buf[pl.ds(pl.multiple_of(k * ROWS, ROWS), ROWS), :] = data
-            out = dot(wyt[OWN:, :], data).astype(bf16)
-            at = pl.ds(pl.multiple_of(k * RIM, RIM), RIM)
-            out_ylo[at, :] = out[:RIM]
-            out_yhi[at, :] = out[RIM:]
-        copy(c).start()
-        return carry
-
-    lax.fori_loop(0, CHUNKS, last, 0)
-    for c in range(CHUNKS):
-        copy(c).wait()
+
+    def last(k, carry):
+        data = planes(k)
+        kept[pl.ds(pl.multiple_of(k * ROWS, ROWS), ROWS), :] = data
+        out = dot(wyt[OWN:, :], data).astype(bf16)
+        at = pl.ds(pl.multiple_of(k * RIM, RIM), RIM)
+        out_ylo[at, :] = out[:RIM]
+        out_yhi[at, :] = out[RIM:]
+        return carry
+
+    lax.fori_loop(0, BLOCKS, last, 0, unroll=8)
 
 
 def solve(*args):
@@ -343,12 +354,12 @@
     return call(
         solve_kernel,
         (sds((BLOCKS * ROWS, NZ), bf16), strip, strip, rim, rim),
-        [VM] * 13 + [ANY],
-        24,
-        out_specs=(ANY, VM, VM, VM, VM),
+        [HBM] + [VM] * 12 + [ANY],
+        WIDE_SOLVE,
         scratch=[
             pltpu.VMEM((2, EX * EY, NZ // 2), f32), pltpu.VMEM((EX * EY, NZ), f32),
-            pltpu.VMEM((BLOCKS * ROWS, NZ), bf16), pltpu.SemaphoreType.DMA((CHUNKS,)),
+            pltpu.VMEM((EX * EY, NZ), bf16), pltpu.VMEM((CELLS, NZ), f32),
+            pltpu.SemaphoreType.DMA((CHUNKS,)),
         ],
     )(*args)
 
@@ -391,6 +402,12 @@
         out[i] = part
 
 
+def coarse_y_kernel(rows, after, out):
+    both = jnp.concatenate([rows[j] for j in range(rows.shape[0])], 0)
+    for i in range(out.shape[0]):
+        out[i] = both
+
+
 def coarse_kernel(rows, modes_xz, mode_y, ceig_x, ceig_y, ceig_z, cxt, czt, out):
     to_a, to_c = modes_a()
     eight_x = jnp.broadcast_to(ceig_x[...], (8, 32))
@@ -398,10 +415,11 @@
     row = (dot_hi(eight_x, to_a) + dot_hi(eight_z, to_c))[:1]
     r, b = iotas((128, 128))
     column = jnp.sum(jnp.where(r == b, ceig_y[...], 0.0), axis=1, keepdims=True)
-    columns = jnp.concatenate([rows[j] for j in range(rows.shape[0])], 0)
+    columns = rows[...].reshape(128, 128)
     hat = dot_hi(mode_y[...].T, columns) / (column + row)
     row, col = iotas((8, 128))
-    mine = pick(col == lax.axis_index("gy") * MODES + row, f32)
+    place_y = lax.axis_index("gz") * 4 + lax.axis_index("gw")
+    mine = pick(col == place_y * MODES + row, f32)
     rows_y = dot_hi(mine, mode_y[...])
     rows_xz = modes_xz[pl.ds(pl.multiple_of(lax.axis_index("gx") * 16, 16), 16), :]
     sol = dot_t_hi(dot_hi(rows_y, hat), rows_xz)
@@ -420,29 +438,16 @@
         out[(2 * k + 1) * RIM : (2 * k + 2) * RIM, :] = low[at]
 
 
-def finish_kernel(field, wfin, shape, after, fix, buf, sems):
-    rows = BLOCKS * ROWS // CHUNKS
-    per = BLOCKS // CHUNKS
-
-    def copy(c):
-        at = pl.ds(pl.multiple_of(c * rows, rows), rows)
-        return pltpu.make_async_copy(field.at[at, :], buf.at[at, :], sems.at[c])
-
-    for c in range(CHUNKS):
-        copy(c).start()
-
-    def step(c, carry):
-        copy(c).wait()
-        for b in range(per):
-            k = c * per + b
-            data = jnp.concatenate([tile(buf, k, ROWS), tile(shape, k, 2 * RIM)], 0)
-            fix[pl.ds(pl.multiple_of(k * OWN, OWN), OWN), :] = dot(wfin[...], data)
-        return carry
-
-    lax.fori_loop(0, CHUNKS, step, 0)
-
-
-def combine_kernel(fix, spread, rxlo, rxhi, rylo, ryhi, out, buf, sems):
+def finish_kernel(field, wyt, fix):
+    def step(k, carry):
+        planes = tile(field, k, ROWS)
+        fix[pl.ds(pl.multiple_of(k * OWN, OWN), OWN), :] = dot(wyt[:OWN, :], planes)
+        return carry
+
+    lax.fori_loop(0, BLOCKS, step, 0, unroll=8)
+
+
+def combine_kernel(fix, spread, shape, rxlo, rxhi, rylo, ryhi, out, buf, sems):
     rows = CELLS // CHUNKS
 
     def copy(c):
@@ -453,7 +458,9 @@
         for b in range(rows // OWN):
             k = c * (rows // OWN) + b
             rim = slice(k * RIM, (k + 1) * RIM)
-            data = jnp.concatenate([rylo[rim, :], ryhi[rim, :]], 0)
+            data = jnp.concatenate(
+                [shape[2 * k * RIM : 2 * (k + 1) * RIM, :], rylo[rim, :], ryhi[rim, :]], 0
+            )
             total = fix[k * OWN : (k + 1) * OWN, :] + dot(spread[...], data)
             if k == 0:
                 total = total + rxlo[:OWN, :].astype(f32)
@@ -469,13 +476,16 @@
     return call(
         combine_kernel,
         sds((CELLS, NZ), f32),
-        [VM] * 6,
+        [VM] * 7,
         16,
         out_specs=HBM,
         scratch=[pltpu.VMEM((CELLS, NZ), f32), pltpu.SemaphoreType.DMA((CHUNKS,))],
     )(*args)
 
 
+GY = ("gz", "gw")
+
+
 def shift(x, axis, step):
     size = lax.axis_size(axis)
     return lax.ppermute(x, axis, [(i, (i + step) % size) for i in range(size)])
@@ -489,9 +499,8 @@
     residual, local_x, local_y, local_z, eig_x, eig_y, eig_z, coarse_x, coarse_y, coarse_z,
     mode_x, mode_y, mode_z, coarse_eig_x, coarse_eig_y, coarse_eig_z,
 ):
-    own, first_x, last_x, rim_lo, rim_hi, along_y, sel = load(
-        residual.reshape(CELLS, NZ), coarse_y
-    )
+    cells = residual.reshape(CELLS, NZ)
+    first_x, last_x, rim_lo, rim_hi, along_y, sel = load(cells, coarse_y)
     xlo = shift(last_x, "gx", 1)
     xhi = shift(first_x, "gx", -1)
     own_coarse, modes_xz = call(
@@ -499,38 +508,40 @@
     )(along_y, coarse_x.T, coarse_z.T, mode_x, mode_z)
     rows = exchange(own_coarse, "gx")
     down, up = corners(sel, rim_lo, rim_hi, xlo, xhi, own_coarse)
-    ylo = shift(up, "gy", 1)
-    yhi = shift(down, "gy", -1)
-    part = call(coarse_x_kernel, sds((32, MODES, 128), f32), [VM] * 2, 4)(rows, modes_xz)
-    rows = exchange(part, "gy")
-
-    wy, wyt, wfin, spread, wx, wxt, lz, lzt, exb, eyz = prepare(
+    ylo = shift(up, GY, 1)
+    yhi = shift(down, GY, -1)
+    part = call(coarse_x_kernel, sds((4, MODES, 128), f32), [VM] * 2, 4)(
+        rows, modes_xz
+    )
+    rows = exchange(part, "gw")
+
+    wy, wyt, spread, wx, wxt, lz, lzt, exb, eyz = prepare(
         local_x, local_y, local_z, eig_x[None], eig_y[None], eig_z[None], coarse_y.T, part
     )
     field, out_xlo, out_xhi, out_ylo, out_yhi = solve(
-        own, xlo, xhi, ylo, yhi, wy, wyt, wx, wxt, lz, lzt, exb, eyz, part
+        cells, xlo, xhi, ylo, yhi, wy, wyt, wx, wxt, lz, lzt, exb, eyz, rows
     )
 
     rxlo = shift(out_xhi, "gx", 1)
     rxhi = shift(out_xlo, "gx", -1)
+    fix = call(finish_kernel, sds((CELLS, NZ), f32), [VM] * 2, 8)(field, wyt)
+    down, up = fold(out_ylo, out_yhi, rxlo, rxhi, fix)
+    rylo = shift(up, GY, 1)
+    ryhi = shift(down, GY, -1)
+    rows = call(coarse_y_kernel, sds((8, 16, 128), f32), [VM, ANY], 4)(rows, up)
+    rows = exchange(rows, "gz")
     shape = call(coarse_kernel, sds((2 * CX * MODES, NZ), bf16), [VM] * 8, 8)(
         rows, modes_xz, mode_y, coarse_eig_x[None], coarse_eig_y[None], coarse_eig_z[None],
         coarse_x.T, coarse_z.T,
     )
-    down, up = fold(out_ylo, out_yhi, rxlo, rxhi, shape)
-    rylo = shift(up, "gy", 1)
-    ryhi = shift(down, "gy", -1)
-    fix = call(
-        finish_kernel, sds((CELLS, NZ), f32), [ANY] + [VM] * 2 + [ANY], 16,
-        scratch=[pltpu.VMEM((BLOCKS * ROWS, NZ), bf16), pltpu.SemaphoreType.DMA((CHUNKS,))],
-    )(field, wfin, shape, up)
-    out = combine(fix, spread, rxlo, rxhi, rylo, ryhi)
+    out = combine(fix, spread, shape, rxlo, rxhi, rylo, ryhi)
     return out.reshape(CX, CY, NZ)
 
 
 def solution(mesh):
-    placed = (P("gx", "gy", None),) + (P(),) * 15
+    fine = Mesh(mesh.devices.reshape(8, 8, 4), ("gx", "gz", "gw"))
+    cells = P("gx", GY, None)
 
     return jax.shard_map(
-        local, mesh=mesh, in_specs=placed, out_specs=P("gx", "gy", None), check_vma=False
-    )
+        local, mesh=fine, in_specs=(cells,) + (P(),) * 15, out_specs=cells, check_vma=False
+    )

time: 77.8 us -> 69.8 us (0.90)
  the two profiles are of different devices: /device:TPU:1 before, /device:TPU:24 now
where the time goes in v5:
time: 69.8 us; the launch traced here: 69.5 us
  starting transfers between devices  22.3 us (32%)
  blocking collectives  22.1 us (32%)
  Pallas kernels  20.1 us (29%)
  waiting for transfers between devices  4.02 us (6%)
  local copies, waits for them, and re-layouts  0.8 us (1%)
    all_to_all x2, blocking collectives, exchange(): return lax.all_to_all(x, axis, 0, 0)  22.1 us
    ppermute x8, starting transfers between devices, shift(): return lax.ppermute(x, axis, [(i, (i + step) % size) for i in range(size)])  12.2 us
    all_to_all x1, starting transfers between devices, exchange(): return lax.all_to_all(x, axis, 0, 0)  10.1 us
    pallas_call x1, Pallas kernels, solve(): call(solve_kernel, (sds((BLOCKS * ROWS, NZ), bf16), strip, strip, rim, ri...  9.56 us
    pallas_call x1, Pallas kernels, load(): call(load_kernel, (sds((OWN, NZ), bf16), sds((OWN, NZ), bf16), rim, rim,...  2.56 us
    pallas_call x1, Pallas kernels, combine(): call(combine_kernel, sds((CELLS, NZ), f32), [VM] * 7, 16, out_specs=HBM,...  2.28 us
    all_to_all x1, waiting for transfers between devices, exchange(): return lax.all_to_all(x, axis, 0, 0)  2.23 us
    ppermute x8, waiting for transfers between devices, shift(): return lax.ppermute(x, axis, [(i, (i + step) % size) for i in range(size)])  1.79 us
  transfers between devices with their start and end apart: 9, of which 3 were waited for; matrix products, arithmetic and copies ran while one was open for 0% of the time, Pallas kernels for 8%

profile of v5, /device:TPU:24, one launch (start us, length us, event | category | flops | bytes accessed | tf_op | source)
XLA Modules:
  0.0 69.5 jit_solution(1178335295565228283)
XLA Ops:
  0.0 0.0 copy-start.4
  0.0 0.0 copy-start.1
  0.0 0.0 copy-start.6
  0.0 0.7 %copy-done.6 = bf16[32,4]{0,1:T(4,128)(2,1)S(1)} copy-done((bf16[32,4]{0,1:T(4,128)(2,1)S(1)}, bf16[32,4]{0,1:T(4,128)(2,1)}, u32[]{:S(2)}) %copy-start.6) | copy-done | bytes 280
  0.8 0.0 copy-start.11
  0.8 0.0 copy-start.12
  0.8 2.6 %shard_map.154 = (bf16[128,256]{1,0:T(8,128)(2,1)S(1)}, bf16[128,256]{1,0:T(8,128)(2,1)S(1)}, bf16[512,256]{1,0:T(8,128)(2,1)S(1)}, bf16[512,256]{1,0:T(8,128)(2...) custom-call(f32[4096,256]{1,0:T(8,128)} %bitcast.23, bf16[4,32]{1,0:T(4,128)(2,1)S(1)} %bitcast.13), custom_call_target="tpu_custom_call" | custom-call | tf_op jit(solution)/shard_map/pallas_call | solution.py:131
  3.4 0.0 collective-permute-start
  3.4 2.9 %collective-permute-start.1 = (bf16[128,256]{1,0:T(8,128)(2,1)S(1)}, bf16[128,256]{1,0:T(8,128)(2,1)S(1)}, u32[]{:S(2)}, u32[]{:S(2)}) collective-permute-start(bf16[128,256]{1,0:T(8,128)(2,1)S(1)} %get-tuple-element.32), channel_id=1, source_target_pairs={{0,224},{32,0},{64,32},{96,64},{128,96},{160,128},{192,160},{224,1... | collective-permute-start | bytes 196616 | tf_op jit(solution)/shard_map/ppermute | solution.py:491
  6.3 0.0 copy-done.3
  6.3 0.0 copy-done.5
  6.3 0.0 copy-done.8
  6.3 0.0 copy-done.9
  6.4 1.0 %shard_map.155 = (f32[8,4,16]{2,1,0:T(4,128)S(1)}, f32[128,128]{1,0:T(8,128)S(1)}) custom-call(f32[512,256]{1,0:T(8,128)S(1)} %get-tuple-element.36.along_y, bf16[4,128]{1,0:T(4,128)(2,1)S(1)} %bitcast.15, bf16[4,256]{1,0:T(4,128)(2,1)S(1)} %bitcast.11, f32[32,32]{1,0:T(8,128)S(1)} %copy-done.3, f32[4,4]{1,0:T(4,128)S(1)} %copy-done.9), custom_call_target="tpu_custom_call" | custom-call | tf_op jit(solution)/shard_map/pallas_call | solution.py:506
  7.4 0.9 %collective-permute-done.xlo = bf16[128,256]{1,0:T(8,128)(2,1)S(1)} collective-permute-done((bf16[128,256]{1,0:T(8,128)(2,1)S(1)}, bf16[128,256]{1,0:T(8,128)(2,1)S(1)}, u32[]{:S(2)}, u32[]{:S(2)}) %collective-permute-start) | collective-permute-done | bytes 65568 | tf_op jit(solution)/shard_map/ppermute | solution.py:491
  8.3 0.0 collective-permute-done.1.xhi
  8.3 0.1 shard_map.156
  8.4 1.6 %collective-permute-start.2 = (bf16[544,256]{1,0:T(8,128)(2,1)S(1)}, bf16[544,256]{1,0:T(8,128)(2,1)S(1)}, u32[]{:S(2)}, u32[]{:S(2)}) collective-permute-start(bf16[544,256]{1,0:T(8,128)(2,1)S(1)} %get-tuple-element.38), channel_id=1, source_target_pairs={{0,1},{1,2},{2,3},{3,4},{4,5},{5,6},{6,7},{7,8},{8,9},{9,10},{10,1... | collective-permute-start | bytes 835592 | tf_op jit(solution)/shard_map/ppermute | solution.py:491
  10.0 0.4 collective-permute-start.3
  10.5 8.8 %all_to_all.15.rows = f32[8,4,16]{2,1,0:T(4,128)S(1)} all-to-all(f32[8,4,16]{2,1,0:T(4,128)S(1)} %get-tuple-element.37.after), channel_id=1, replica_groups=mesh['gx'=8,'gz'=8,'gw'=4] {'gx'}, dimensions={0} | all-to-all | bytes 4096 | tf_op jit(solution)/shard_map/all_to_all | solution.py:495
  19.3 0.8 %shard_map.157.refs_7_ = f32[4,4,128]{2,1,0:T(4,128)} custom-call(f32[8,4,16]{2,1,0:T(4,128)S(1)} %all_to_all.15.rows, f32[128,128]{1,0:T(8,128)S(1)} %get-tuple-element.40.modes_xz), custom_call_target="tpu_custom_call" | custom-call | tf_op jit(solution)/shard_map/pallas_call | solution.py:513
  20.2 10.1 %all-to-all-start.1 = ((f32[4,4,128]{2,1,0:T(4,128)}), f32[4,4,128]{2,1,0:T(4,128)S(1)}, u32[]{:S(2)}, u32[]{:S(2)}) async-start(f32[4,4,128]{2,1,0:T(4,128)} %shard_map.157.refs_7_), calls=%async_computation.1 | async-start | bytes 16384 | tf_op jit(solution)/shard_map/all_to_all | solution.py:495
  30.2 0.0 copy-done
  30.2 0.0 copy-done.4
  30.2 0.0 copy-done.1
  30.3 0.0 copy-done.7
  30.3 0.0 copy-done.10
  30.3 1.0 %shard_map.158 = (bf16[160,160]{1,0:T(8,128)(2,1)S(1)}, bf16[160,160]{1,0:T(8,128)(2,1)S(1)}, bf16[128,64]{1,0:T(8,128)(2,1)S(1)}, bf16[136,136]{1,0:T(8,128)(2,...) custom-call(bf16[136,136]{1,0:T(8,128)(2,1)S(1)} %copy-done.1, ...), custom_call_target="tpu_custom_call" | custom-call | tf_op jit(solution)/shard_map/pallas_call | solution.py:252
  31.3 2.2 %all-to-all-done.1.after.rows = f32[4,4,128]{2,1,0:T(4,128)S(1)} async-done(((f32[4,4,128]{2,1,0:T(4,128)}), f32[4,4,128]{2,1,0:T(4,128)S(1)}, u32[]{:S(2)}, u32[]{:S(2)}) %all-to-all-start.1) | async-done | bytes 8224 | tf_op jit(solution)/shard_map/all_to_all | solution.py:495
  33.5 0.0 collective-permute-done.2.ylo
  33.5 0.0 collective-permute-done.3.yhi
  33.5 9.6 %shard_map.159 = (bf16[5120,256]{1,0:T(8,128)(2,1)S(1)}, bf16[160,256]{1,0:T(8,128)(2,1)S(1)}, bf16[160,256]{1,0:T(8,128)(2,1)S(1)}, bf16[512,256]{1,0:T(8,128)(2,1)S(1)}, bf16[512,256]{1,0:T(8,128)(2,1)S(1)}) custom-call(f32[4096,256]{1,0:T(8,128)} %bitcast.24, bf16[128,256]{1,0:T(8,128)(2,1)S(1)} %collective-permute-done.xlo, ...), custom_call_target="tpu_custom_call" | custom-call | tf_op jit(solution)/shard_map/pallas_call | solution.py:354
  43.1 0.0 collective-permute-start.4
  43.1 2.9 %collective-permute-start.5 = (bf16[160,256]{1,0:T(8,128)(2,1)S(1)}, bf16[160,256]{1,0:T(8,128)(2,1)S(1)}, u32[]{:S(2)}, u32[]{:S(2)}) collective-permute-start(bf16[160,256]{1,0:T(8,128)(2,1)S(1)} %get-tuple-element.54), channel_id=1, source_target_pairs={{0,224},{32,0},{64,32},{96,64},{128,96},{160,128},{192,160},{224,1... | collective-permute-start | bytes 245768 | tf_op jit(solution)/shard_map/ppermute | solution.py:491
  46.0 1.2 %shard_map.160.after.fix = f32[4096,256]{1,0:T(8,128)S(1)} custom-call(bf16[5120,256]{1,0:T(8,128)(2,1)S(1)} %get-tuple-element.49.field, bf16[160,160]{1,0:T(8,128)(2,1)S(1)} %get-tuple-element.42.wyt), custom_call_target="tpu_custom_call" | custom-call | tf_op jit(solution)/shard_map/pallas_call | solution.py:527
  47.2 0.0 copy-start.2
  47.3 0.0 copy-start.13
  47.3 0.0 copy-start.14
  47.3 0.0 copy-start.15
  47.3 0.9 %collective-permute-done.4.rxlo = bf16[160,256]{1,0:T(8,128)(2,1)S(1)} collective-permute-done((bf16[160,256]{1,0:T(8,128)(2,1)S(1)}, bf16[160,256]{1,0:T(8,128)(2,1)S(1)}, u32[]{:S(2)}, u32[]{:S(2)}) %collective-permute-start.4) | collective-permute-done | bytes 81952 | tf_op jit(solution)/shard_map/ppermute | solution.py:491
  48.2 0.0 collective-permute-done.5.rxhi
  48.2 0.6 collective-permute-start.7
  48.8 3.6 %collective-permute-start.6 = (bf16[512,256]{1,0:T(8,128)(2,1)S(1)}, bf16[512,256]{1,0:T(8,128)(2,1)S(1)}, u32[]{:S(2)}, u32[]{:S(2)}) collective-permute-start(bf16[512,256]{1,0:T(8,128)(2,1)S(1)} %get-tuple-element.55.after), channel_id=1, source_target_pairs={{0,1},{1,2},{2,3},{3,4},{4,5},{5,6},{6,7},{7,8},{8,9},{9,10},{10,1... | collective-permute-start | bytes 786440 | tf_op jit(solution)/shard_map/ppermute | solution.py:491
  52.4 13.3 %all_to_all.16.rows = f32[8,16,128]{2,1,0:T(8,128)S(1)} all-to-all(f32[8,16,128]{2,1,0:T(8,128)S(1)} %shard_map.162), channel_id=1, replica_groups=mesh['gx'=8,'gz'=8,'gw'=4] {'gz'}, dimensions={0} | all-to-all | bytes 131072 | tf_op jit(solution)/shard_map/all_to_all | solution.py:495
  65.8 1.5 %shard_map.163.shape = bf16[1024,256]{1,0:T(8,128)(2,1)S(1)} custom-call(f32[8,16,128]{2,1,0:T(8,128)S(1)} %all_to_all.16.rows, f32[128,128]{1,0:T(8,128)S(1)} %get-tuple-element.40.modes_xz, f32[128,128]{1,0:T(8,128)S(1)} %copy-done.2, f32[1,32]{1,0:T(1,128)S(1)} %bitcast.20, f32[1,128]{1,0:T(1,128)S(1)} %bitcast.21, f32[1,4]{1,0:T(1,128)S(1)} %bitcast.22, ...), custom_call_target="tpu_custom_call" | custom-call | tf_op jit(solution)/shard_map/pallas_call | solution.py:533
  67.2 0.0 collective-permute-done.7.ryhi
  67.2 0.0 collective-permute-done.6.rylo
  67.2 2.3 %shard_map.164 = f32[4096,256]{1,0:T(8,128)} custom-call(f32[4096,256]{1,0:T(8,128)S(1)} %shard_map.160.after.fix, bf16[128,64]{1,0:T(8,128)(2,1)S(1)} %get-tuple-element.50.spread, bf16[1024,256]{1,0:T(8,128)(2,1)S(1)} %shard_map.163.shape, bf16[160,256]{1,0:T(8,128)(2,1)S(1)} %collective-permute-done.4.rxlo, ...), custom_call_target="tpu_custom_call" | custom-call | tf_op jit(solution)/shard_map/pallas_call | solution.py:476
  (15 shorter events, 0.1 us)
Async XLA Ops:
  0.0 6.3 %copy-start.3 = (f32[32,32]{1,0:T(8,128)S(1)}, f32[32,32]{1,0:T(8,128)}, u32[]{:S(2)}) copy-start(f32[32,32]{1,0:T(8,128)} %mode_x.1) | copy-start | bytes 12292
  0.0 6.3 %copy-start.5 = (bf16[256,4]{0,1:T(4,128)(2,1)S(1)}, bf16[256,4]{0,1:T(4,128)(2,1)}, u32[]{:S(2)}) copy-start(bf16[256,4]{0,1:T(4,128)(2,1)} %param.25) | copy-start | bytes 6148
  0.0 30.2 %copy-start = (bf16[256,256]{1,0:T(8,128)(2,1)S(1)}, bf16[256,256]{1,0:T(8,128)(2,1)}, u32[]{:S(2)}) copy-start(bf16[256,256]{1,0:T(8,128)(2,1)} %refs_2_.1) | copy-start | bytes 393220
  0.0 30.2 %copy-start.4 = (bf16[40,40]{1,0:T(8,128)(2,1)S(1)}, bf16[40,40]{1,0:T(8,128)(2,1)}, u32[]{:S(2)}) copy-start(bf16[40,40]{1,0:T(8,128)(2,1)} %refs_1_.1) | copy-start | bytes 9604
  0.0 30.2 %copy-start.1 = (bf16[136,136]{1,0:T(8,128)(2,1)S(1)}, bf16[136,136]{1,0:T(8,128)(2,1)}, u32[]{:S(2)}) copy-start(bf16[136,136]{1,0:T(8,128)(2,1)} %refs_0_.1) | copy-start | bytes 110980
  0.0 0.7 %copy-start.6 = (bf16[32,4]{0,1:T(4,128)(2,1)S(1)}, bf16[32,4]{0,1:T(4,128)(2,1)}, u32[]{:S(2)}) copy-start(bf16[32,4]{0,1:T(4,128)(2,1)} %param.24) | copy-start | bytes 772
  0.8 5.6 %copy-start.8 = (bf16[128,4]{0,1:T(4,128)(2,1)S(1)}, bf16[128,4]{0,1:T(4,128)(2,1)}, u32[]{:S(2)}) copy-start(bf16[128,4]{0,1:T(4,128)(2,1)} %param.23) | copy-start | bytes 3076
  0.8 5.6 %copy-start.9 = (f32[4,4]{1,0:T(4,128)S(1)}, f32[4,4]{1,0:T(4,128)}, u32[]{:S(2)}) copy-start(f32[4,4]{1,0:T(4,128)} %mode_z.1) | copy-start | bytes 196
  0.8 29.5 %copy-start.7 = (bf16[32,4]{0,1:T(4,128)(2,1)S(1)}, bf16[32,4]{0,1:T(4,128)(2,1)}, u32[]{:S(2)}) copy-start(bf16[32,4]{0,1:T(4,128)(2,1)} %param.24) | copy-start | bytes 772
  0.8 29.5 %copy-start.10 = (f32[136]{0:T(256)S(1)}, f32[136]{0:T(256)}, u32[]{:S(2)}) copy-start(f32[136]{0:T(256)} %param.20) | copy-start | bytes 1636
  0.8 29.5 %copy-start.11 = (f32[256]{0:T(256)S(1)}, f32[256]{0:T(256)}, u32[]{:S(2)}) copy-start(f32[256]{0:T(256)} %param.22) | copy-start | bytes 3076
  0.8 29.5 %copy-start.12 = (f32[40]{0:T(128)S(1)}, f32[40]{0:T(128)}, u32[]{:S(2)}) copy-start(f32[40]{0:T(128)} %param.21) | copy-start | bytes 484
  3.4 4.9 %collective-permute-start = (bf16[128,256]{1,0:T(8,128)(2,1)S(1)}, bf16[128,256]{1,0:T(8,128)(2,1)S(1)}, u32[]{:S(2)}, u32[]{:S(2)}) collective-permute-start(bf16[128,256]{1,0:T(8,128)(2,1)S(1)} %get-tuple-element.31), channel_id=1, source_target_pairs={{0,32},{32,64},{64,96},{96,128},{128,160},{160,192},{192,224},{224... | collective-permute-start | bytes 196616 | tf_op jit(solution)/shard_map/ppermute | solution.py:491
  3.4 4.9 %collective-permute-start.1 = (bf16[128,256]{1,0:T(8,128)(2,1)S(1)}, bf16[128,256]{1,0:T(8,128)(2,1)S(1)}, u32[]{:S(2)}, u32[]{:S(2)}) collective-permute-start(bf16[128,256]{1,0:T(8,128)(2,1)S(1)} %get-tuple-element.32), channel_id=1, source_target_pairs={{0,224},{32,0},{64,32},{96,64},{128,96},{160,128},{192,160},{224,1... | collective-permute-start | bytes 196616 | tf_op jit(solution)/shard_map/ppermute | solution.py:491
  8.4 25.1 %collective-permute-start.2 = (bf16[544,256]{1,0:T(8,128)(2,1)S(1)}, bf16[544,256]{1,0:T(8,128)(2,1)S(1)}, u32[]{:S(2)}, u32[]{:S(2)}) collective-permute-start(bf16[544,256]{1,0:T(8,128)(2,1)S(1)} %get-tuple-element.38), channel_id=1, source_target_pairs={{0,1},{1,2},{2,3},{3,4},{4,5},{5,6},{6,7},{7,8},{8,9},{9,10},{10,1... | collective-permute-start | bytes 835592 | tf_op jit(solution)/shard_map/ppermute | solution.py:491
  10.0 23.5 %collective-permute-start.3 = (bf16[544,256]{1,0:T(8,128)(2,1)S(1)}, bf16[544,256]{1,0:T(8,128)(2,1)S(1)}, u32[]{:S(2)}, u32[]{:S(2)}) collective-permute-start(bf16[544,256]{1,0:T(8,128)(2,1)S(1)} %get-tuple-element.39), channel_id=1, source_target_pairs={{0,31},{1,0},{2,1},{3,2},{4,3},{5,4},{6,5},{7,6},{8,7},{9,8},{10,9... | collective-permute-start | bytes 835592 | tf_op jit(solution)/shard_map/ppermute | solution.py:491
  20.2 13.3 %all-to-all-start.1 = ((f32[4,4,128]{2,1,0:T(4,128)}), f32[4,4,128]{2,1,0:T(4,128)S(1)}, u32[]{:S(2)}, u32[]{:S(2)}) async-start(f32[4,4,128]{2,1,0:T(4,128)} %shard_map.157.refs_7_), calls=%async_computation.1 | async-start | bytes 16384 | tf_op jit(solution)/shard_map/all_to_all | solution.py:495
  43.1 5.1 %collective-permute-start.4 = (bf16[160,256]{1,0:T(8,128)(2,1)S(1)}, bf16[160,256]{1,0:T(8,128)(2,1)S(1)}, u32[]{:S(2)}, u32[]{:S(2)}) collective-permute-start(bf16[160,256]{1,0:T(8,128)(2,1)S(1)} %get-tuple-element.53), channel_id=1, source_target_pairs={{0,32},{32,64},{64,96},{96,128},{128,160},{160,192},{192,224},{224... | collective-permute-start | bytes 245768 | tf_op jit(solution)/shard_map/ppermute | solution.py:491
  43.1 5.1 %collective-permute-start.5 = (bf16[160,256]{1,0:T(8,128)(2,1)S(1)}, bf16[160,256]{1,0:T(8,128)(2,1)S(1)}, u32[]{:S(2)}, u32[]{:S(2)}) collective-permute-start(bf16[160,256]{1,0:T(8,128)(2,1)S(1)} %get-tuple-element.54), channel_id=1, source_target_pairs={{0,224},{32,0},{64,32},{96,64},{128,96},{160,128},{192,160},{224,1... | collective-permute-start | bytes 245768 | tf_op jit(solution)/shard_map/ppermute | solution.py:491
  47.2 18.5 %copy-start.2 = (f32[128,128]{1,0:T(8,128)S(1)}, f32[128,128]{1,0:T(8,128)}, u32[]{:S(2)}) copy-start(f32[128,128]{1,0:T(8,128)} %mode_y.1) | copy-start | bytes 196612
  47.3 18.5 %copy-start.13 = (f32[32]{0:T(128)S(1)}, f32[32]{0:T(128)}, u32[]{:S(2)}) copy-start(f32[32]{0:T(128)} %param.29) | copy-start | bytes 388
  47.3 18.5 %copy-start.14 = (f32[128]{0:T(128)S(1)}, f32[128]{0:T(128)}, u32[]{:S(2)}) copy-start(f32[128]{0:T(128)} %param.30) | copy-start | bytes 1540
  47.3 18.5 %copy-start.15 = (f32[4]{0:T(128)S(1)}, f32[4]{0:T(128)}, u32[]{:S(2)}) copy-start(f32[4]{0:T(128)} %param.31) | copy-start | bytes 52
  48.2 19.0 %collective-permute-start.7 = (bf16[512,256]{1,0:T(8,128)(2,1)S(1)}, bf16[512,256]{1,0:T(8,128)(2,1)S(1)}, u32[]{:S(2)}, u32[]{:S(2)}) collective-permute-start(bf16[512,256]{1,0:T(8,128)(2,1)S(1)} %get-tuple-element.56), channel_id=1, source_target_pairs={{0,31},{1,0},{2,1},{3,2},{4,3},{5,4},{6,5},{7,6},{8,7},{9,8},{10,9... | collective-permute-start | bytes 786440 | tf_op jit(solution)/shard_map/ppermute | solution.py:491
  48.8 18.4 %collective-permute-start.6 = (bf16[512,256]{1,0:T(8,128)(2,1)S(1)}, bf16[512,256]{1,0:T(8,128)(2,1)S(1)}, u32[]{:S(2)}, u32[]{:S(2)}) collective-permute-start(bf16[512,256]{1,0:T(8,128)(2,1)S(1)} %get-tuple-element.55.after), channel_id=1, source_target_pairs={{0,1},{1,2},{2,3},{3,4},{4,5},{5,6},{6,7},{7,8},{8,9},{9,10},{10,1... | collective-permute-start | bytes 786440 | tf_op jit(solution)/shard_map/ppermute | solution.py:491
